TPU v7x, 128 devices: a whole 4x4x4 slice. The times are simulated.
128 devices in a mesh: lat: 8 (over y, z_hi), lon: 16 (over z_lo, x, core).
Axes of the slice: x: 4, y: 4, z: 4 (z_hi: 2, z_lo: 2; z = z_hi * 2 + z_lo), core: 2. Of those that a mesh axis runs over, the one named last changes fastest.
Arguments:
- ocean: float32 [4, 1024, 6144], P(None, ('lat', 'lon')), may hold values from -6 to 6
- grid_mass: float32 [1024, 6144], P('lat', 'lon'), may hold values from 0.5 to 4
- grid_momentum: float32 [2, 1024, 6144], P(None, 'lat', 'lon'), may hold values from -6 to 6
- cells: int32 [4194304], P(('lat', 'lon')), may hold values from 0 to 49151
- offsets: float32 [2, 4194304], P(None, ('lat', 'lon')), may hold values from -0.5 to 0.5
- moves: int32 [4194304], P(('lat', 'lon')), may hold values from 0 to 4, as said below
- slots: int32 [4194304], P(('lat', 'lon')), may hold values from 0 to 8191, as said below
Outputs:
- parcels: float32 [8, 4194304], P(None, ('lat', 'lon'))
- arrivals: float32 [8, 4194304], P(None, ('lat', 'lon'))
Inputs may be any that keep to these rules, and one draw needn't show every extreme that they name: `moves`: for each brick and direction the leaving parcels have distinct slots 0 to their count - 1, that count is at most 8192, and in every draw for each direction some brick sends exactly 8192 parcels in it; parcels of the first and last latitude bricks never leave the grid in latitude. `slots`: slots of parcels that stay are 0.
All inputs are finite; a program needn't handle non-finite values.
Results may differ from a plain program's by a relative error of at most 0.0003.
Values sent between devices are 32-bit elements; how exact they have to be, the bound alone decides.
No kernel may reach another device: no remote copies, remote signals or barrier semaphores. Data moves between devices by JAX's collectives and lax.ppermute only.
A program may use at most 128 MiB of HBM per device.

v0:
```python
import jax
import jax.numpy as jnp
from jax import lax
from jax.sharding import PartitionSpec as P

CAP = 8192


step_dt = 0.5
drag_coef = 2.0


def extended(cells, sides, width):
    for axis, dim in sides:
        count = lax.axis_size(axis)
        head = lax.slice_in_dim(cells, 0, width, axis=dim)
        tail = lax.slice_in_dim(cells, cells.shape[dim] - width, cells.shape[dim], axis=dim)
        cells = jnp.concatenate(
            [
                lax.ppermute(tail, axis, [(i, (i + 1) % count) for i in range(count)]),
                cells,
                lax.ppermute(head, axis, [((i + 1) % count, i) for i in range(count)]),
            ],
            axis=dim,
        )
    return cells


def from_behind(block, axis, distance):
    devices = range(lax.axis_size(axis))
    route = [(i - distance, i) for i in devices if i - distance in devices]
    return lax.ppermute(block, axis, route)


def passed_along(value, axis, by):
    count = lax.axis_size(axis)
    return lax.ppermute(value, axis, [(i, (i + by) % count) for i in range(count)])


def spline(frac):
    lower = 0.5 * (0.5 - frac) * (0.5 - frac)
    middle = 0.75 - frac * frac
    upper = 0.5 * (0.5 + frac) * (0.5 + frac)
    return (lower, middle, upper)


def interpolate(fetch, frac):
    weights_row = spline(frac[0])
    weights_col = spline(frac[1])
    speed = jnp.zeros(frac.shape, jnp.float32)
    affine = jnp.zeros((4, frac.shape[1]), jnp.float32)
    for row_step in (-1, 0, 1):
        for col_step in (-1, 0, 1):
            weight = weights_row[row_step + 1] * weights_col[col_step + 1]
            sample = fetch(row_step, col_step)
            speed = speed + weight * sample
            arm_row = row_step - frac[0]
            arm_col = col_step - frac[1]
            terms = jnp.stack(
                [sample[0] * arm_row, sample[0] * arm_col, sample[1] * arm_row, sample[1] * arm_col]
            )
            affine = affine + 4.0 * weight * terms
    return jnp.concatenate([frac + step_dt * speed, speed, affine], axis=0)


def shards(ocean, grid_mass, grid_momentum, cells, offsets, moves, slots):
    num_rows, num_cols = grid_mass.shape
    strips = lax.all_gather(ocean, "lon", axis=1, tiled=True)
    forcing = lax.dynamic_slice_in_dim(strips, lax.axis_index("lon") * num_cols, num_cols, 2)
    current = forcing[0:2]
    stress = forcing[2:4]
    velocity = (grid_momentum + step_dt * stress + step_dt * drag_coef * grid_mass * current) / (
        grid_mass * (1.0 + step_dt * drag_coef)
    )
    padded = extended(velocity, (("lat", 1), ("lon", 2)), 1)
    lat_pos = lax.axis_index("lat")
    lat_count = lax.axis_size("lat")
    row_ids = lax.broadcasted_iota(jnp.int32, (1, num_rows + 2, 1), 1)
    outside = (row_ids == 0) & (lat_pos == 0) | (row_ids == num_rows + 1) & (
        lat_pos == lat_count - 1
    )
    padded = jnp.where(outside, 0.0, padded)
    shifted = []
    for row_step in (-1, 0, 1):
        for col_step in (-1, 0, 1):
            shifted.append(
                padded[
                    :,
                    1 + row_step : 1 + row_step + num_rows,
                    1 + col_step : 1 + col_step + num_cols,
                ]
            )
    neighbours = jnp.stack(shifted).reshape(18, num_rows * num_cols).T
    stencil = jnp.take(neighbours, cells, axis=0).T

    def fetch(row_step, col_step):
        place = 2 * ((row_step + 1) * 3 + col_step + 1)
        return stencil[place : place + 2]

    state = interpolate(fetch, offsets)
    count = state.shape[1]
    target = jnp.where(moves > 0, (moves - 1) * CAP + slots, 4 * CAP)
    owner = (
        jnp.full((4 * CAP,), count, jnp.int32)
        .at[target]
        .set(jnp.arange(count, dtype=jnp.int32), mode="drop")
    )
    state_rows = jnp.concatenate([state.T, jnp.zeros((1, 8), jnp.float32)], axis=0)
    outgoing = jnp.take(state_rows, owner, axis=0).T
    north = from_behind(outgoing[:, 0:CAP], "lat", 1)
    south = from_behind(outgoing[:, CAP : 2 * CAP], "lat", -1)
    east = passed_along(outgoing[:, 2 * CAP : 3 * CAP], "lon", 1)
    west = passed_along(outgoing[:, 3 * CAP :], "lon", -1)
    arrivals = jnp.concatenate([north, south, east, west], axis=1)
    return (state, arrivals)


def solution(mesh):
    in_specs = (
        P(None, ("lat", "lon"), None),
        P("lat", "lon"),
        P(None, "lat", "lon"),
        P(("lat", "lon")),
        P(None, ("lat", "lon")),
        P(("lat", "lon")),
        P(("lat", "lon")),
    )
    out_specs = (P(None, ("lat", "lon")), P(None, ("lat", "lon")))
    return jax.shard_map(shards, mesh=mesh, in_specs=in_specs, out_specs=out_specs, check_vma=False)
```

profile of v0, /device:TPU:8, one launch (start us, length us, event | category | flops | bytes accessed | tf_op | source)
XLA Modules:
  0.0 512.3 jit_solution(5253687309127150790)
XLA Ops:
  7.2 0.0 copy-start.1
  7.2 0.0 all-gather.2.cloned.1.call-start
  7.2 0.7 all-gather.2.cloned.1.call-update
  7.9 1.0 compare_select_fusion.1
  9.0 120.1 %scatter_custom_fusion = s32[32768]{0:T(1024)S(1)} fusion(s32[32768]{0:T(1024)S(1)} %compare_select_fusion.1, s32[32768]{0:T(1024)S(1)} %iota.13, s32[]{:T(128)} %constant.40.clone.1), kind=kCustom, calls=%fused_computation.119 | custom fusion | bytes 131076 | tf_op jit(solution)/shard_map/scatter | solution.py:106
  129.0 0.9 broadcast_multiply_fusion
  130.0 1.5 compare_and_fusion.1
  131.5 0.9 fusion.28
  132.5 0.7 fusion.29
  133.2 4.7 broadcast_multiply_fusion.9
  137.9 0.0 copy-done.18
  137.9 1.2 fusion.18
  139.1 3.9 collective-permute-start
  143.1 0.6 collective-permute-start.1
  143.6 0.7 compare_and_fusion
  144.3 0.9 collective-permute-done
  145.2 3.0 collective-permute-done.1
  148.2 0.1 pad_maximum_fusion.4
  148.3 0.1 collective-permute-start.2
  148.4 3.8 collective-permute-start.3
  152.2 2.7 collective-permute-done.2
  154.9 0.0 collective-permute-done.3
  154.9 0.3 maximum_select_fusion
  155.3 0.2 fusion.15
  155.5 0.2 fusion.14
  155.7 0.2 fusion.12
  155.9 0.2 fusion.11
  156.1 0.2 fusion.9
  156.3 0.2 fusion.8
  156.4 0.4 pad.60
  156.9 5.0 copy.297
  161.8 13.9 %copy.289 = f32[18,49152]{0,1:T(8,128)} copy(f32[18,49152]{1,0:T(8,128)} %bitcast.66) | data formatting | bytes 7077888 | tf_op jit(solution)/shard_map/reshape | solution.py:93
  175.7 117.1 %gather_fusion = f32[32768,18]{1,0:T(8,128)} fusion(f32[49152,18]{1,0:T(8,128)} %bitcast.65, s32[32768]{0:T(1024)S(1)} %fusion.28), kind=kCustom, calls=%fused_computation | custom fusion | bytes 4849664 | tf_op jit(solution)/shard_map/jit(_take)/gather | solution.py:94
  292.9 10.2 %copy.290 = f32[32768,18]{0,1:T(8,128)S(1)} copy(f32[32768,18]{1,0:T(8,128)} %gather_fusion) | data formatting | bytes 4718592 | tf_op jit(solution)/shard_map/jit(_take)/gather | solution.py:94
  303.0 0.0 copy-start
  303.0 1.1 select_bitcast_fusion.1
  304.1 1.3 slice_multiply_fusion.12
  305.4 0.0 copy-start.8
  305.4 0.0 copy-start.9
  305.5 1.3 slice_multiply_fusion.11
  306.9 1.3 slice_multiply_fusion.10
  308.3 1.3 slice_multiply_fusion.16
  309.7 1.2 multiply_add_fusion
  311.0 5.6 %fusion.7 = f32[4,32768]{1,0:T(4,128)S(1)} fusion(f32[1,32768]{1,0:T(1,128)S(1)} %get-tuple-element.34, f32[1,32768]{1,0:T(1,128)S(1)} %get-tuple-element.61, f32[1,32768]{1,0:T(1,128)S(1)} %get-tuple-element.33, f32[1,32768]{1,0:T(1,128)S(1)} %get-tuple-element.62, f32[1,32768]{1,0:T(1,128)S(1)} %get-tuple-element.36, f32[1,32768]{1,0:T(1,128)S(1)} %get-tuple-element.58, ...), kind=kLoop, calls=%fused_computation.16 | loop fusion | flops 5767168 | bytes 6422528 | tf_op jit(solution)/shard_map/add | solution.py:62
  316.6 0.3 fusion.53
  317.0 8.9 %copy.296 = f32[32768,8]{1,0:T(8,128)} copy(f32[32768,8]{0,1:T(8,128)S(1)} %fusion.53) | data formatting | bytes 2097152
  325.9 13.3 %concatenate.18.clone = f32[32769,8]{1,0:T(8,128)} pad(f32[32768,8]{1,0:T(8,128)} %copy.296, f32[]{:T(128)} %constant.30.clone.1), padding=0_1x0_0 | pad | bytes 2097188 | tf_op jit(solution)/shard_map/concatenate | solution.py:108
  339.2 114.1 %gather_fusion.1 = f32[32768,8]{1,0:T(8,128)} fusion(f32[32769,8]{1,0:T(8,128)} %concatenate.18.clone, s32[32768]{0:T(1024)S(1)} %copy-done.17), kind=kCustom, calls=%fused_computation.1 | custom fusion | bytes 2228224 | tf_op jit(solution)/shard_map/jit(_take)/gather | solution.py:109
  453.3 17.9 %select_bitcast_fusion = f32[8,32768]{0,1:T(8,128)S(1)} fusion(f32[32768,8]{1,0:T(8,128)} %gather_fusion.1, pred[32768]{0:T(1024)(128)(4,1)S(1)} %copy-done.19), kind=kLoop, calls=%fused_computation.3 | loop fusion | flops 262144 | bytes 2129920 | tf_op jit(solution)/shard_map/jit(_take)/select_n | solution.py:109
  471.2 5.9 %fusion.51 = (f32[8,8192]{0,1:T(8,128)}, f32[8,8192]{0,1:T(8,128)}, f32[8,8192]{0,1:T(8,128)}, f32[8,8192]{0,1:T(8,128)}) fusion(f32[8,32768]{0,1:T(8,128)S(1)} %select_bitcast_fusion), kind=kLoop, calls=%fused_computation.146 | loop fusion | bytes 2097152 | tf_op jit(solution)/shard_map/slice | solution.py:110
  477.1 2.8 copy.292
  479.9 3.5 collective-permute-start.4
  483.4 2.8 copy.293
  486.2 4.8 collective-permute-start.5
  491.0 2.8 copy.294
  493.8 0.1 collective-permute-start.6
  493.9 2.8 copy.295
  496.6 3.9 collective-permute-start.7
  500.6 1.3 pad_maximum_fusion
  501.9 0.0 collective-permute-done.4
  501.9 0.0 collective-permute-done.5
  501.9 0.0 collective-permute-done.6
  501.9 2.6 collective-permute-done.7
  504.4 1.0 pad_maximum_fusion.1
  (42 shorter events, 0.2 us)
Async XLA Ops:
  7.2 130.7 %copy-start.1 = (f32[128,384]{1,0:T(8,128)S(1)}, f32[128,384]{1,0:T(8,128)}, u32[]{:S(2)}) copy-start(f32[128,384]{1,0:T(8,128)} %param.8) | copy-start | bytes 589828
  7.2 130.7 %copy-start.18 = (f32[2,128,384]{2,1,0:T(8,128)S(1)}, f32[2,128,384]{2,1,0:T(8,128)}, u32[]{:S(2)}) copy-start(f32[2,128,384]{2,1,0:T(8,128)} %param.9) | copy-start | bytes 1179652
  7.2 130.7 %all-gather.2.cloned.1.call-start = ((), (), s32[]{:S(2)}) async-start(), calls=%async_computation | async-start | bytes 13369344 | tf_op jit(solution)/shard_map/all_gather | solution.py:68
  139.1 6.1 %collective-permute-start = (f32[2,1,384]{2,1,0:T(1,128)S(1)}, f32[2,1,384]{2,1,0:T(1,128)S(1)}, u32[]{:S(2)}, u32[]{:S(2)}) collective-permute-start(f32[2,1,384]{2,1,0:T(1,128)S(1)} %get-tuple-element.70), channel_id=1, source_target_pairs={{0,16},{16,32},{32,48},{48,64},{64,80},{80,96},{96,112},{112,0},{1... | collective-permute-start | bytes 9224 | tf_op jit(solution)/shard_map/ppermute | solution.py:20
  143.1 5.1 collective-permute-start.1
  148.3 6.7 %collective-permute-start.2 = (f32[2,130,1]{2,1,0:T(8,128)S(1)}, f32[2,130,1]{2,1,0:T(8,128)S(1)}, u32[]{:S(2)}, u32[]{:S(2)}) collective-permute-start(f32[2,130,1]{2,1,0:T(8,128)S(1)} %get-tuple-element.68), channel_id=1, source_target_pairs={{0,1},{1,2},{2,3},{3,4},{4,5},{5,6},{6,7},{7,8},{8,9},{9,10},{10,1... | collective-permute-start | bytes 3128 | tf_op jit(solution)/shard_map/ppermute | solution.py:20
  148.4 6.6 %collective-permute-start.3 = (f32[2,130,1]{2,1,0:T(8,128)S(1)}, f32[2,130,1]{2,1,0:T(8,128)S(1)}, u32[]{:S(2)}, u32[]{:S(2)}) collective-permute-start(f32[2,130,1]{2,1,0:T(8,128)S(1)} %get-tuple-element.69), channel_id=1, source_target_pairs={{1,0},{2,1},{3,2},{4,3},{5,4},{6,5},{7,6},{8,7},{9,8},{10,9},{11,1... | collective-permute-start | bytes 3128 | tf_op jit(solution)/shard_map/ppermute | solution.py:22
  303.0 1.1 copy-start
  305.4 4.2 copy-start.8
  305.4 4.2 copy-start.9
  305.4 4.2 copy-start.10
  305.4 4.2 copy-start.11
  305.5 4.2 copy-start.12
  305.5 4.2 copy-start.13
  305.5 4.2 copy-start.14
  305.5 4.2 copy-start.15
  305.5 4.2 copy-start.16
  308.2 2.7 copy-start.2
  308.2 2.7 copy-start.3
  308.2 2.7 copy-start.4
  308.2 2.7 copy-start.5
  308.3 2.7 copy-start.6
  308.3 2.7 copy-start.7
  325.9 13.3 %copy-start.17 = (s32[32768]{0:T(1024)S(1)}, s32[32768]{0:T(1024)}, u32[]{:S(2)}) copy-start(s32[32768]{0:T(1024)} %fusion.29) | copy-start | bytes 393220
  339.2 114.1 %copy-start.19 = (pred[32768]{0:T(1024)(128)(4,1)S(1)}, pred[32768]{0:T(1024)(128)(4,1)}, u32[]{:S(2)}) copy-start(pred[32768]{0:T(1024)(128)(4,1)} %compare_and_fusion) | copy-start | bytes 98308
  479.9 21.9 %collective-permute-start.4 = (f32[8,8192]{1,0:T(8,128)S(1)}, f32[8,8192]{1,0:T(8,128)S(1)}, u32[]{:S(2)}, u32[]{:S(2)}) collective-permute-start(f32[8,8192]{1,0:T(8,128)S(1)} %copy.292), channel_id=1, source_target_pairs={{0,16},{16,32},{32,48},{48,64},{64,80},{80,96},{96,112},{1,17},{17... | collective-permute-start | bytes 786440 | tf_op jit(solution)/shard_map/ppermute | solution.py:32
  486.2 15.7 %collective-permute-start.5 = (f32[8,8192]{1,0:T(8,128)S(1)}, f32[8,8192]{1,0:T(8,128)S(1)}, u32[]{:S(2)}, u32[]{:S(2)}) collective-permute-start(f32[8,8192]{1,0:T(8,128)S(1)} %copy.293), channel_id=1, source_target_pairs={{16,0},{32,16},{48,32},{64,48},{80,64},{96,80},{112,96},{17,1},{33... | collective-permute-start | bytes 786440 | tf_op jit(solution)/shard_map/ppermute | solution.py:32
  493.8 8.1 %collective-permute-start.6 = (f32[8,8192]{1,0:T(8,128)S(1)}, f32[8,8192]{1,0:T(8,128)S(1)}, u32[]{:S(2)}, u32[]{:S(2)}) collective-permute-start(f32[8,8192]{1,0:T(8,128)S(1)} %copy.294), channel_id=1, source_target_pairs={{0,1},{1,2},{2,3},{3,4},{4,5},{5,6},{6,7},{7,8},{8,9},{9,10},{10,1... | collective-permute-start | bytes 786440 | tf_op jit(solution)/shard_map/ppermute | solution.py:37
  496.6 7.8 %collective-permute-start.7 = (f32[8,8192]{1,0:T(8,128)S(1)}, f32[8,8192]{1,0:T(8,128)S(1)}, u32[]{:S(2)}, u32[]{:S(2)}) collective-permute-start(f32[8,8192]{1,0:T(8,128)S(1)} %copy.295), channel_id=1, source_target_pairs={{0,15},{1,0},{2,1},{3,2},{4,3},{5,4},{6,5},{7,6},{8,7},{9,8},{10,9... | collective-permute-start | bytes 786440 | tf_op jit(solution)/shard_map/ppermute | solution.py:37
Sparse Core Ops, SparseCore 0:
  9.7 74.1 all-gather.1
where the time goes:
time: 514 us; the launch traced here: 512 us
  local copies, waits for them, and re-layouts  421 us (82%)
  other arithmetic  46 us (9%)
  starting transfers between devices  20.7 us (4%)
  between operations  14.6 us (3%)
  waiting for transfers between devices  9.88 us (2%)
    gather x2, local copies, waits for them, and re-layouts, shards(): stencil = jnp.take(neighbours, cells, axis=0).T  127 us
    scatter x1, local copies, waits for them, and re-layouts, shards(): owner = jnp.full((4 * CAP,), count, jnp.int32).at[target].set(jnp.arange(...  120 us
    gather x1, local copies, waits for them, and re-layouts, shards(): outgoing = jnp.take(state_rows, owner, axis=0).T  114 us
    select_n x1, other arithmetic, shards(): outgoing = jnp.take(state_rows, owner, axis=0).T  17.9 us
    unnamed x51, local copies, waits for them, and re-layouts  15.3 us
    reshape x1, local copies, waits for them, and re-layouts, shards(): neighbours = jnp.stack(shifted).reshape(18, num_rows * num_cols).T  13.9 us
    concatenate x1, local copies, waits for them, and re-layouts, shards(): jnp.concatenate([state.T, jnp.zeros((1, 8), jnp.float32)], axis=0)  13.3 us
  transfers between devices with their start and end apart: 9, of which 4 were waited for; matrix products, arithmetic and copies ran while one was open for 27% of the time, Pallas kernels for 0%

commit v1 on v0

v1 whole, which is shorter than its diff:
```python
import jax
import jax.numpy as jnp
from jax import lax
from jax.experimental import pallas as pl
from jax.experimental.pallas import tpu as pltpu
from jax.sharding import PartitionSpec as P

CAP = 8192
ROWS = 128
COLS = 384
BLOCKS = 3
VREGS = 32
PAD_ROWS = 144
PLANE = BLOCKS * PAD_ROWS

step_dt = 0.5
drag_coef = 2.0

f32 = jnp.float32
i32 = jnp.int32


def lane_ids():
    return lax.broadcasted_iota(i32, (8, 128), 1)


def sublane_ids():
    return lax.broadcasted_iota(i32, (8, 128), 0)


def from_lanes(x, index):
    return jnp.take_along_axis(x, index, axis=1, mode="promise_in_bounds")


def from_sublanes(x, index):
    return jnp.take_along_axis(x, index, axis=0, mode="promise_in_bounds")


def bit_set(words, place):
    return lax.shift_left(words, 31 - place) < 0


def lane_pass(xs, distance_bit, flips):
    lane = lane_ids()
    perm = lane ^ lax.shift_left(1, distance_bit)
    place = lax.shift_right_logical(lane, distance_bit) & 1
    uppers = [(place ^ flip) != 0 for flip in flips]
    out = []
    for v, x in enumerate(xs):
        other = from_lanes(x, perm)
        out.append(
            jnp.where(uppers[v % len(uppers)], jnp.maximum(x, other), jnp.minimum(x, other))
        )
    return tuple(out)


def sort_network(key, payloads, index_out, word_out, sub_word_out):
    lane = lane_ids()
    sub = sublane_ids()

    xs = tuple((key[v] & -128) | lane for v in range(VREGS))

    def early_stage(k, xs):
        flip = lax.shift_right_logical(lane, k) & 1

        def one(step, xs):
            return lane_pass(xs, k - 1 - step, (flip,))

        return lax.fori_loop(0, k, one, xs)

    xs = lax.fori_loop(1, 7, early_stage, xs)
    xs = lax.fori_loop(0, 7, lambda step, xs: lane_pass(xs, 6 - step, (0, 1)), xs)
    for v in range(VREGS):
        key[v] = xs[v]
        index = xs[v] & 127
        if index_out is not None:
            index_out[0, v] = index
            word_out[v] = jnp.zeros((8, 128), i32)
            sub_word_out[v] = jnp.zeros((8, 128), i32)
        for payload in payloads:
            payload[v] = from_lanes(payload[v], index)

    def stage(t, carry):
        def flip_of(v):
            return -(lax.shift_right_logical(sub * 32 + v, t) & 1)

        for v in range(VREGS):
            key[v] = key[v] ^ flip_of(v)

        for i in (7, 6, 5):

            @pl.when(i < t)
            def _():
                near = i - 5
                perm = sub ^ (1 << near)
                upper = (lax.shift_right_logical(sub, near) & 1) != 0
                place = jnp.where(t == 6, 0, jnp.where(t == 7, 1, 3)) + t - 1 - i
                for v in range(VREGS):
                    x = key[v]
                    other = from_sublanes(x, perm)
                    take = jnp.where(upper, other, x) > jnp.where(upper, x, other)
                    key[v] = jnp.where(take, other, x)
                    if index_out is not None:
                        sub_word_out[v] = sub_word_out[v] | jnp.where(
                            take, lax.shift_left(1, place), 0
                        )
                    for payload in payloads:
                        y = payload[v]
                        payload[v] = jnp.where(take, from_sublanes(y, perm), y)

        for i in (4, 3, 2, 1, 0):

            @pl.when(i < t)
            def _():
                place = jnp.where(t <= 5, t * (t - 1) // 2, 5 * t - 15) + t - 1 - i
                place = jnp.where(t <= 5, place, 5 * t - 15 + 4 - i)
                for a in range(VREGS):
                    if a & (1 << i):
                        continue
                    b = a | (1 << i)
                    x, y = key[a], key[b]
                    swap = x > y
                    key[a] = jnp.minimum(x, y)
                    key[b] = jnp.maximum(x, y)
                    if index_out is not None:
                        word_out[a] = word_out[a] | jnp.where(swap, lax.shift_left(1, place), 0)
                    for payload in payloads:
                        x, y = payload[a], payload[b]
                        payload[a] = jnp.where(swap, y, x)
                        payload[b] = jnp.where(swap, x, y)

        xs = []
        for v in range(VREGS):
            flip = flip_of(v)
            xs.append((((key[v] ^ flip) & -128) | lane) ^ flip)
        xs = lax.fori_loop(0, 7, lambda step, xs: lane_pass(xs, 6 - step, (0,)), tuple(xs))
        for v in range(VREGS):
            x = xs[v] ^ flip_of(v)
            key[v] = x
            index = x & 127
            if index_out is not None:
                index_out[t, v] = index
            for payload in payloads:
                payload[v] = from_lanes(payload[v], index)
        return carry

    lax.fori_loop(1, 9, stage, 0)


def row_place(t, i):
    return t * (t - 1) // 2 + t - 1 - i if t <= 5 else 5 * t - 15 + 4 - i


def sub_place(t, i):
    return {6: 0, 7: 1, 8: 3}[t] + t - 1 - i


def apply_network(xs, index, words, sub_words):
    sub = sublane_ids()
    xs = [from_lanes(xs[v], index[0, v]) for v in range(VREGS)]
    for t in range(1, 9):
        for i in range(t - 1, -1, -1):
            if i >= 5:
                perm = sub ^ (1 << (i - 5))
                place = sub_place(t, i)
                xs = [
                    jnp.where(bit_set(sub_words[v], place), from_sublanes(xs[v], perm), xs[v])
                    for v in range(VREGS)
                ]
            else:
                place = row_place(t, i)
                for a in range(VREGS):
                    if a & (1 << i):
                        continue
                    b = a | (1 << i)
                    swap = bit_set(words[a], place)
                    x, y = xs[a], xs[b]
                    xs[a] = jnp.where(swap, y, x)
                    xs[b] = jnp.where(swap, x, y)
        xs = [from_lanes(xs[v], index[t, v]) for v in range(VREGS)]
    return xs


def plan_kernel(
    cells, offsets, moves, slots,
    near_out, frac_out, counts_out,
    index_a, word_a, sub_a, index_b, word_b, sub_b,
    key, tags,
):
    lane = lane_ids()
    sub = sublane_ids()
    stay = jnp.where(moves[...] == 0, 1.0, 0.0)
    before = jnp.where(
        lax.broadcasted_iota(i32, (128, 128), 0) < lax.broadcasted_iota(i32, (128, 128), 1), 1.0, 0.0
    )
    rank = jnp.dot(stay, before, preferred_element_type=f32)
    above = jnp.where(
        lax.broadcasted_iota(i32, (256, 256), 1) < lax.broadcasted_iota(i32, (256, 256), 0), 1.0, 0.0
    )
    totals = jnp.broadcast_to(jnp.sum(stay, axis=1, keepdims=True), (256, 128))
    rank = rank + jnp.dot(above, totals, preferred_element_type=f32)
    rank = rank.astype(i32)
    counts = []
    for k in range(4):
        count = jnp.sum(jnp.where(moves[...] == k + 1, 1.0, 0.0)).astype(i32)
        counts.append(count)
        counts_out[k] = count
    hole = rank + counts[0]
    filled = counts[0]
    for k in range(1, 4):
        hole = hole + jnp.where(rank >= k * CAP - filled, counts[k], 0)
        filled = filled + counts[k]
    target = jnp.where(moves[...] > 0, (moves[...] - 1) * CAP + slots[...], hole)
    number = lax.broadcasted_iota(i32, (256, 128), 0) * 128 + lax.broadcasted_iota(i32, (256, 128), 1)
    cell = cells[...]
    row = (cell.astype(f32) * (1.0 / COLS)).astype(i32)
    row = row - jnp.where(row * COLS > cell, 1, 0)
    row = row + jnp.where((row + 1) * COLS <= cell, 1, 0)
    col = cell - row * COLS
    spot = lax.shift_right_logical(col, 7) * (ROWS * 128) + row * 128 + (col & 127)
    for v in range(VREGS):
        part = slice(v * 8, v * 8 + 8)
        key[v] = lax.shift_left(spot[part], 7)
        tags[v] = lax.shift_left(target[part], 15) | number[part]
        frac_out[0, v] = offsets[0, part]
        frac_out[1, v] = offsets[1, part]
    sort_network(key, (frac_out.at[0], frac_out.at[1], tags), None, None, None)
    for v in range(VREGS):
        near_out[v] = lax.shift_right_logical(key[v], 7)
        key[v] = lax.shift_left(lax.shift_right_logical(tags[v], 15), 7)
    sort_network(key, (), index_a, word_a, sub_a)
    for v in range(VREGS):
        key[v] = lax.shift_left(tags[v] & 32767, 7)
    sort_network(key, (), index_b, word_b, sub_b)


def plan(cells, offsets, moves, slots):
    vmem = pl.BlockSpec(memory_space=pltpu.VMEM)
    smem = pl.BlockSpec(memory_space=pltpu.SMEM)
    network = [
        jax.ShapeDtypeStruct((9, VREGS, 8, 128), i32),
        jax.ShapeDtypeStruct((VREGS, 8, 128), i32),
        jax.ShapeDtypeStruct((VREGS, 8, 128), i32),
    ]
    return pl.pallas_call(
        plan_kernel,
        out_shape=[
            jax.ShapeDtypeStruct((VREGS, 8, 128), i32),
            jax.ShapeDtypeStruct((2, VREGS, 8, 128), f32),
            jax.ShapeDtypeStruct((4,), i32),
        ]
        + network
        + network,
        in_specs=[vmem] * 4,
        out_specs=[vmem, vmem, smem] + [vmem] * 6,
        scratch_shapes=[pltpu.VMEM((VREGS, 8, 128), i32), pltpu.VMEM((VREGS, 8, 128), i32)],
        compiler_params=pltpu.CompilerParams(vmem_limit_bytes=32 << 20),
        cost_estimate=pl.CostEstimate(flops=20_000_000, bytes_accessed=8_000_000, transcendentals=0),
        name="plan",
    )(cells.reshape(256, 128), offsets.reshape(2, 256, 128), moves.reshape(256, 128), slots.reshape(256, 128))


def velocity_kernel(forcing, mass, momentum, out):
    heavy = mass[...]
    for part in range(2):
        current = forcing[:, part].reshape(ROWS, COLS)
        stress = forcing[:, 2 + part].reshape(ROWS, COLS)
        out[part] = (momentum[part] + step_dt * stress + step_dt * drag_coef * heavy * current) / (
            heavy * (1.0 + step_dt * drag_coef)
        )


def node_velocity(forcing, mass, momentum):
    vmem = pl.BlockSpec(memory_space=pltpu.VMEM)
    return pl.pallas_call(
        velocity_kernel,
        out_shape=jax.ShapeDtypeStruct((2, ROWS, COLS), f32),
        in_specs=[vmem] * 3,
        out_specs=vmem,
        name="velocity",
    )(forcing, mass, momentum)


def table_kernel(velocity, west, east, table, first_edge, last_edge):
    lane = lax.broadcasted_iota(i32, (ROWS, 128), 1)
    for part in range(2):
        blocks = [velocity[part, :, 128 * k : 128 * k + 128] for k in range(BLOCKS)]
        left = [west[part]] + blocks[:-1]
        right = blocks[1:] + [east[part]]
        for k in range(BLOCKS):
            shifted = [
                jnp.where(lane == 0, pltpu.roll(left[k], 1, 1), pltpu.roll(blocks[k], 1, 1)),
                blocks[k],
                jnp.where(lane == 127, pltpu.roll(right[k], 127, 1), pltpu.roll(blocks[k], 127, 1)),
            ]
            for q in range(3):
                plane = part * 3 + q
                table[plane, k] = shifted[q]
                first_edge[plane, k] = shifted[q][0:1]
                last_edge[plane, k] = shifted[q][ROWS - 1 : ROWS]


def node_table(velocity, west, east):
    vmem = pl.BlockSpec(memory_space=pltpu.VMEM)
    return pl.pallas_call(
        table_kernel,
        out_shape=[
            jax.ShapeDtypeStruct((6, BLOCKS, ROWS, 128), f32),
            jax.ShapeDtypeStruct((6, BLOCKS, 1, 128), f32),
            jax.ShapeDtypeStruct((6, BLOCKS, 1, 128), f32),
        ],
        in_specs=[vmem] * 3,
        out_specs=[vmem] * 3,
        name="table",
    )(velocity, west, east)


def spline(frac):
    lower = 0.5 * (0.5 - frac) * (0.5 - frac)
    middle = 0.75 - frac * frac
    upper = 0.5 * (0.5 + frac) * (0.5 + frac)
    return (lower, middle, upper)


def transfer_kernel(
    first, last, spans, counts,
    table, above, below, near, frac, index, words, sub_words,
    state, north, south, east, west,
    nodes, samples, columns,
):
    nodes[6 * PLANE : 8 * PLANE, :] = jnp.zeros((2 * PLANE, 128), f32)
    for plane in range(6):
        for k in range(BLOCKS):
            base = plane * PLANE + k * PAD_ROWS
            nodes[base + 8 : base + 8 + ROWS, :] = table[plane, k]
            nodes[base + 7 : base + 8, :] = above[plane, k]
            nodes[base + 8 + ROWS : base + 9 + ROWS, :] = below[plane, k]

    def group(v, carry):
        def chunk(step, sums):
            sums = list(sums)
            for s in range(8):
                block = v * 8 + s
                here = jnp.minimum(first[block] + step, last[block])
                base = here + lax.shift_right_logical(here, 7) * 16 + 8
                spot = near[pl.ds(block, 8, stride=0), :]
                lanes = spot & 127
                inside = lax.shift_right_logical(spot, 7) == here
                for r in range(3):
                    got = from_lanes(nodes[pl.ds(base + r - 1, 8, stride=PLANE), :], lanes)
                    sums[3 * s + r] = jnp.where(inside, got, sums[3 * s + r])
            return tuple(sums)

        sums = lax.fori_loop(0, spans[v], chunk, tuple(jnp.zeros((8, 128), f32) for _ in range(24)))
        for s in range(8):
            for r in range(3):
                samples[pl.ds(r * 2048 + v * 8 + s, 8, stride=256), :] = sums[3 * s + r]
        here = pl.ds(pl.multiple_of(v * 8, 8), 8)
        d_row = frac[0, v]
        d_col = frac[1, v]
        w_row = spline(d_row)
        w_col = spline(d_col)
        arm_row = [4.0 * w_row[r] * (r - 1 - d_row) for r in range(3)]
        arm_col = [4.0 * w_col[q] * (q - 1 - d_col) for q in range(3)]
        speeds = []
        affines = []
        for part in range(2):
            speed = along_row = along_col = None
            for q in range(3):
                plane = part * 3 + q
                got = [
                    samples[pl.ds(pl.multiple_of(r * 2048 + plane * 256 + v * 8, 8), 8), :]
                    for r in range(3)
                ]
                plain = w_row[0] * got[0] + w_row[1] * got[1] + w_row[2] * got[2]
                tilted = arm_row[0] * got[0] + arm_row[1] * got[1] + arm_row[2] * got[2]
                terms = (w_col[q] * plain, w_col[q] * tilted, arm_col[q] * plain)
                if q == 0:
                    speed, along_row, along_col = terms
                else:
                    speed = speed + terms[0]
                    along_row = along_row + terms[1]
                    along_col = along_col + terms[2]
            speeds.append(speed)
            affines += [along_row, along_col]
        values = [d_row + step_dt * speeds[0], d_col + step_dt * speeds[1]] + speeds + affines
        for c in range(8):
            state[c, v] = values[c]
        return carry

    lax.fori_loop(0, VREGS, group, 0)

    lane = lane_ids()
    sub = sublane_ids()

    def component(c, carry):
        xs = apply_network([state[c, v] for v in range(VREGS)], index, words, sub_words)
        direction = lax.shift_right_logical(sub, 1)
        count = jnp.where(
            direction < 2,
            jnp.where(direction == 0, counts[0], counts[1]),
            jnp.where(direction == 2, counts[2], counts[3]),
        )
        slot = (sub & 1) * 4096 + lane
        for v in range(VREGS):
            kept = jnp.where(slot + v * 128 < count, xs[v], 0.0)
            columns[pl.ds(v * 8 + c, 8, stride=256), :] = kept
        return carry

    lax.fori_loop(0, 8, component, 0)
    for k, out in enumerate((north, south, east, west)):
        for j in range(64):
            base = (k * 64 + j) * 8
            out[:, 128 * j : 128 * j + 128] = columns[base : base + 8, :]


def transfer(bounds, spans, counts, table, above, below, near, frac, network):
    vmem = pl.BlockSpec(memory_space=pltpu.VMEM)
    smem = pl.BlockSpec(memory_space=pltpu.SMEM)
    return pl.pallas_call(
        transfer_kernel,
        out_shape=[jax.ShapeDtypeStruct((8, VREGS, 8, 128), f32)]
        + [jax.ShapeDtypeStruct((8, CAP), f32)] * 4,
        in_specs=[smem] * 4 + [vmem] * 8,
        out_specs=[vmem] * 5,
        scratch_shapes=[
            pltpu.VMEM((8 * PLANE, 128), f32),
            pltpu.VMEM((3 * 2048, 128), f32),
            pltpu.VMEM((2048, 128), f32),
        ],
        compiler_params=pltpu.CompilerParams(vmem_limit_bytes=40 << 20),
        cost_estimate=pl.CostEstimate(flops=20_000_000, bytes_accessed=8_000_000, transcendentals=0),
        name="transfer",
    )(bounds[0], bounds[1], spans, counts, table, above, below, near.reshape(256, 128), frac, *network)


def restore_kernel(state, index, words, sub_words, out, columns):
    def component(c, carry):
        xs = apply_network([state[c, v] for v in range(VREGS)], index, words, sub_words)
        for v in range(VREGS):
            columns[pl.ds(v * 8 + c, 8, stride=256), :] = xs[v]
        return carry

    lax.fori_loop(0, 8, component, 0)
    for j in range(256):
        out[:, 128 * j : 128 * j + 128] = columns[8 * j : 8 * j + 8, :]


def restore(state, network):
    vmem = pl.BlockSpec(memory_space=pltpu.VMEM)
    return pl.pallas_call(
        restore_kernel,
        out_shape=jax.ShapeDtypeStruct((8, 4 * CAP), f32),
        in_specs=[vmem] * 4,
        out_specs=vmem,
        scratch_shapes=[pltpu.VMEM((2048, 128), f32)],
        compiler_params=pltpu.CompilerParams(vmem_limit_bytes=32 << 20),
        cost_estimate=pl.CostEstimate(flops=10_000_000, bytes_accessed=4_000_000, transcendentals=0),
        name="restore",
    )(state, *network)


def from_behind(block, axis, distance):
    devices = range(lax.axis_size(axis))
    route = [(i - distance, i) for i in devices if i - distance in devices]
    return lax.ppermute(block, axis, route)


def passed_along(value, axis, by):
    count = lax.axis_size(axis)
    return lax.ppermute(value, axis, [(i, (i + by) % count) for i in range(count)])


def shards(ocean, grid_mass, grid_momentum, cells, offsets, moves, slots):
    outgoing = ocean.reshape(4, 8, 16, COLS).transpose(2, 0, 1, 3)
    forcing = lax.all_to_all(outgoing, "lon", 0, 0)
    planned = plan(cells, offsets, moves, slots)
    near, frac, counts = planned[:3]
    slot_network, home_network = planned[3:6], planned[6:9]
    ends = lax.shift_right_logical(near.reshape(256, 128), 7)
    bounds = (ends[:, 0], ends[:, 127])
    spans = jnp.max((bounds[1] - bounds[0]).reshape(VREGS, 8), axis=1) + 1
    velocity = node_velocity(forcing, grid_mass, grid_momentum)
    west = passed_along(velocity[:, :, COLS - 128 :], "lon", 1)
    east = passed_along(velocity[:, :, :128], "lon", -1)
    table, first_edge, last_edge = node_table(velocity, west, east)
    above = from_behind(last_edge, "lat", 1)
    below = from_behind(first_edge, "lat", -1)
    state, north, south, east, west = transfer(
        bounds, spans, counts, table, above, below, near, frac, slot_network
    )
    north = from_behind(north, "lat", 1)
    south = from_behind(south, "lat", -1)
    east = passed_along(east, "lon", 1)
    west = passed_along(west, "lon", -1)
    parcels = restore(state, home_network)
    return (parcels, jnp.concatenate([north, south, east, west], axis=1))


def solution(mesh):
    in_specs = (
        P(None, ("lat", "lon"), None),
        P("lat", "lon"),
        P(None, "lat", "lon"),
        P(("lat", "lon")),
        P(None, ("lat", "lon")),
        P(("lat", "lon")),
        P(("lat", "lon")),
    )
    out_specs = (P(None, ("lat", "lon")), P(None, ("lat", "lon")))
    return jax.shard_map(shards, mesh=mesh, in_specs=in_specs, out_specs=out_specs, check_vma=False)
```

time: 514 us -> 127 us (0.25)
  local copies, waits for them, and re-layouts: 421 us -> 7.12 us
  Pallas kernels: 0 us -> 77.4 us
  other arithmetic: 46 us -> 2.15 us
  between operations: 14.6 us -> 0.79 us
  starting transfers between devices: 20.7 us -> 30.1 us
    gather x3 -> x0, local copies, waits for them, and re-layouts: 241 us -> none  [the longest x2 127 us: shards(): stencil = jnp.take(neighbours, cells, axis=0).T]
    scatter x1 -> x0, local copies, waits for them, and re-layouts: 120 us -> none  [shards(): owner = jnp.full((4 * CAP,), count, jnp.int32).at[target].set(jnp.arange(...]
    pallas_call x0 -> x5, Pallas kernels: none -> 77.4 us  [the longest x1 35.8 us: plan(): pl.pallas_call(plan_kernel, out_shape=[jax.ShapeDtypeStruct((VREGS, 8, 12...]
    select_n x4 -> x0, other arithmetic: 20.3 us -> none  [the longest x1 17.9 us: shards(): outgoing = jnp.take(state_rows, owner, axis=0).T]
    slice x6 -> x1, local copies, waits for them, and re-layouts: 17.1 us -> 1.72 us  [shards(): east = passed_along(velocity[:, :, :128], 'lon', -1)]
    concatenate x1 -> x0, local copies, waits for them, and re-layouts: 13.3 us -> none  [shards(): jnp.concatenate([state.T, jnp.zeros((1, 8), jnp.float32)], axis=0)]
    unnamed x51 -> x19, local copies, waits for them, and re-layouts: 15.3 us -> 2.61 us
    reshape x1, local copies, waits for them, and re-layouts: 13.9 us -> 2.1 us  [shards(): outgoing = ocean.reshape(4, 8, 16, COLS).transpose(2, 0, 1, 3)]
  transfers between devices with their start and end apart: 9 -> 9, of which waited for: 4 -> 3; matrix products, arithmetic and copies ran while one was open for 27% -> 1% of each run, Pallas kernels for 0% -> 37%
where the time goes in v1:
time: 127 us
  Pallas kernels  77.4 us (61%)
  starting transfers between devices  30.1 us (24%)
  waiting for transfers between devices  9.4 us (7%)
  local copies, waits for them, and re-layouts  7.12 us (6%)
  other arithmetic  2.15 us (2%)
    pallas_call x1, Pallas kernels, plan(): pl.pallas_call(plan_kernel, out_shape=[jax.ShapeDtypeStruct((VREGS, 8, 12...  35.8 us
    pallas_call x1, Pallas kernels, transfer(): pl.pallas_call(transfer_kernel, out_shape=[jax.ShapeDtypeStruct((8, VREGS...  25.7 us
    ppermute x4, starting transfers between devices, from_behind(): return lax.ppermute(block, axis, route)  16.5 us
    pallas_call x1, Pallas kernels, restore(): pl.pallas_call(restore_kernel, out_shape=jax.ShapeDtypeStruct((8, 4 * CAP...  11.3 us
    ppermute x4, starting transfers between devices, passed_along(): lax.ppermute(value, axis, [(i, (i + by) % count) for i in range(count)])  7.67 us
    all_to_all x1, starting transfers between devices, shards(): forcing = lax.all_to_all(outgoing, 'lon', 0, 0)  5.95 us
    ppermute x4, waiting for transfers between devices, passed_along(): lax.ppermute(value, axis, [(i, (i + by) % count) for i in range(count)])  4.91 us
    ppermute x4, waiting for transfers between devices, from_behind(): return lax.ppermute(block, axis, route)  4.49 us
  transfers between devices with their start and end apart: 9, of which 3 were waited for; matrix products, arithmetic and copies ran while one was open for 1% of the time, Pallas kernels for 37%

profile of v1, /device:TPU:8, one launch (start us, length us, event | category | flops | bytes accessed | tf_op | source)
XLA Modules:
  0.0 127.0 jit_solution(13041030359229822062)
XLA Ops:
  0.6 2.1 %copy.14 = f32[4,1,16,8,384]{4,3,1,0,2:T(8,128)} copy(f32[4,1,16,8,384]{4,3,2,1,0:T(8,128)} %bitcast.21) | data formatting | bytes 1572864 | tf_op jit(solution)/shard_map/reshape | solution.py:475
  2.7 0.0 copy-start.6
  2.7 0.0 copy-start.1
  2.7 0.0 copy-start.2
  2.7 0.0 copy-start.3
  2.7 5.9 %all-to-all-start = ((f32[16,4,8,384]{3,2,1,0:T(8,128)}), f32[16,4,8,384]{3,2,1,0:T(8,128)}, u32[]{:S(2)}, u32[]{:S(2)}) async-start(f32[16,4,8,384]{3,2,1,0:T(8,128)} %bitcast.14), calls=%async_computation | async-start | bytes 1572864 | tf_op jit(solution)/shard_map/all_to_all | solution.py:476
  8.7 0.0 copy-done.6
  8.7 0.0 copy-done.1
  8.7 0.0 copy-done.2
  8.7 0.0 copy-done.3
  8.8 35.8 %plan.1 = (s32[32,8,128]{2,1,0:T(8,128)S(1)}, f32[2,32,8,128]{3,2,1,0:T(8,128)S(1)}, s32[4]{0:T(128)S(1)}, s32[9,32,8,128]{3,2,1,0:T(8,128)S(1)}, s32[32,8,128]{...) custom-call(s32[256,128]{1,0:T(8,128)S(1)} %bitcast.18, ...), custom_call_target="tpu_custom_call" | custom-call | flops 20000000 | bytes 8000000 | tf_op jit(solution)/shard_map/plan/pallas_call | solution.py:245
  44.5 0.0 copy-start.4
  44.6 0.6 copy-done.4
  45.2 0.0 all-to-all-done.forcing
  45.2 2.2 %velocity.1 = f32[2,128,384]{2,1,0:T(8,128)} custom-call(f32[16,4,8,384]{3,2,1,0:T(8,128)} %all-to-all-done.forcing, f32[128,384]{1,0:T(8,128)} %mass.1, f32[2,128,384]{2,1,0:T(8,128)} %momentum.1), custom_call_target="tpu_custom_call" | custom-call | tf_op jit(solution)/shard_map/velocity/pallas_call | solution.py:275
  47.4 0.0 copy-start.5
  47.4 1.7 %fusion = (f32[2,128,128]{2,1,0:T(8,128)}, f32[2,128,128]{2,1,0:T(8,128)}) fusion(f32[2,128,384]{2,1,0:T(8,128)} %velocity.1), kind=kLoop, calls=%fused_computation.8 | loop fusion | bytes 524288 | tf_op jit(solution)/shard_map/slice | solution.py:485
  49.1 3.7 %collective-permute-start.1 = (f32[2,128,128]{2,1,0:T(8,128)}, f32[2,128,128]{2,1,0:T(8,128)S(1)}, u32[]{:S(2)}, u32[]{:S(2)}) collective-permute-start(f32[2,128,128]{2,1,0:T(8,128)} %get-tuple-element.39), channel_id=1, source_target_pairs={{0,15},{1,0},{2,1},{3,2},{4,3},{5,4},{6,5},{7,6},{8,7},{9,8},{10,9... | collective-permute-start | bytes 393224 | tf_op jit(solution)/shard_map/ppermute | solution.py:471
  52.8 0.0 collective-permute-start
  52.9 0.3 subtract_reduce_fusion
  53.1 0.7 sub.12
  53.8 0.8 reduce_max.9
  54.6 1.0 collective-permute-done.1.east
  55.7 0.0 copy-start.7
  55.7 3.9 %collective-permute-done.west = f32[2,128,128]{2,1,0:T(8,128)S(1)} collective-permute-done((f32[2,128,128]{2,1,0:T(8,128)}, f32[2,128,128]{2,1,0:T(8,128)S(1)}, u32[]{:S(2)}, u32[]{:S(2)}) %collective-permute-start) | collective-permute-done | bytes 131104 | tf_op jit(solution)/shard_map/ppermute | solution.py:471
  59.6 0.0 copy-done.7
  59.6 0.0 copy-start.8
  59.6 0.7 copy-done.8
  60.2 2.5 %table.1 = (f32[6,3,128,128]{3,2,1,0:T(8,128)}, f32[6,3,1,128]{3,2,1,0:T(1,128)}, f32[6,3,1,128]{3,2,1,0:T(1,128)}) custom-call(f32[2,128,384]{2,1,0:T(8,128)} %velocity.1, f32[2,128,128]{2,1,0:T(8,128)} %copy-done.8, f32[2,128,128]{2,1,0:T(8,128)} %copy-done.7), custom_call_target="tpu_custom_call" | custom-call | tf_op jit(solution)/shard_map/table/pallas_call | solution.py:305
  62.7 5.5 %collective-permute-start.2 = (f32[6,3,1,128]{3,2,1,0:T(1,128)}, f32[6,3,1,128]{3,2,1,0:T(1,128)S(1)}, u32[]{:S(2)}, u32[]{:S(2)}) collective-permute-start(f32[6,3,1,128]{3,2,1,0:T(1,128)} %get-tuple-element.22), channel_id=1, source_target_pairs={{0,16},{16,32},{32,48},{48,64},{64,80},{80,96},{96,112},{1,17},{17... | collective-permute-start | bytes 27656 | tf_op jit(solution)/shard_map/ppermute | solution.py:466
  68.2 2.8 %collective-permute-start.3 = (f32[6,3,1,128]{3,2,1,0:T(1,128)}, f32[6,3,1,128]{3,2,1,0:T(1,128)S(1)}, u32[]{:S(2)}, u32[]{:S(2)}) collective-permute-start(f32[6,3,1,128]{3,2,1,0:T(1,128)} %get-tuple-element.23), channel_id=1, source_target_pairs={{16,0},{32,16},{48,32},{64,48},{80,64},{96,80},{112,96},{17,1},{33... | collective-permute-start | bytes 27656 | tf_op jit(solution)/shard_map/ppermute | solution.py:466
  70.9 0.0 collective-permute-done.2.above
  70.9 4.5 %collective-permute-done.3.below = f32[6,3,1,128]{3,2,1,0:T(1,128)S(1)} collective-permute-done((f32[6,3,1,128]{3,2,1,0:T(1,128)}, f32[6,3,1,128]{3,2,1,0:T(1,128)S(1)}, u32[]{:S(2)}, u32[]{:S(2)}) %collective-permute-start.3) | collective-permute-done | bytes 9248 | tf_op jit(solution)/shard_map/ppermute | solution.py:466
  75.4 0.0 copy-done.5
  75.4 0.0 copy-start
  75.4 1.3 copy-done
  76.7 25.7 %transfer.1 = (f32[8,32,8,128]{3,2,1,0:T(8,128)S(1)}, f32[8,8192]{1,0:T(8,128)S(1)}, f32[8,8192]{1,0:T(8,128)S(1)}, f32[8,8192]{1,0:T(8,128)S(1)}, f32[8,8192]{1,0:T(8,128)S(1)}) custom-call(s32[256]{0:T(256)S(1)} %get-tuple-element.38.first, s32[256]{0:T(256)S(1)} %get-tuple-element.37.last, s32[32]{0:T(128)S(1)} %broadcast_add_fusion.spans, ...), custom_call_target="tpu_custom_call" | custom-call | flops 20000000 | bytes 8000000 | tf_op jit(solution)/shard_map/transfer/pallas_call | solution.py:420
  102.5 3.8 %collective-permute-start.4 = (f32[8,8192]{1,0:T(8,128)S(1)}, f32[8,8192]{1,0:T(8,128)S(1)}, u32[]{:S(2)}, u32[]{:S(2)}) collective-permute-start(f32[8,8192]{1,0:T(8,128)S(1)} %get-tuple-element.32), channel_id=1, source_target_pairs={{0,16},{16,32},{32,48},{48,64},{64,80},{80,96},{96,112},{1,17},{17... | collective-permute-start | bytes 786440 | tf_op jit(solution)/shard_map/ppermute | solution.py:466
  106.3 4.4 %collective-permute-start.5 = (f32[8,8192]{1,0:T(8,128)S(1)}, f32[8,8192]{1,0:T(8,128)S(1)}, u32[]{:S(2)}, u32[]{:S(2)}) collective-permute-start(f32[8,8192]{1,0:T(8,128)S(1)} %get-tuple-element.33), channel_id=1, source_target_pairs={{16,0},{32,16},{48,32},{64,48},{80,64},{96,80},{112,96},{17,1},{33... | collective-permute-start | bytes 786440 | tf_op jit(solution)/shard_map/ppermute | solution.py:466
  110.7 0.1 collective-permute-start.6
  110.8 3.8 %collective-permute-start.7 = (f32[8,8192]{1,0:T(8,128)S(1)}, f32[8,8192]{1,0:T(8,128)S(1)}, u32[]{:S(2)}, u32[]{:S(2)}) collective-permute-start(f32[8,8192]{1,0:T(8,128)S(1)} %get-tuple-element.35), channel_id=1, source_target_pairs={{0,15},{1,0},{2,1},{3,2},{4,3},{5,4},{6,5},{7,6},{8,7},{9,8},{10,9... | collective-permute-start | bytes 786440 | tf_op jit(solution)/shard_map/ppermute | solution.py:471
  114.6 11.3 %restore.1 = f32[8,32768]{1,0:T(8,128)} custom-call(f32[8,32,8,128]{3,2,1,0:T(8,128)S(1)} %get-tuple-element.28.state, s32[9,32,8,128]{3,2,1,0:T(8,128)S(1)} %get-tuple-element.29.index, s32[32,8,128]{2,1,0:T(8,128)S(1)} %get-tuple-element.30.words, s32[32,8,128]{2,1,0:T(8,128)S(1)} %get-tuple-element.31.sub_words), custom_call_target="tpu_custom_call" | custom-call | flops 10000000 | bytes 4000000 | tf_op jit(solution)/shard_map/restore/pallas_call | solution.py:451
  125.9 0.0 collective-permute-done.4
  125.9 0.0 collective-permute-done.5
  125.9 0.0 collective-permute-done.6
  125.9 0.0 collective-permute-done.7
  125.9 1.0 pad_maximum_fusion
  (3 shorter events, 0.0 us)
Async XLA Ops:
  2.7 6.0 %copy-start.6 = (f32[2,32768]{1,0:T(2,128)S(1)}, f32[2,32768]{1,0:T(2,128)}, u32[]{:S(2)}) copy-start(f32[2,32768]{1,0:T(2,128)} %param.11) | copy-start | bytes 786436
  2.7 6.0 %copy-start.1 = (s32[32768]{0:T(1024)S(1)}, s32[32768]{0:T(1024)}, u32[]{:S(2)}) copy-start(s32[32768]{0:T(1024)} %param.10) | copy-start | bytes 393220
  2.7 6.0 %copy-start.2 = (s32[32768]{0:T(1024)S(1)}, s32[32768]{0:T(1024)}, u32[]{:S(2)}) copy-start(s32[32768]{0:T(1024)} %param.12) | copy-start | bytes 393220
  2.7 6.0 %copy-start.3 = (s32[32768]{0:T(1024)S(1)}, s32[32768]{0:T(1024)}, u32[]{:S(2)}) copy-start(s32[32768]{0:T(1024)} %param.13) | copy-start | bytes 393220
  2.7 42.5 %all-to-all-start = ((f32[16,4,8,384]{3,2,1,0:T(8,128)}), f32[16,4,8,384]{3,2,1,0:T(8,128)}, u32[]{:S(2)}, u32[]{:S(2)}) async-start(f32[16,4,8,384]{3,2,1,0:T(8,128)} %bitcast.14), calls=%async_computation | async-start | bytes 1572864 | tf_op jit(solution)/shard_map/all_to_all | solution.py:476
  44.5 0.7 copy-start.4
  47.4 28.1 %copy-start.5 = (s32[32,8,128]{2,1,0:T(8,128)S(1)}, s32[32,8,128]{2,1,0:T(8,128)}, u32[]{:S(2)}) copy-start(s32[32,8,128]{2,1,0:T(8,128)} %copy-done.4) | copy-start | bytes 393220
  49.1 6.6 %collective-permute-start.1 = (f32[2,128,128]{2,1,0:T(8,128)}, f32[2,128,128]{2,1,0:T(8,128)S(1)}, u32[]{:S(2)}, u32[]{:S(2)}) collective-permute-start(f32[2,128,128]{2,1,0:T(8,128)} %get-tuple-element.39), channel_id=1, source_target_pairs={{0,15},{1,0},{2,1},{3,2},{4,3},{5,4},{6,5},{7,6},{8,7},{9,8},{10,9... | collective-permute-start | bytes 393224 | tf_op jit(solution)/shard_map/ppermute | solution.py:471
  52.8 6.7 %collective-permute-start = (f32[2,128,128]{2,1,0:T(8,128)}, f32[2,128,128]{2,1,0:T(8,128)S(1)}, u32[]{:S(2)}, u32[]{:S(2)}) collective-permute-start(f32[2,128,128]{2,1,0:T(8,128)} %get-tuple-element.40), channel_id=1, source_target_pairs={{0,1},{1,2},{2,3},{3,4},{4,5},{5,6},{6,7},{7,8},{8,9},{9,10},{10,1... | collective-permute-start | bytes 393224 | tf_op jit(solution)/shard_map/ppermute | solution.py:471
  55.7 3.9 %copy-start.7 = (f32[2,128,128]{2,1,0:T(8,128)}, f32[2,128,128]{2,1,0:T(8,128)S(1)}, u32[]{:S(2)}) copy-start(f32[2,128,128]{2,1,0:T(8,128)S(1)} %collective-permute-done.1.east) | copy-start | bytes 393220
  59.6 0.7 copy-start.8
  62.7 8.3 %collective-permute-start.2 = (f32[6,3,1,128]{3,2,1,0:T(1,128)}, f32[6,3,1,128]{3,2,1,0:T(1,128)S(1)}, u32[]{:S(2)}, u32[]{:S(2)}) collective-permute-start(f32[6,3,1,128]{3,2,1,0:T(1,128)} %get-tuple-element.22), channel_id=1, source_target_pairs={{0,16},{16,32},{32,48},{48,64},{64,80},{80,96},{96,112},{1,17},{17... | collective-permute-start | bytes 27656 | tf_op jit(solution)/shard_map/ppermute | solution.py:466
  68.2 7.3 %collective-permute-start.3 = (f32[6,3,1,128]{3,2,1,0:T(1,128)}, f32[6,3,1,128]{3,2,1,0:T(1,128)S(1)}, u32[]{:S(2)}, u32[]{:S(2)}) collective-permute-start(f32[6,3,1,128]{3,2,1,0:T(1,128)} %get-tuple-element.23), channel_id=1, source_target_pairs={{16,0},{32,16},{48,32},{64,48},{80,64},{96,80},{112,96},{17,1},{33... | collective-permute-start | bytes 27656 | tf_op jit(solution)/shard_map/ppermute | solution.py:466
  75.4 1.3 %copy-start = (f32[6,3,128,128]{3,2,1,0:T(8,128)S(1)}, f32[6,3,128,128]{3,2,1,0:T(8,128)}, u32[]{:S(2)}) copy-start(f32[6,3,128,128]{3,2,1,0:T(8,128)} %get-tuple-element.21.table) | copy-start | bytes 3538948
  102.5 23.5 %collective-permute-start.4 = (f32[8,8192]{1,0:T(8,128)S(1)}, f32[8,8192]{1,0:T(8,128)S(1)}, u32[]{:S(2)}, u32[]{:S(2)}) collective-permute-start(f32[8,8192]{1,0:T(8,128)S(1)} %get-tuple-element.32), channel_id=1, source_target_pairs={{0,16},{16,32},{32,48},{48,64},{64,80},{80,96},{96,112},{1,17},{17... | collective-permute-start | bytes 786440 | tf_op jit(solution)/shard_map/ppermute | solution.py:466
  106.3 19.6 %collective-permute-start.5 = (f32[8,8192]{1,0:T(8,128)S(1)}, f32[8,8192]{1,0:T(8,128)S(1)}, u32[]{:S(2)}, u32[]{:S(2)}) collective-permute-start(f32[8,8192]{1,0:T(8,128)S(1)} %get-tuple-element.33), channel_id=1, source_target_pairs={{16,0},{32,16},{48,32},{64,48},{80,64},{96,80},{112,96},{17,1},{33... | collective-permute-start | bytes 786440 | tf_op jit(solution)/shard_map/ppermute | solution.py:466
  110.7 15.2 %collective-permute-start.6 = (f32[8,8192]{1,0:T(8,128)S(1)}, f32[8,8192]{1,0:T(8,128)S(1)}, u32[]{:S(2)}, u32[]{:S(2)}) collective-permute-start(f32[8,8192]{1,0:T(8,128)S(1)} %get-tuple-element.34), channel_id=1, source_target_pairs={{0,1},{1,2},{2,3},{3,4},{4,5},{5,6},{6,7},{7,8},{8,9},{9,10},{10,1... | collective-permute-start | bytes 786440 | tf_op jit(solution)/shard_map/ppermute | solution.py:471
  110.8 15.1 %collective-permute-start.7 = (f32[8,8192]{1,0:T(8,128)S(1)}, f32[8,8192]{1,0:T(8,128)S(1)}, u32[]{:S(2)}, u32[]{:S(2)}) collective-permute-start(f32[8,8192]{1,0:T(8,128)S(1)} %get-tuple-element.35), channel_id=1, source_target_pairs={{0,15},{1,0},{2,1},{3,2},{4,3},{5,4},{6,5},{7,6},{8,7},{9,8},{10,9... | collective-permute-start | bytes 786440 | tf_op jit(solution)/shard_map/ppermute | solution.py:471

commit v2 on v1

--- a/solution.py
+++ b/solution.py
@@ -40,111 +40,105 @@
     return lax.shift_left(words, 31 - place) < 0
 
 
-def lane_pass(xs, distance_bit, flips):
-    lane = lane_ids()
-    perm = lane ^ lax.shift_left(1, distance_bit)
-    place = lax.shift_right_logical(lane, distance_bit) & 1
-    uppers = [(place ^ flip) != 0 for flip in flips]
+def lane_pass(xs, distance_bit, uppers, perm):
     out = []
     for v, x in enumerate(xs):
         other = from_lanes(x, perm)
         out.append(
             jnp.where(uppers[v % len(uppers)], jnp.maximum(x, other), jnp.minimum(x, other))
         )
-    return tuple(out)
-
-
-def sort_network(key, payloads, index_out, word_out, sub_word_out):
+    return out
+
+
+def lane_bit(k):
+    return lax.shift_right_logical(lane_ids(), k) & 1
+
+
+def lane_passes(xs, top, flips):
     lane = lane_ids()
+    for j in range(top, -1, -1):
+        uppers = [(lane_bit(j) ^ flip) != 0 for flip in flips]
+        xs = lane_pass(xs, j, uppers, lane ^ (1 << j))
+    return xs
+
+
+def sort_network(keys, payloads, record):
+    lane = lane_ids()
+    lane_f = lane.astype(f32)
     sub = sublane_ids()
-
-    xs = tuple((key[v] & -128) | lane for v in range(VREGS))
-
-    def early_stage(k, xs):
-        flip = lax.shift_right_logical(lane, k) & 1
-
-        def one(step, xs):
-            return lane_pass(xs, k - 1 - step, (flip,))
-
-        return lax.fori_loop(0, k, one, xs)
-
-    xs = lax.fori_loop(1, 7, early_stage, xs)
-    xs = lax.fori_loop(0, 7, lambda step, xs: lane_pass(xs, 6 - step, (0, 1)), xs)
-    for v in range(VREGS):
-        key[v] = xs[v]
-        index = xs[v] & 127
-        if index_out is not None:
-            index_out[0, v] = index
-            word_out[v] = jnp.zeros((8, 128), i32)
-            sub_word_out[v] = jnp.zeros((8, 128), i32)
-        for payload in payloads:
-            payload[v] = from_lanes(payload[v], index)
-
-    def stage(t, carry):
-        def flip_of(v):
-            return -(lax.shift_right_logical(sub * 32 + v, t) & 1)
-
+    words = [jnp.zeros((8, 128), i32) for _ in range(VREGS)] if record else None
+    sub_words = [jnp.zeros((8, 128), i32) for _ in range(VREGS)] if record else None
+
+    xs = [key * 128.0 + lane_f for key in keys]
+    for k in range(1, 7):
+        xs = lane_passes(xs, k - 1, (lane_bit(k),))
+    xs = lane_passes(xs, 6, (0, 1))
+
+    def settle(t, xs):
+        out = []
         for v in range(VREGS):
-            key[v] = key[v] ^ flip_of(v)
-
-        for i in (7, 6, 5):
-
-            @pl.when(i < t)
-            def _():
+            index = xs[v].astype(i32) & 127
+            if record:
+                record(t, v, index)
+            for payload in payloads:
+                payload[v] = from_lanes(payload[v], index)
+            out.append(xs[v] - index.astype(f32) + lane_f)
+        return out
+
+    xs = settle(0, xs)
+    for t in range(1, 9):
+        sign = None
+        if 5 <= t <= 7:
+            sign = jnp.where((lax.shift_right_logical(sub, t - 5) & 1) != 0, -1.0, 1.0)
+            xs = [x * sign for x in xs]
+        for i in range(t - 1, -1, -1):
+            if i >= 5:
                 near = i - 5
                 perm = sub ^ (1 << near)
                 upper = (lax.shift_right_logical(sub, near) & 1) != 0
-                place = jnp.where(t == 6, 0, jnp.where(t == 7, 1, 3)) + t - 1 - i
                 for v in range(VREGS):
-                    x = key[v]
+                    x = xs[v]
                     other = from_sublanes(x, perm)
                     take = jnp.where(upper, other, x) > jnp.where(upper, x, other)
-                    key[v] = jnp.where(take, other, x)
-                    if index_out is not None:
-                        sub_word_out[v] = sub_word_out[v] | jnp.where(
-                            take, lax.shift_left(1, place), 0
-                        )
+                    xs[v] = jnp.where(take, other, x)
+                    if record:
+                        sub_words[v] = sub_words[v] | jnp.where(take, 1 << sub_place(t, i), 0)
                     for payload in payloads:
                         y = payload[v]
                         payload[v] = jnp.where(take, from_sublanes(y, perm), y)
-
-        for i in (4, 3, 2, 1, 0):
-
-            @pl.when(i < t)
-            def _():
-                place = jnp.where(t <= 5, t * (t - 1) // 2, 5 * t - 15) + t - 1 - i
-                place = jnp.where(t <= 5, place, 5 * t - 15 + 4 - i)
+            else:
                 for a in range(VREGS):
                     if a & (1 << i):
                         continue
                     b = a | (1 << i)
-                    x, y = key[a], key[b]
-                    swap = x > y
-                    key[a] = jnp.minimum(x, y)
-                    key[b] = jnp.maximum(x, y)
-                    if index_out is not None:
-                        word_out[a] = word_out[a] | jnp.where(swap, lax.shift_left(1, place), 0)
+                    x, y = xs[a], xs[b]
+                    down = t <= 4 and (a >> t) & 1
+                    swap = x < y if down else x > y
+                    low, high = jnp.minimum(x, y), jnp.maximum(x, y)
+                    xs[a], xs[b] = (high, low) if down else (low, high)
+                    if record:
+                        words[a] = words[a] | jnp.where(swap, 1 << row_place(t, i), 0)
                     for payload in payloads:
                         x, y = payload[a], payload[b]
                         payload[a] = jnp.where(swap, y, x)
                         payload[b] = jnp.where(swap, x, y)
-
-        xs = []
-        for v in range(VREGS):
-            flip = flip_of(v)
-            xs.append((((key[v] ^ flip) & -128) | lane) ^ flip)
-        xs = lax.fori_loop(0, 7, lambda step, xs: lane_pass(xs, 6 - step, (0,)), tuple(xs))
-        for v in range(VREGS):
-            x = xs[v] ^ flip_of(v)
-            key[v] = x
-            index = x & 127
-            if index_out is not None:
-                index_out[t, v] = index
-            for payload in payloads:
-                payload[v] = from_lanes(payload[v], index)
-        return carry
-
-    lax.fori_loop(1, 9, stage, 0)
+        if t <= 4:
+            runs = [xs[v] for v in range(VREGS)]
+            lane_done = []
+            ups = [v for v in range(VREGS) if not (v >> t) & 1]
+            downs = [v for v in range(VREGS) if (v >> t) & 1]
+            up_x = lane_passes([runs[v] for v in ups], 6, (0,))
+            down_x = lane_passes([runs[v] for v in downs], 6, (1,)) if downs else []
+            for v, x in zip(ups, up_x):
+                xs[v] = x
+            for v, x in zip(downs, down_x):
+                xs[v] = x
+        else:
+            xs = lane_passes(xs, 6, (0,))
+            if sign is not None:
+                xs = [x * sign for x in xs]
+        xs = settle(t, xs)
+    return xs, words, sub_words
 
 
 def row_place(t, i):
@@ -155,37 +149,62 @@
     return {6: 0, 7: 1, 8: 3}[t] + t - 1 - i
 
 
-def apply_network(xs, index, words, sub_words):
+def apply_network(count, source, buffer, index, words, sub_words, finish):
     sub = sublane_ids()
-    xs = [from_lanes(xs[v], index[0, v]) for v in range(VREGS)]
+    for v in range(VREGS):
+        lanes = index[0, v]
+        for c in range(count):
+            buffer[c, v] = from_lanes(source(c, v), lanes)
     for t in range(1, 9):
-        for i in range(t - 1, -1, -1):
-            if i >= 5:
-                perm = sub ^ (1 << (i - 5))
-                place = sub_place(t, i)
-                xs = [
-                    jnp.where(bit_set(sub_words[v], place), from_sublanes(xs[v], perm), xs[v])
-                    for v in range(VREGS)
-                ]
+        steps = [i for i in range(t - 1, -1, -1) if i >= 5]
+        if steps:
+            for v in range(VREGS):
+                takes = [bit_set(sub_words[v], sub_place(t, i)) for i in steps]
+                for c in range(count):
+                    x = buffer[c, v]
+                    for i, take in zip(steps, takes):
+                        x = jnp.where(take, from_sublanes(x, sub ^ (1 << (i - 5))), x)
+                    buffer[c, v] = x
+        top = min(t, 5)
+        rounds = {1: ((0,),), 2: ((1, 0),), 3: ((2, 1, 0),), 4: ((3, 2), (1, 0)), 5: ((4, 3), (2, 1, 0))}[top]
+        for bits in rounds:
+            mask = sum(1 << i for i in bits)
+            for base in range(VREGS):
+                if base & mask:
+                    continue
+                members = [v for v in range(VREGS) if v & ~mask == base]
+                swaps = {}
+                for i in bits:
+                    for a in members:
+                        if not a & (1 << i):
+                            swaps[i, a] = bit_set(words[a], row_place(t, i))
+                for c in range(count):
+                    xs = {v: buffer[c, v] for v in members}
+                    for i in bits:
+                        for a in members:
+                            if a & (1 << i):
+                                continue
+                            b = a | (1 << i)
+                            x, y = xs[a], xs[b]
+                            xs[a] = jnp.where(swaps[i, a], y, x)
+                            xs[b] = jnp.where(swaps[i, a], x, y)
+                    for v in members:
+                        buffer[c, v] = xs[v]
+        for v in range(VREGS):
+            lanes = index[t, v]
+            moved = [from_lanes(buffer[c, v], lanes) for c in range(count)]
+            if t < 8:
+                for c in range(count):
+                    buffer[c, v] = moved[c]
             else:
-                place = row_place(t, i)
-                for a in range(VREGS):
-                    if a & (1 << i):
-                        continue
-                    b = a | (1 << i)
-                    swap = bit_set(words[a], place)
-                    x, y = xs[a], xs[b]
-                    xs[a] = jnp.where(swap, y, x)
-                    xs[b] = jnp.where(swap, x, y)
-        xs = [from_lanes(xs[v], index[t, v]) for v in range(VREGS)]
-    return xs
+                finish(v, moved)
 
 
 def plan_kernel(
     cells, offsets, moves, slots,
     near_out, frac_out, counts_out,
-    index_a, word_a, sub_a, index_b, word_b, sub_b,
-    key, tags,
+    index_out, words_out,
+    tags,
 ):
     lane = lane_ids()
     sub = sublane_ids()
@@ -218,42 +237,50 @@
     row = row + jnp.where((row + 1) * COLS <= cell, 1, 0)
     col = cell - row * COLS
     spot = lax.shift_right_logical(col, 7) * (ROWS * 128) + row * 128 + (col & 127)
+    keys = []
     for v in range(VREGS):
         part = slice(v * 8, v * 8 + 8)
-        key[v] = lax.shift_left(spot[part], 7)
+        keys.append(spot[part].astype(f32))
         tags[v] = lax.shift_left(target[part], 15) | number[part]
         frac_out[0, v] = offsets[0, part]
         frac_out[1, v] = offsets[1, part]
-    sort_network(key, (frac_out.at[0], frac_out.at[1], tags), None, None, None)
+    keys, _, _ = sort_network(keys, (frac_out.at[0], frac_out.at[1], tags), None)
     for v in range(VREGS):
-        near_out[v] = lax.shift_right_logical(key[v], 7)
-        key[v] = lax.shift_left(lax.shift_right_logical(tags[v], 15), 7)
-    sort_network(key, (), index_a, word_a, sub_a)
-    for v in range(VREGS):
-        key[v] = lax.shift_left(tags[v] & 32767, 7)
-    sort_network(key, (), index_b, word_b, sub_b)
+        near_out[v] = lax.shift_right_logical(keys[v].astype(i32), 7)
+
+    def one(which, carry):
+        keys = [
+            (lax.shift_right_logical(tags[v], jnp.where(which == 0, 15, 0)) & 32767).astype(f32)
+            for v in range(VREGS)
+        ]
+
+        def record(t, v, index):
+            index_out[which, t, v] = index
+
+        _, words, sub_words = sort_network(keys, (), record)
+        for v in range(VREGS):
+            words_out[which, 0, v] = words[v]
+            words_out[which, 1, v] = sub_words[v]
+        return carry
+
+    lax.fori_loop(0, 2, one, 0)
 
 
 def plan(cells, offsets, moves, slots):
     vmem = pl.BlockSpec(memory_space=pltpu.VMEM)
     smem = pl.BlockSpec(memory_space=pltpu.SMEM)
-    network = [
-        jax.ShapeDtypeStruct((9, VREGS, 8, 128), i32),
-        jax.ShapeDtypeStruct((VREGS, 8, 128), i32),
-        jax.ShapeDtypeStruct((VREGS, 8, 128), i32),
-    ]
     return pl.pallas_call(
         plan_kernel,
         out_shape=[
             jax.ShapeDtypeStruct((VREGS, 8, 128), i32),
             jax.ShapeDtypeStruct((2, VREGS, 8, 128), f32),
             jax.ShapeDtypeStruct((4,), i32),
-        ]
-        + network
-        + network,
+            jax.ShapeDtypeStruct((2, 9, VREGS, 8, 128), i32),
+            jax.ShapeDtypeStruct((2, 2, VREGS, 8, 128), i32),
+        ],
         in_specs=[vmem] * 4,
-        out_specs=[vmem, vmem, smem] + [vmem] * 6,
-        scratch_shapes=[pltpu.VMEM((VREGS, 8, 128), i32), pltpu.VMEM((VREGS, 8, 128), i32)],
+        out_specs=[vmem, vmem, smem, vmem, vmem],
+        scratch_shapes=[pltpu.VMEM((VREGS, 8, 128), i32)],
         compiler_params=pltpu.CompilerParams(vmem_limit_bytes=32 << 20),
         cost_estimate=pl.CostEstimate(flops=20_000_000, bytes_accessed=8_000_000, transcendentals=0),
         name="plan",
@@ -324,9 +351,9 @@
 
 def transfer_kernel(
     first, last, spans, counts,
-    table, above, below, near, frac, index, words, sub_words,
+    table, above, below, near, frac, index, words,
     state, north, south, east, west,
-    nodes, samples, columns,
+    nodes, samples, columns, buffer,
 ):
     nodes[6 * PLANE : 8 * PLANE, :] = jnp.zeros((2 * PLANE, 128), f32)
     for plane in range(6):
@@ -390,74 +417,76 @@
 
     lax.fori_loop(0, VREGS, group, 0)
 
-    lane = lane_ids()
-    sub = sublane_ids()
-
-    def component(c, carry):
-        xs = apply_network([state[c, v] for v in range(VREGS)], index, words, sub_words)
-        direction = lax.shift_right_logical(sub, 1)
-        count = jnp.where(
-            direction < 2,
-            jnp.where(direction == 0, counts[0], counts[1]),
-            jnp.where(direction == 2, counts[2], counts[3]),
-        )
-        slot = (sub & 1) * 4096 + lane
-        for v in range(VREGS):
-            kept = jnp.where(slot + v * 128 < count, xs[v], 0.0)
-            columns[pl.ds(v * 8 + c, 8, stride=256), :] = kept
-        return carry
-
-    lax.fori_loop(0, 8, component, 0)
+    direction = lax.shift_right_logical(sublane_ids(), 1)
+    count = jnp.where(
+        direction < 2,
+        jnp.where(direction == 0, counts[0], counts[1]),
+        jnp.where(direction == 2, counts[2], counts[3]),
+    )
+    slot = (sublane_ids() & 1) * 4096 + lane_ids()
+
+    def finish(v, moved):
+        kept = slot + v * 128 < count
+        for c in range(8):
+            columns[pl.ds(v * 8 + c, 8, stride=256), :] = jnp.where(kept, moved[c], 0.0)
+
+    apply_network(
+        8, lambda c, v: state[c, v], buffer, index.at[0], words.at[0, 0], words.at[0, 1], finish
+    )
     for k, out in enumerate((north, south, east, west)):
         for j in range(64):
             base = (k * 64 + j) * 8
             out[:, 128 * j : 128 * j + 128] = columns[base : base + 8, :]
 
 
-def transfer(bounds, spans, counts, table, above, below, near, frac, network):
+def transfer(bounds, spans, counts, table, above, below, near, frac, index, words):
     vmem = pl.BlockSpec(memory_space=pltpu.VMEM)
     smem = pl.BlockSpec(memory_space=pltpu.SMEM)
     return pl.pallas_call(
         transfer_kernel,
         out_shape=[jax.ShapeDtypeStruct((8, VREGS, 8, 128), f32)]
         + [jax.ShapeDtypeStruct((8, CAP), f32)] * 4,
-        in_specs=[smem] * 4 + [vmem] * 8,
+        in_specs=[smem] * 4 + [vmem] * 7,
         out_specs=[vmem] * 5,
         scratch_shapes=[
             pltpu.VMEM((8 * PLANE, 128), f32),
             pltpu.VMEM((3 * 2048, 128), f32),
             pltpu.VMEM((2048, 128), f32),
+            pltpu.VMEM((8, VREGS, 8, 128), f32),
         ],
         compiler_params=pltpu.CompilerParams(vmem_limit_bytes=40 << 20),
         cost_estimate=pl.CostEstimate(flops=20_000_000, bytes_accessed=8_000_000, transcendentals=0),
         name="transfer",
-    )(bounds[0], bounds[1], spans, counts, table, above, below, near.reshape(256, 128), frac, *network)
-
-
-def restore_kernel(state, index, words, sub_words, out, columns):
-    def component(c, carry):
-        xs = apply_network([state[c, v] for v in range(VREGS)], index, words, sub_words)
-        for v in range(VREGS):
-            columns[pl.ds(v * 8 + c, 8, stride=256), :] = xs[v]
-        return carry
-
-    lax.fori_loop(0, 8, component, 0)
+    )(bounds[0], bounds[1], spans, counts, table, above, below, near.reshape(256, 128), frac, index, words)
+
+
+def restore_kernel(state, offsets, index, words, out, columns, buffer):
+    def finish(v, moved):
+        for c in range(2):
+            frac = offsets[pl.ds(c * 256 + v, 8, stride=32), :]
+            columns[pl.ds(v * 8 + c, 8, stride=256), :] = frac + step_dt * moved[c]
+        for c in range(6):
+            columns[pl.ds(v * 8 + c + 2, 8, stride=256), :] = moved[c]
+
+    apply_network(
+        6, lambda c, v: state[c + 2, v], buffer, index.at[1], words.at[1, 0], words.at[1, 1], finish
+    )
     for j in range(256):
         out[:, 128 * j : 128 * j + 128] = columns[8 * j : 8 * j + 8, :]
 
 
-def restore(state, network):
+def restore(state, offsets, index, words):
     vmem = pl.BlockSpec(memory_space=pltpu.VMEM)
     return pl.pallas_call(
         restore_kernel,
         out_shape=jax.ShapeDtypeStruct((8, 4 * CAP), f32),
         in_specs=[vmem] * 4,
         out_specs=vmem,
-        scratch_shapes=[pltpu.VMEM((2048, 128), f32)],
+        scratch_shapes=[pltpu.VMEM((2048, 128), f32), pltpu.VMEM((6, VREGS, 8, 128), f32)],
         compiler_params=pltpu.CompilerParams(vmem_limit_bytes=32 << 20),
         cost_estimate=pl.CostEstimate(flops=10_000_000, bytes_accessed=4_000_000, transcendentals=0),
         name="restore",
-    )(state, *network)
+    )(state, offsets.reshape(512, 128), index, words)
 
 
 def from_behind(block, axis, distance):
@@ -475,8 +504,7 @@
     outgoing = ocean.reshape(4, 8, 16, COLS).transpose(2, 0, 1, 3)
     forcing = lax.all_to_all(outgoing, "lon", 0, 0)
     planned = plan(cells, offsets, moves, slots)
-    near, frac, counts = planned[:3]
-    slot_network, home_network = planned[3:6], planned[6:9]
+    near, frac, counts, index, words = planned
     ends = lax.shift_right_logical(near.reshape(256, 128), 7)
     bounds = (ends[:, 0], ends[:, 127])
     spans = jnp.max((bounds[1] - bounds[0]).reshape(VREGS, 8), axis=1) + 1
@@ -487,13 +515,13 @@
     above = from_behind(last_edge, "lat", 1)
     below = from_behind(first_edge, "lat", -1)
     state, north, south, east, west = transfer(
-        bounds, spans, counts, table, above, below, near, frac, slot_network
+        bounds, spans, counts, table, above, below, near, frac, index, words
     )
     north = from_behind(north, "lat", 1)
     south = from_behind(south, "lat", -1)
     east = passed_along(east, "lon", 1)
     west = passed_along(west, "lon", -1)
-    parcels = restore(state, home_network)
+    parcels = restore(state, offsets, index, words)
     return (parcels, jnp.concatenate([north, south, east, west], axis=1))
 
 

time: 127 us -> 104 us (0.82); the launches traced: 127 us -> 102 us
  Pallas kernels: 77.4 us -> 51.6 us
  waiting for transfers between devices: 9.4 us -> 6.09 us
  local copies, waits for them, and re-layouts: 7.12 us -> 9.76 us
    pallas_call x1, Pallas kernels: 35.8 us -> 21.2 us  [plan(): pl.pallas_call(plan_kernel, out_shape=[jax.ShapeDtypeStruct((VREGS, 8, 12...]
    pallas_call x1, Pallas kernels: 11.3 us -> 4.93 us  [restore(): pl.pallas_call(restore_kernel, out_shape=jax.ShapeDtypeStruct((8, 4 * CAP...]
    pallas_call x1, Pallas kernels: 25.7 us -> 20.8 us  [transfer(): pl.pallas_call(transfer_kernel, out_shape=[jax.ShapeDtypeStruct((8, VREGS...]
    ppermute x4, waiting for transfers between devices: 4.91 us -> 1.06 us  [passed_along(): lax.ppermute(value, axis, [(i, (i + by) % count) for i in range(count)])]
    unnamed x19, local copies, waits for them, and re-layouts: 2.61 us -> 5.05 us
  transfers between devices with their start and end apart: 9 -> 9, of which waited for: 3 -> 3; matrix products, arithmetic and copies ran while one was open for 1% -> 2% of each run, Pallas kernels for 37% -> 26%
where the time goes in v2:
time: 104 us; the launch traced here: 102 us
  Pallas kernels  51.6 us (50%)
  starting transfers between devices  30.2 us (29%)
  local copies, waits for them, and re-layouts  9.76 us (9%)
  waiting for transfers between devices  6.09 us (6%)
  other arithmetic  3.34 us (3%)
    pallas_call x1, Pallas kernels, plan(): pl.pallas_call(plan_kernel, out_shape=[jax.ShapeDtypeStruct((VREGS, 8, 12...  21.2 us
    pallas_call x1, Pallas kernels, transfer(): pl.pallas_call(transfer_kernel, out_shape=[jax.ShapeDtypeStruct((8, VREGS...  20.8 us
    ppermute x4, starting transfers between devices, from_behind(): return lax.ppermute(block, axis, route)  16.6 us
    ppermute x4, starting transfers between devices, passed_along(): lax.ppermute(value, axis, [(i, (i + by) % count) for i in range(count)])  7.77 us
    all_to_all x1, starting transfers between devices, shards(): forcing = lax.all_to_all(outgoing, 'lon', 0, 0)  5.8 us
    unnamed x19, local copies, waits for them, and re-layouts  5.05 us
    ppermute x4, waiting for transfers between devices, from_behind(): return lax.ppermute(block, axis, route)  5.03 us
    pallas_call x1, Pallas kernels, restore(): pl.pallas_call(restore_kernel, out_shape=jax.ShapeDtypeStruct((8, 4 * CAP...  4.93 us
  transfers between devices with their start and end apart: 9, of which 3 were waited for; matrix products, arithmetic and copies ran while one was open for 2% of the time, Pallas kernels for 26%

profile of v2, /device:TPU:8, one launch (start us, length us, event | category | flops | bytes accessed | tf_op | source)
XLA Modules:
  0.0 101.8 jit_solution(12763907406653437059)
XLA Ops:
  0.6 0.0 copy-start.6
  0.6 0.0 copy-start.3
  0.7 0.0 copy-start.4
  0.7 2.2 %copy.14 = f32[4,1,16,8,384]{4,3,1,0,2:T(8,128)} copy(f32[4,1,16,8,384]{4,3,2,1,0:T(8,128)} %bitcast.22) | data formatting | bytes 1572864 | tf_op jit(solution)/shard_map/reshape | solution.py:504
  2.8 5.8 %all-to-all-start = ((f32[16,4,8,384]{3,2,1,0:T(8,128)}), f32[16,4,8,384]{3,2,1,0:T(8,128)}, u32[]{:S(2)}, u32[]{:S(2)}) async-start(f32[16,4,8,384]{3,2,1,0:T(8,128)} %bitcast.14), calls=%async_computation | async-start | bytes 1572864 | tf_op jit(solution)/shard_map/all_to_all | solution.py:505
  8.6 0.0 copy-done.6
  8.7 0.0 copy-done.3
  8.7 0.0 copy-done.4
  8.7 0.0 copy-start.5
  8.7 0.9 copy-done.5
  9.6 21.2 %plan.1 = (s32[32,8,128]{2,1,0:T(8,128)S(1)}, f32[2,32,8,128]{3,2,1,0:T(8,128)S(1)}, s32[4]{0:T(128)S(1)}, s32[2,9,32,8,128]{4,3,2,1,0:T(8,128)S(1)}, s32[2,2,32,8,128]{4,3,2,1,0:T(8,128)S(1)}) custom-call(s32[256,128]{1,0:T(8,128)S(1)} %bitcast.18, f32[2,256,128]{2,1,0:T(8,128)S(1)} %bitcast.16, s32[256,128]{1,0:T(8,128)S(1)} %bitcast.19, ...), custom_call_target="tpu_custom_call" | custom-call | flops 20000000 | bytes 8000000 | tf_op jit(solution)/shard_map/plan/pallas_call | solution.py:272
  30.8 0.0 all-to-all-done.forcing
  30.8 2.2 %velocity.1 = f32[2,128,384]{2,1,0:T(8,128)} custom-call(f32[16,4,8,384]{3,2,1,0:T(8,128)} %all-to-all-done.forcing, f32[128,384]{1,0:T(8,128)} %mass.1, f32[2,128,384]{2,1,0:T(8,128)} %momentum.1), custom_call_target="tpu_custom_call" | custom-call | tf_op jit(solution)/shard_map/velocity/pallas_call | solution.py:302
  33.0 1.6 %fusion = (f32[2,128,128]{2,1,0:T(8,128)S(1)}, f32[2,128,128]{2,1,0:T(8,128)}) fusion(f32[2,128,384]{2,1,0:T(8,128)} %velocity.1), kind=kLoop, calls=%fused_computation.8 | loop fusion | bytes 524288 | tf_op jit(solution)/shard_map/slice | solution.py:513
  34.6 0.4 collective-permute-start
  35.0 3.5 %collective-permute-start.1 = (f32[2,128,128]{2,1,0:T(8,128)S(1)}, f32[2,128,128]{2,1,0:T(8,128)}, u32[]{:S(2)}, u32[]{:S(2)}) collective-permute-start(f32[2,128,128]{2,1,0:T(8,128)S(1)} %get-tuple-element.31), channel_id=1, source_target_pairs={{0,15},{1,0},{2,1},{3,2},{4,3},{5,4},{6,5},{7,6},{8,7},{9,8},{10,9... | collective-permute-start | bytes 393224 | tf_op jit(solution)/shard_map/ppermute | solution.py:500
  38.5 0.3 subtract_reduce_fusion
  38.7 0.7 sub.12
  39.4 0.8 reduce_max.9
  40.3 1.1 %collective-permute-done.west = f32[2,128,128]{2,1,0:T(8,128)S(1)} collective-permute-done((f32[2,128,128]{2,1,0:T(8,128)}, f32[2,128,128]{2,1,0:T(8,128)S(1)}, u32[]{:S(2)}, u32[]{:S(2)}) %collective-permute-start) | collective-permute-done | bytes 131104 | tf_op jit(solution)/shard_map/ppermute | solution.py:500
  41.3 0.0 copy-start.8
  41.3 0.7 copy-done.8
  42.0 0.0 collective-permute-done.1.east
  42.0 0.0 copy-start.7
  42.0 2.5 %table.1 = (f32[6,3,128,128]{3,2,1,0:T(8,128)}, f32[6,3,1,128]{3,2,1,0:T(1,128)}, f32[6,3,1,128]{3,2,1,0:T(1,128)}) custom-call(f32[2,128,384]{2,1,0:T(8,128)} %velocity.1, f32[2,128,128]{2,1,0:T(8,128)} %copy-done.8, f32[2,128,128]{2,1,0:T(8,128)} %collective-permute-done.1.east), custom_call_target="tpu_custom_call" | custom-call | tf_op jit(solution)/shard_map/table/pallas_call | solution.py:332
  44.5 5.5 %collective-permute-start.2 = (f32[6,3,1,128]{3,2,1,0:T(1,128)}, f32[6,3,1,128]{3,2,1,0:T(1,128)S(1)}, u32[]{:S(2)}, u32[]{:S(2)}) collective-permute-start(f32[6,3,1,128]{3,2,1,0:T(1,128)} %get-tuple-element.18), channel_id=1, source_target_pairs={{0,16},{16,32},{32,48},{48,64},{64,80},{80,96},{96,112},{1,17},{17... | collective-permute-start | bytes 27656 | tf_op jit(solution)/shard_map/ppermute | solution.py:495
  50.0 2.9 %collective-permute-start.3 = (f32[6,3,1,128]{3,2,1,0:T(1,128)}, f32[6,3,1,128]{3,2,1,0:T(1,128)S(1)}, u32[]{:S(2)}, u32[]{:S(2)}) collective-permute-start(f32[6,3,1,128]{3,2,1,0:T(1,128)} %get-tuple-element.19), channel_id=1, source_target_pairs={{16,0},{32,16},{48,32},{64,48},{80,64},{96,80},{112,96},{17,1},{33... | collective-permute-start | bytes 27656 | tf_op jit(solution)/shard_map/ppermute | solution.py:495
  52.9 0.0 collective-permute-done.2.above
  52.9 4.3 %collective-permute-done.3.below = f32[6,3,1,128]{3,2,1,0:T(1,128)S(1)} collective-permute-done((f32[6,3,1,128]{3,2,1,0:T(1,128)}, f32[6,3,1,128]{3,2,1,0:T(1,128)S(1)}, u32[]{:S(2)}, u32[]{:S(2)}) %collective-permute-start.3) | collective-permute-done | bytes 9248 | tf_op jit(solution)/shard_map/ppermute | solution.py:495
  57.2 0.0 copy-start
  57.2 1.3 %copy-done = f32[6,3,128,128]{3,2,1,0:T(8,128)S(1)} copy-done((f32[6,3,128,128]{3,2,1,0:T(8,128)S(1)}, f32[6,3,128,128]{3,2,1,0:T(8,128)}, u32[]{:S(2)}) %copy-start) | copy-done | bytes 1179672
  58.5 20.8 %transfer.1 = (f32[8,32,8,128]{3,2,1,0:T(8,128)S(1)}, f32[8,8192]{1,0:T(8,128)}, f32[8,8192]{1,0:T(8,128)}, f32[8,8192]{1,0:T(8,128)}, f32[8,8192]{1,0:T(8,128)}) custom-call(s32[256]{0:T(256)S(1)} %get-tuple-element.30.first, s32[256]{0:T(256)S(1)} %get-tuple-element.29.last, s32[32]{0:T(128)S(1)} %broadcast_add_fusion.spans, ...), custom_call_target="tpu_custom_call" | custom-call | flops 20000000 | bytes 8000000 | tf_op jit(solution)/shard_map/transfer/pallas_call | solution.py:445
  79.3 0.0 copy-start.1
  79.3 1.0 copy-done.1
  80.3 3.9 %collective-permute-start.4 = (f32[8,8192]{1,0:T(8,128)}, f32[8,8192]{1,0:T(8,128)}, u32[]{:S(2)}, u32[]{:S(2)}) collective-permute-start(f32[8,8192]{1,0:T(8,128)} %get-tuple-element.24), channel_id=1, source_target_pairs={{0,16},{16,32},{32,48},{48,64},{64,80},{80,96},{96,112},{1,17},{17... | collective-permute-start | bytes 786440 | tf_op jit(solution)/shard_map/ppermute | solution.py:495
  84.3 4.3 %collective-permute-start.5 = (f32[8,8192]{1,0:T(8,128)}, f32[8,8192]{1,0:T(8,128)}, u32[]{:S(2)}, u32[]{:S(2)}) collective-permute-start(f32[8,8192]{1,0:T(8,128)} %get-tuple-element.25), channel_id=1, source_target_pairs={{16,0},{32,16},{48,32},{64,48},{80,64},{96,80},{112,96},{17,1},{33... | collective-permute-start | bytes 786440 | tf_op jit(solution)/shard_map/ppermute | solution.py:495
  88.6 0.1 collective-permute-start.6
  88.6 3.8 %collective-permute-start.7 = (f32[8,8192]{1,0:T(8,128)}, f32[8,8192]{1,0:T(8,128)}, u32[]{:S(2)}, u32[]{:S(2)}) collective-permute-start(f32[8,8192]{1,0:T(8,128)} %get-tuple-element.27), channel_id=1, source_target_pairs={{0,15},{1,0},{2,1},{3,2},{4,3},{5,4},{6,5},{7,6},{8,7},{9,8},{10,9... | collective-permute-start | bytes 786440 | tf_op jit(solution)/shard_map/ppermute | solution.py:500
  92.5 0.0 copy-done.7
  92.5 0.2 reshape.36.offsets
  92.7 0.0 copy-start.2
  92.7 1.2 %copy-done.2 = f32[8,32,8,128]{3,2,1,0:T(8,128)S(1)} copy-done((f32[8,32,8,128]{3,2,1,0:T(8,128)S(1)}, f32[8,32,8,128]{3,2,1,0:T(8,128)}, u32[]{:S(2)}) %copy-start.2) | copy-done | bytes 1048600
  94.0 4.9 %restore.1 = f32[8,32768]{1,0:T(8,128)} custom-call(f32[8,32,8,128]{3,2,1,0:T(8,128)S(1)} %copy-done.2, f32[512,128]{1,0:T(8,128)S(1)} %reshape.36.offsets, s32[2,9,32,8,128]{4,3,2,1,0:T(8,128)S(1)} %get-tuple-element.21.index, s32[2,2,32,8,128]{4,3,2,1,0:T(8,128)S(1)} %get-tuple-element.22.words), custom_call_target="tpu_custom_call" | custom-call | flops 10000000 | bytes 4000000 | tf_op jit(solution)/shard_map/restore/pallas_call | solution.py:480
  98.9 0.0 collective-permute-done.4
  98.9 0.7 collective-permute-done.5
  99.6 0.0 collective-permute-done.6
  99.6 0.0 collective-permute-done.7
  99.6 2.2 %pad_maximum_fusion = f32[8,32768]{1,0:T(8,128)} fusion(f32[8,8192]{1,0:T(8,128)} %collective-permute-done.7, f32[8,8192]{1,0:T(8,128)} %collective-permute-done.6, f32[8,8192]{1,0:T(8,128)} %collective-permute-done.5, f32[8,8192]{1,0:T(8,128)} %collective-permute-done.4), kind=kLoop, calls=%fused_computation | loop fusion | flops 786432 | bytes 2097152 | tf_op jit(solution)/shard_map/concatenate | solution.py:525
  (3 shorter events, 0.0 us)
Async XLA Ops:
  0.6 8.0 %copy-start.6 = (f32[2,32768]{1,0:T(2,128)S(1)}, f32[2,32768]{1,0:T(2,128)}, u32[]{:S(2)}) copy-start(f32[2,32768]{1,0:T(2,128)} %param.11) | copy-start | bytes 786436
  0.6 8.0 %copy-start.3 = (s32[32768]{0:T(1024)S(1)}, s32[32768]{0:T(1024)}, u32[]{:S(2)}) copy-start(s32[32768]{0:T(1024)} %param.10) | copy-start | bytes 393220
  0.7 8.0 %copy-start.4 = (s32[32768]{0:T(1024)S(1)}, s32[32768]{0:T(1024)}, u32[]{:S(2)}) copy-start(s32[32768]{0:T(1024)} %param.12) | copy-start | bytes 393220
  2.8 28.0 %all-to-all-start = ((f32[16,4,8,384]{3,2,1,0:T(8,128)}), f32[16,4,8,384]{3,2,1,0:T(8,128)}, u32[]{:S(2)}, u32[]{:S(2)}) async-start(f32[16,4,8,384]{3,2,1,0:T(8,128)} %bitcast.14), calls=%async_computation | async-start | bytes 1572864 | tf_op jit(solution)/shard_map/all_to_all | solution.py:505
  8.7 0.9 copy-start.5
  34.6 6.7 %collective-permute-start = (f32[2,128,128]{2,1,0:T(8,128)}, f32[2,128,128]{2,1,0:T(8,128)S(1)}, u32[]{:S(2)}, u32[]{:S(2)}) collective-permute-start(f32[2,128,128]{2,1,0:T(8,128)} %get-tuple-element.32), channel_id=1, source_target_pairs={{0,1},{1,2},{2,3},{3,4},{4,5},{5,6},{6,7},{7,8},{8,9},{9,10},{10,1... | collective-permute-start | bytes 393224 | tf_op jit(solution)/shard_map/ppermute | solution.py:500
  35.0 7.0 %collective-permute-start.1 = (f32[2,128,128]{2,1,0:T(8,128)S(1)}, f32[2,128,128]{2,1,0:T(8,128)}, u32[]{:S(2)}, u32[]{:S(2)}) collective-permute-start(f32[2,128,128]{2,1,0:T(8,128)S(1)} %get-tuple-element.31), channel_id=1, source_target_pairs={{0,15},{1,0},{2,1},{3,2},{4,3},{5,4},{6,5},{7,6},{8,7},{9,8},{10,9... | collective-permute-start | bytes 393224 | tf_op jit(solution)/shard_map/ppermute | solution.py:500
  41.3 0.7 copy-start.8
  42.0 50.5 %copy-start.7 = (f32[2,32768]{1,0:T(2,128)S(1)}, f32[2,32768]{1,0:T(2,128)}, u32[]{:S(2)}) copy-start(f32[2,32768]{1,0:T(2,128)} %param.11) | copy-start | bytes 786436
  44.5 8.4 %collective-permute-start.2 = (f32[6,3,1,128]{3,2,1,0:T(1,128)}, f32[6,3,1,128]{3,2,1,0:T(1,128)S(1)}, u32[]{:S(2)}, u32[]{:S(2)}) collective-permute-start(f32[6,3,1,128]{3,2,1,0:T(1,128)} %get-tuple-element.18), channel_id=1, source_target_pairs={{0,16},{16,32},{32,48},{48,64},{64,80},{80,96},{96,112},{1,17},{17... | collective-permute-start | bytes 27656 | tf_op jit(solution)/shard_map/ppermute | solution.py:495
  50.0 7.3 %collective-permute-start.3 = (f32[6,3,1,128]{3,2,1,0:T(1,128)}, f32[6,3,1,128]{3,2,1,0:T(1,128)S(1)}, u32[]{:S(2)}, u32[]{:S(2)}) collective-permute-start(f32[6,3,1,128]{3,2,1,0:T(1,128)} %get-tuple-element.19), channel_id=1, source_target_pairs={{16,0},{32,16},{48,32},{64,48},{80,64},{96,80},{112,96},{17,1},{33... | collective-permute-start | bytes 27656 | tf_op jit(solution)/shard_map/ppermute | solution.py:495
  57.2 1.3 %copy-start = (f32[6,3,128,128]{3,2,1,0:T(8,128)S(1)}, f32[6,3,128,128]{3,2,1,0:T(8,128)}, u32[]{:S(2)}) copy-start(f32[6,3,128,128]{3,2,1,0:T(8,128)} %get-tuple-element.17.table) | copy-start | bytes 3538948
  79.3 1.0 copy-start.1
  80.3 18.6 %collective-permute-start.4 = (f32[8,8192]{1,0:T(8,128)}, f32[8,8192]{1,0:T(8,128)}, u32[]{:S(2)}, u32[]{:S(2)}) collective-permute-start(f32[8,8192]{1,0:T(8,128)} %get-tuple-element.24), channel_id=1, source_target_pairs={{0,16},{16,32},{32,48},{48,64},{64,80},{80,96},{96,112},{1,17},{17... | collective-permute-start | bytes 786440 | tf_op jit(solution)/shard_map/ppermute | solution.py:495
  84.3 15.3 %collective-permute-start.5 = (f32[8,8192]{1,0:T(8,128)}, f32[8,8192]{1,0:T(8,128)}, u32[]{:S(2)}, u32[]{:S(2)}) collective-permute-start(f32[8,8192]{1,0:T(8,128)} %get-tuple-element.25), channel_id=1, source_target_pairs={{16,0},{32,16},{48,32},{64,48},{80,64},{96,80},{112,96},{17,1},{33... | collective-permute-start | bytes 786440 | tf_op jit(solution)/shard_map/ppermute | solution.py:495
  88.6 11.0 %collective-permute-start.6 = (f32[8,8192]{1,0:T(8,128)}, f32[8,8192]{1,0:T(8,128)}, u32[]{:S(2)}, u32[]{:S(2)}) collective-permute-start(f32[8,8192]{1,0:T(8,128)} %get-tuple-element.26), channel_id=1, source_target_pairs={{0,1},{1,2},{2,3},{3,4},{4,5},{5,6},{6,7},{7,8},{8,9},{9,10},{10,1... | collective-permute-start | bytes 786440 | tf_op jit(solution)/shard_map/ppermute | solution.py:500
  88.6 11.0 %collective-permute-start.7 = (f32[8,8192]{1,0:T(8,128)}, f32[8,8192]{1,0:T(8,128)}, u32[]{:S(2)}, u32[]{:S(2)}) collective-permute-start(f32[8,8192]{1,0:T(8,128)} %get-tuple-element.27), channel_id=1, source_target_pairs={{0,15},{1,0},{2,1},{3,2},{4,3},{5,4},{6,5},{7,6},{8,7},{9,8},{10,9... | collective-permute-start | bytes 786440 | tf_op jit(solution)/shard_map/ppermute | solution.py:500
  92.7 1.2 %copy-start.2 = (f32[8,32,8,128]{3,2,1,0:T(8,128)S(1)}, f32[8,32,8,128]{3,2,1,0:T(8,128)}, u32[]{:S(2)}) copy-start(f32[8,32,8,128]{3,2,1,0:T(8,128)} %copy-done.1) | copy-start | bytes 3145732

commit v3 on v2

--- a/solution.py
+++ b/solution.py
@@ -10,8 +10,9 @@
 COLS = 384
 BLOCKS = 3
 VREGS = 32
-PAD_ROWS = 144
-PLANE = BLOCKS * PAD_ROWS
+PLANE = BLOCKS * ROWS
+EDGE_PLANE = PLANE + 32
+LON = 16
 
 step_dt = 0.5
 drag_coef = 2.0
@@ -202,9 +203,9 @@
 
 def plan_kernel(
     cells, offsets, moves, slots,
-    near_out, frac_out, counts_out,
+    near_out, ends_out, frac_out, counts_out,
     index_out, words_out,
-    tags,
+    tags, chunks,
 ):
     lane = lane_ids()
     sub = sublane_ids()
@@ -236,7 +237,10 @@
     row = row - jnp.where(row * COLS > cell, 1, 0)
     row = row + jnp.where((row + 1) * COLS <= cell, 1, 0)
     col = cell - row * COLS
-    spot = lax.shift_right_logical(col, 7) * (ROWS * 128) + row * 128 + (col & 127)
+    part = lax.shift_right_logical(col, 7)
+    edge = jnp.where(row == 0, 0, 1)
+    inner = (row > 0) & (row < ROWS - 1)
+    spot = jnp.where(inner, 8 + part * ROWS + row, 2 * part + edge) * 128 + (col & 127)
     keys = []
     for v in range(VREGS):
         part = slice(v * 8, v * 8 + 8)
@@ -246,7 +250,13 @@
         frac_out[1, v] = offsets[1, part]
     keys, _, _ = sort_network(keys, (frac_out.at[0], frac_out.at[1], tags), None)
     for v in range(VREGS):
-        near_out[v] = lax.shift_right_logical(keys[v].astype(i32), 7)
+        spots = lax.shift_right_logical(keys[v].astype(i32), 7)
+        near_out[v] = spots
+        chunks[v * 8 : v * 8 + 8, :] = lax.shift_right_logical(spots, 7).astype(f32)
+    for half in range(2):
+        turned = jnp.transpose(chunks[half * 128 : half * 128 + 128, :]).astype(i32)
+        ends_out[half : half + 1, :] = turned[0:1]
+        ends_out[half + 2 : half + 3, :] = turned[127:128]
 
     def one(which, carry):
         keys = [
@@ -273,73 +283,128 @@
         plan_kernel,
         out_shape=[
             jax.ShapeDtypeStruct((VREGS, 8, 128), i32),
+            jax.ShapeDtypeStruct((4, 128), i32),
             jax.ShapeDtypeStruct((2, VREGS, 8, 128), f32),
             jax.ShapeDtypeStruct((4,), i32),
             jax.ShapeDtypeStruct((2, 9, VREGS, 8, 128), i32),
             jax.ShapeDtypeStruct((2, 2, VREGS, 8, 128), i32),
         ],
         in_specs=[vmem] * 4,
-        out_specs=[vmem, vmem, smem, vmem, vmem],
-        scratch_shapes=[pltpu.VMEM((VREGS, 8, 128), i32)],
+        out_specs=[vmem, vmem, vmem, smem, vmem, vmem],
+        scratch_shapes=[pltpu.VMEM((VREGS, 8, 128), i32), pltpu.VMEM((256, 128), f32)],
         compiler_params=pltpu.CompilerParams(vmem_limit_bytes=32 << 20),
         cost_estimate=pl.CostEstimate(flops=20_000_000, bytes_accessed=8_000_000, transcendentals=0),
         name="plan",
     )(cells.reshape(256, 128), offsets.reshape(2, 256, 128), moves.reshape(256, 128), slots.reshape(256, 128))
 
 
-def velocity_kernel(forcing, mass, momentum, out):
-    heavy = mass[...]
-    for part in range(2):
-        current = forcing[:, part].reshape(ROWS, COLS)
-        stress = forcing[:, 2 + part].reshape(ROWS, COLS)
-        out[part] = (momentum[part] + step_dt * stress + step_dt * drag_coef * heavy * current) / (
-            heavy * (1.0 + step_dt * drag_coef)
-        )
-
-
-def node_velocity(forcing, mass, momentum):
+def pack_kernel(ocean, mass, momentum, out, last, first):
+    lane = lax.broadcasted_iota(i32, (8, 128), 1)
+    tiles = LON * BLOCKS
+
+    def tile(part, k):
+        k = k % tiles
+        return ocean[part, :, 128 * k : 128 * k + 128]
+
+    spots = (0, 1, 4, 5)
+    for b in range(LON):
+        rim = jnp.zeros((8, 128), f32)
+        for part in range(4):
+            for k in range(BLOCKS):
+                column = (part * BLOCKS + k) * 128
+                out[b, :, column : column + 128] = tile(part, BLOCKS * b + k)
+            spot = spots[part]
+            rim = jnp.where(lane == spot, pltpu.roll(tile(part, BLOCKS * b - 1), spot + 1, 1), rim)
+            rim = jnp.where(lane == spot + 2, pltpu.roll(tile(part, BLOCKS * b + BLOCKS), spot + 2, 1), rim)
+        out[b, :, 4 * COLS : 4 * COLS + 128] = rim
+    lanes = lax.broadcasted_iota(i32, (ROWS, 128), 1)
+    for side, out_side in ((0, last), (1, first)):
+        column = 0 if side else COLS - 128
+        sources = [mass[:, column : column + 128]] * 2 + [
+            momentum[part, :, column : column + 128] for part in range(2)
+        ]
+        rim = jnp.ones((ROWS, 128), f32)
+        for source, spot in zip(sources, spots):
+            spot = spot + 2 * side
+            shift = spot if side else spot + 1
+            rim = jnp.where(lanes == spot, pltpu.roll(source, shift, 1), rim)
+        out_side[...] = rim
+
+
+def pack(ocean, mass, momentum):
     vmem = pl.BlockSpec(memory_space=pltpu.VMEM)
     return pl.pallas_call(
-        velocity_kernel,
-        out_shape=jax.ShapeDtypeStruct((2, ROWS, COLS), f32),
+        pack_kernel,
+        out_shape=[
+            jax.ShapeDtypeStruct((LON, 8, 4 * COLS + 128), f32),
+            jax.ShapeDtypeStruct((ROWS, 128), f32),
+            jax.ShapeDtypeStruct((ROWS, 128), f32),
+        ],
         in_specs=[vmem] * 3,
-        out_specs=vmem,
-        name="velocity",
-    )(forcing, mass, momentum)
-
-
-def table_kernel(velocity, west, east, table, first_edge, last_edge):
+        out_specs=[vmem] * 3,
+        name="pack",
+    )(ocean, mass, momentum)
+
+
+def drive(momentum, stress, mass, current):
+    return (momentum + step_dt * stress + step_dt * drag_coef * mass * current) / (
+        mass * (1.0 + step_dt * drag_coef)
+    )
+
+
+def table_kernel(forcing, mass, momentum, west, east, table, first_edge, last_edge):
     lane = lax.broadcasted_iota(i32, (ROWS, 128), 1)
+    rim = forcing[:, :, 4 * COLS : 4 * COLS + 128].reshape(ROWS, 128)
+    beside = jnp.where((lane & 2) == 0, west[...], east[...])
+    rim = drive(pltpu.roll(beside, 124, 1), pltpu.roll(rim, 124, 1), beside, rim)
     for part in range(2):
-        blocks = [velocity[part, :, 128 * k : 128 * k + 128] for k in range(BLOCKS)]
-        left = [west[part]] + blocks[:-1]
-        right = blocks[1:] + [east[part]]
+        blocks, after, before = [], [], []
         for k in range(BLOCKS):
-            shifted = [
-                jnp.where(lane == 0, pltpu.roll(left[k], 1, 1), pltpu.roll(blocks[k], 1, 1)),
+            column = 128 * k
+            current = forcing[:, :, COLS * part + column : COLS * part + column + 128]
+            stress = forcing[:, :, COLS * (2 + part) + column : COLS * (2 + part) + column + 128]
+            block = drive(
+                momentum[part, :, column : column + 128],
+                stress.reshape(ROWS, 128),
+                mass[:, column : column + 128],
+                current.reshape(ROWS, 128),
+            )
+            blocks.append(block)
+            after.append(pltpu.roll(block, 1, 1))
+            before.append(pltpu.roll(block, 127, 1))
+        left = [pltpu.roll(rim, 127, 1) if part else rim] + after[:-1]
+        right = before[1:] + [pltpu.roll(rim, 125 - part, 1)]
+        for k in range(BLOCKS):
+            shifted = (
+                jnp.where(lane == 0, left[k], after[k]),
                 blocks[k],
-                jnp.where(lane == 127, pltpu.roll(right[k], 127, 1), pltpu.roll(blocks[k], 127, 1)),
-            ]
+                jnp.where(lane == 127, right[k], before[k]),
+            )
             for q in range(3):
                 plane = part * 3 + q
-                table[plane, k] = shifted[q]
-                first_edge[plane, k] = shifted[q][0:1]
-                last_edge[plane, k] = shifted[q][ROWS - 1 : ROWS]
-
-
-def node_table(velocity, west, east):
+                spot = plane * BLOCKS + k
+                table[plane, ROWS * k : ROWS * k + ROWS, :] = shifted[q]
+                first_edge[spot : spot + 1, :] = shifted[q][0:1]
+                last_edge[spot : spot + 1, :] = shifted[q][ROWS - 1 : ROWS]
+    for plane in (6, 7):
+        table[plane] = jnp.zeros((PLANE, 128), f32)
+    first_edge[18:24, :] = jnp.zeros((6, 128), f32)
+    last_edge[18:24, :] = jnp.zeros((6, 128), f32)
+
+
+def node_table(forcing, mass, momentum, west, east):
     vmem = pl.BlockSpec(memory_space=pltpu.VMEM)
     return pl.pallas_call(
         table_kernel,
         out_shape=[
-            jax.ShapeDtypeStruct((6, BLOCKS, ROWS, 128), f32),
-            jax.ShapeDtypeStruct((6, BLOCKS, 1, 128), f32),
-            jax.ShapeDtypeStruct((6, BLOCKS, 1, 128), f32),
+            jax.ShapeDtypeStruct((8, PLANE, 128), f32),
+            jax.ShapeDtypeStruct((24, 128), f32),
+            jax.ShapeDtypeStruct((24, 128), f32),
         ],
-        in_specs=[vmem] * 3,
+        in_specs=[vmem] * 5,
         out_specs=[vmem] * 3,
         name="table",
-    )(velocity, west, east)
+    )(forcing, mass, momentum, west, east)
 
 
 def spline(frac):
@@ -349,70 +414,127 @@
     return (lower, middle, upper)
 
 
+def interpolate_group(g, ends, near, frac, nodes, stride, address, samples, state):
+    high = lax.shift_right_logical(g & 3, 1)
+    low = (g & 1) * 64 + lax.shift_right_logical(g, 2)
+    start = (g & 3) * 64 + lax.shift_right_logical(g, 2)
+    first = [ends[high, low + 8 * j] for j in range(8)]
+    last = [ends[high + 2, low + 8 * j] for j in range(8)]
+    span = last[0] - first[0]
+    for j in range(1, 8):
+        span = jnp.maximum(span, last[j] - first[j])
+
+    def trip(step, sums):
+        sums = list(sums)
+        for j in range(8):
+            spot = near[pl.ds(start + 8 * j, 8, stride=0), :]
+            lanes = spot & 127
+            chunk = lax.shift_right_logical(spot, 7)
+            for more in range(2):
+                here = jnp.minimum(first[j] + 2 * step + more, last[j])
+                base = address(here)
+                inside = chunk == here
+                for r in range(3):
+                    got = from_lanes(nodes[pl.ds(base + r - 1, 8, stride=stride), :], lanes)
+                    sums[3 * j + r] = jnp.where(inside, got, sums[3 * j + r])
+        return tuple(sums)
+
+    trips = lax.shift_right_logical(span, 1) + 1
+    sums = lax.fori_loop(0, trips, trip, tuple(jnp.zeros((8, 128), f32) for _ in range(24)))
+    for j in range(8):
+        for r in range(3):
+            samples[pl.ds(r * 64 + j, 8, stride=8), :] = sums[3 * j + r]
+    rows = pl.ds(start, 8, stride=8)
+    d_row = frac[0, rows, :]
+    d_col = frac[1, rows, :]
+    w_row = spline(d_row)
+    w_col = spline(d_col)
+    arm_row = [4.0 * w_row[r] * (r - 1 - d_row) for r in range(3)]
+    arm_col = [4.0 * w_col[q] * (q - 1 - d_col) for q in range(3)]
+    speeds = []
+    affines = []
+    for part in range(2):
+        speed = along_row = along_col = None
+        for q in range(3):
+            plane = part * 3 + q
+            got = [samples[r * 64 + plane * 8 : r * 64 + plane * 8 + 8, :] for r in range(3)]
+            plain = w_row[0] * got[0] + w_row[1] * got[1] + w_row[2] * got[2]
+            tilted = arm_row[0] * got[0] + arm_row[1] * got[1] + arm_row[2] * got[2]
+            terms = (w_col[q] * plain, w_col[q] * tilted, arm_col[q] * plain)
+            if q == 0:
+                speed, along_row, along_col = terms
+            else:
+                speed = speed + terms[0]
+                along_row = along_row + terms[1]
+                along_col = along_col + terms[2]
+        speeds.append(speed)
+        affines += [along_row, along_col]
+    values = [d_row + step_dt * speeds[0], d_col + step_dt * speeds[1]] + speeds + affines
+    for c in range(8):
+        state[c, rows, :] = values[c]
+
+
+def group_first(g, ends):
+    return ends[lax.shift_right_logical(g & 3, 1), (g & 1) * 64 + lax.shift_right_logical(g, 2)]
+
+
+def inner_kernel(ends, table, near, frac, state, samples):
+    def group(g, carry):
+        @pl.when(group_first(g, ends) >= 8)
+        def _():
+            interpolate_group(
+                g, ends, near, frac, table, PLANE, lambda chunk: chunk - 8, samples, state
+            )
+
+        return carry
+
+    lax.fori_loop(0, VREGS, group, 0)
+
+
+def inner(ends, table, near, frac):
+    vmem = pl.BlockSpec(memory_space=pltpu.VMEM)
+    smem = pl.BlockSpec(memory_space=pltpu.SMEM)
+    return pl.pallas_call(
+        inner_kernel,
+        out_shape=jax.ShapeDtypeStruct((8, 256, 128), f32),
+        in_specs=[smem] + [vmem] * 3,
+        out_specs=vmem,
+        scratch_shapes=[pltpu.VMEM((192, 128), f32)],
+        compiler_params=pltpu.CompilerParams(vmem_limit_bytes=24 << 20),
+        cost_estimate=pl.CostEstimate(flops=20_000_000, bytes_accessed=8_000_000, transcendentals=0),
+        name="inner",
+    )(ends, table.reshape(8 * PLANE, 128), near.reshape(256, 128), frac.reshape(2, 256, 128))
+
+
 def transfer_kernel(
-    first, last, spans, counts,
-    table, above, below, near, frac, index, words,
+    ends, counts,
+    table, above, below, near, frac, early, index, words,
     state, north, south, east, west,
     nodes, samples, columns, buffer,
 ):
-    nodes[6 * PLANE : 8 * PLANE, :] = jnp.zeros((2 * PLANE, 128), f32)
+    for c in range(8):
+        state[c] = early[c]
     for plane in range(6):
+        base = plane * EDGE_PLANE
+        nodes[base : base + PLANE, :] = table[plane]
         for k in range(BLOCKS):
-            base = plane * PLANE + k * PAD_ROWS
-            nodes[base + 8 : base + 8 + ROWS, :] = table[plane, k]
-            nodes[base + 7 : base + 8, :] = above[plane, k]
-            nodes[base + 8 + ROWS : base + 9 + ROWS, :] = below[plane, k]
-
-    def group(v, carry):
-        def chunk(step, sums):
-            sums = list(sums)
-            for s in range(8):
-                block = v * 8 + s
-                here = jnp.minimum(first[block] + step, last[block])
-                base = here + lax.shift_right_logical(here, 7) * 16 + 8
-                spot = near[pl.ds(block, 8, stride=0), :]
-                lanes = spot & 127
-                inside = lax.shift_right_logical(spot, 7) == here
-                for r in range(3):
-                    got = from_lanes(nodes[pl.ds(base + r - 1, 8, stride=PLANE), :], lanes)
-                    sums[3 * s + r] = jnp.where(inside, got, sums[3 * s + r])
-            return tuple(sums)
-
-        sums = lax.fori_loop(0, spans[v], chunk, tuple(jnp.zeros((8, 128), f32) for _ in range(24)))
-        for s in range(8):
-            for r in range(3):
-                samples[pl.ds(r * 2048 + v * 8 + s, 8, stride=256), :] = sums[3 * s + r]
-        here = pl.ds(pl.multiple_of(v * 8, 8), 8)
-        d_row = frac[0, v]
-        d_col = frac[1, v]
-        w_row = spline(d_row)
-        w_col = spline(d_col)
-        arm_row = [4.0 * w_row[r] * (r - 1 - d_row) for r in range(3)]
-        arm_col = [4.0 * w_col[q] * (q - 1 - d_col) for q in range(3)]
-        speeds = []
-        affines = []
-        for part in range(2):
-            speed = along_row = along_col = None
-            for q in range(3):
-                plane = part * 3 + q
-                got = [
-                    samples[pl.ds(pl.multiple_of(r * 2048 + plane * 256 + v * 8, 8), 8), :]
-                    for r in range(3)
-                ]
-                plain = w_row[0] * got[0] + w_row[1] * got[1] + w_row[2] * got[2]
-                tilted = arm_row[0] * got[0] + arm_row[1] * got[1] + arm_row[2] * got[2]
-                terms = (w_col[q] * plain, w_col[q] * tilted, arm_col[q] * plain)
-                if q == 0:
-                    speed, along_row, along_col = terms
-                else:
-                    speed = speed + terms[0]
-                    along_row = along_row + terms[1]
-                    along_col = along_col + terms[2]
-            speeds.append(speed)
-            affines += [along_row, along_col]
-        values = [d_row + step_dt * speeds[0], d_col + step_dt * speeds[1]] + speeds + affines
-        for c in range(8):
-            state[c, v] = values[c]
+            spot = plane * BLOCKS + k
+            edge = base + PLANE + 8 * k
+            top = k * ROWS
+            nodes[edge : edge + 1, :] = above[spot : spot + 1, :]
+            nodes[edge + 1 : edge + 3, :] = table[plane, top : top + 2, :]
+            nodes[edge + 4 : edge + 6, :] = table[plane, top + ROWS - 2 : top + ROWS, :]
+            nodes[edge + 6 : edge + 7, :] = below[spot : spot + 1, :]
+    nodes[6 * EDGE_PLANE : 8 * EDGE_PLANE, :] = jnp.zeros((2 * EDGE_PLANE, 128), f32)
+
+    def address(chunk):
+        return jnp.where(chunk < 8, PLANE + 1 + 4 * chunk, jnp.maximum(chunk - 8, 1))
+
+    def group(g, carry):
+        @pl.when(group_first(g, ends) < 8)
+        def _():
+            interpolate_group(g, ends, near, frac, nodes, EDGE_PLANE, address, samples, state)
+
         return carry
 
     lax.fori_loop(0, VREGS, group, 0)
@@ -431,7 +553,9 @@
             columns[pl.ds(v * 8 + c, 8, stride=256), :] = jnp.where(kept, moved[c], 0.0)
 
     apply_network(
-        8, lambda c, v: state[c, v], buffer, index.at[0], words.at[0, 0], words.at[0, 1], finish
+        8,
+        lambda c, v: state[c, 8 * v : 8 * v + 8, :],
+        buffer, index.at[0], words.at[0, 0], words.at[0, 1], finish,
     )
     for k, out in enumerate((north, south, east, west)):
         for j in range(64):
@@ -439,25 +563,28 @@
             out[:, 128 * j : 128 * j + 128] = columns[base : base + 8, :]
 
 
-def transfer(bounds, spans, counts, table, above, below, near, frac, index, words):
+def transfer(ends, counts, table, above, below, near, frac, early, index, words):
     vmem = pl.BlockSpec(memory_space=pltpu.VMEM)
     smem = pl.BlockSpec(memory_space=pltpu.SMEM)
     return pl.pallas_call(
         transfer_kernel,
-        out_shape=[jax.ShapeDtypeStruct((8, VREGS, 8, 128), f32)]
+        out_shape=[jax.ShapeDtypeStruct((8, 256, 128), f32)]
         + [jax.ShapeDtypeStruct((8, CAP), f32)] * 4,
-        in_specs=[smem] * 4 + [vmem] * 7,
+        in_specs=[smem] * 2 + [vmem] * 8,
         out_specs=[vmem] * 5,
         scratch_shapes=[
-            pltpu.VMEM((8 * PLANE, 128), f32),
-            pltpu.VMEM((3 * 2048, 128), f32),
+            pltpu.VMEM((8 * EDGE_PLANE, 128), f32),
+            pltpu.VMEM((192, 128), f32),
             pltpu.VMEM((2048, 128), f32),
             pltpu.VMEM((8, VREGS, 8, 128), f32),
         ],
-        compiler_params=pltpu.CompilerParams(vmem_limit_bytes=40 << 20),
-        cost_estimate=pl.CostEstimate(flops=20_000_000, bytes_accessed=8_000_000, transcendentals=0),
+        compiler_params=pltpu.CompilerParams(vmem_limit_bytes=32 << 20),
+        cost_estimate=pl.CostEstimate(flops=10_000_000, bytes_accessed=8_000_000, transcendentals=0),
         name="transfer",
-    )(bounds[0], bounds[1], spans, counts, table, above, below, near.reshape(256, 128), frac, index, words)
+    )(
+        ends, counts, table, above, below,
+        near.reshape(256, 128), frac.reshape(2, 256, 128), early, index, words,
+    )
 
 
 def restore_kernel(state, offsets, index, words, out, columns, buffer):
@@ -469,7 +596,9 @@
             columns[pl.ds(v * 8 + c + 2, 8, stride=256), :] = moved[c]
 
     apply_network(
-        6, lambda c, v: state[c + 2, v], buffer, index.at[1], words.at[1, 0], words.at[1, 1], finish
+        6,
+        lambda c, v: state[c + 2, 8 * v : 8 * v + 8, :],
+        buffer, index.at[1], words.at[1, 0], words.at[1, 1], finish,
     )
     for j in range(256):
         out[:, 128 * j : 128 * j + 128] = columns[8 * j : 8 * j + 8, :]
@@ -501,21 +630,18 @@
 
 
 def shards(ocean, grid_mass, grid_momentum, cells, offsets, moves, slots):
-    outgoing = ocean.reshape(4, 8, 16, COLS).transpose(2, 0, 1, 3)
+    outgoing, last, first = pack(ocean, grid_mass, grid_momentum)
     forcing = lax.all_to_all(outgoing, "lon", 0, 0)
-    planned = plan(cells, offsets, moves, slots)
-    near, frac, counts, index, words = planned
-    ends = lax.shift_right_logical(near.reshape(256, 128), 7)
-    bounds = (ends[:, 0], ends[:, 127])
-    spans = jnp.max((bounds[1] - bounds[0]).reshape(VREGS, 8), axis=1) + 1
-    velocity = node_velocity(forcing, grid_mass, grid_momentum)
-    west = passed_along(velocity[:, :, COLS - 128 :], "lon", 1)
-    east = passed_along(velocity[:, :, :128], "lon", -1)
-    table, first_edge, last_edge = node_table(velocity, west, east)
+    west = passed_along(last, "lon", 1)
+    east = passed_along(first, "lon", -1)
+    near, ends, frac, counts, index, words = plan(cells, offsets, moves, slots)
+    forcing, near = lax.optimization_barrier((forcing, near))
+    table, first_edge, last_edge = node_table(forcing, grid_mass, grid_momentum, west, east)
     above = from_behind(last_edge, "lat", 1)
     below = from_behind(first_edge, "lat", -1)
+    early = inner(ends, table, near, frac)
     state, north, south, east, west = transfer(
-        bounds, spans, counts, table, above, below, near, frac, index, words
+        ends, counts, table, above, below, near, frac, early, index, words
     )
     north = from_behind(north, "lat", 1)
     south = from_behind(south, "lat", -1)

time: 104 us -> 95 us (0.913); the launches traced: 102 us -> 94.4 us
  waiting for transfers between devices: 6.09 us -> 0.02 us
  local copies, waits for them, and re-layouts: 9.76 us -> 5.7 us
  Pallas kernels: 51.6 us -> 55.3 us
  other arithmetic: 3.34 us -> 2.23 us
    ppermute x4, waiting for transfers between devices: 5.03 us -> 0.01 us  [from_behind(): return lax.ppermute(block, axis, route)]
    pallas_call x3 -> x4, Pallas kernels: 25.5 us -> 29.1 us  [the longest x1 16 us: inner(): pl.pallas_call(inner_kernel, out_shape=jax.ShapeDtypeStruct((8, 256, 128)...]
    reshape x1 -> x0, local copies, waits for them, and re-layouts: 2.15 us -> none  [shards(): outgoing = ocean.reshape(4, 8, 16, COLS).transpose(2, 0, 1, 3)]
    slice x1 -> x0, local copies, waits for them, and re-layouts: 1.64 us -> none  [shards(): east = passed_along(velocity[:, :, :128], 'lon', -1)]
    ppermute x4, waiting for transfers between devices: 1.06 us -> 0.01 us  [passed_along(): lax.ppermute(value, axis, [(i, (i + by) % count) for i in range(count)])]
    unnamed x19 -> x17, local copies, waits for them, and re-layouts: 5.05 us -> 4.53 us
  transfers between devices with their start and end apart: 9 -> 9, of which waited for: 3 -> 0; matrix products, arithmetic and copies ran while one was open for 2% -> 1% of each run, Pallas kernels for 26% -> 45%
where the time goes in v3:
time: 95 us; the launch traced here: 94.4 us
  Pallas kernels  55.3 us (58%)
  starting transfers between devices  30.3 us (32%)
  local copies, waits for them, and re-layouts  5.7 us (6%)
  other arithmetic  2.23 us (2%)
    pallas_call x1, Pallas kernels, plan(): pl.pallas_call(plan_kernel, out_shape=[jax.ShapeDtypeStruct((VREGS, 8, 12...  21.3 us
    ppermute x4, starting transfers between devices, from_behind(): return lax.ppermute(block, axis, route)  16.6 us
    pallas_call x1, Pallas kernels, inner(): pl.pallas_call(inner_kernel, out_shape=jax.ShapeDtypeStruct((8, 256, 128)...  16 us
    ppermute x4, starting transfers between devices, passed_along(): lax.ppermute(value, axis, [(i, (i + by) % count) for i in range(count)])  7.84 us
    pallas_call x1, Pallas kernels, transfer(): pl.pallas_call(transfer_kernel, out_shape=[jax.ShapeDtypeStruct((8, 256,...  7.55 us
    all_to_all x1, starting transfers between devices, shards(): forcing = lax.all_to_all(outgoing, 'lon', 0, 0)  5.8 us
    pallas_call x1, Pallas kernels, restore(): pl.pallas_call(restore_kernel, out_shape=jax.ShapeDtypeStruct((8, 4 * CAP...  4.93 us
    unnamed x17, local copies, waits for them, and re-layouts  4.53 us
  transfers between devices with their start and end apart: 9, of which 0 were waited for; matrix products, arithmetic and copies ran while one was open for 1% of the time, Pallas kernels for 45%

profile of v3, /device:TPU:8, one launch (start us, length us, event | category | flops | bytes accessed | tf_op | source)
XLA Modules:
  0.0 94.4 jit_solution(1312208750712195890)
XLA Ops:
  0.6 0.0 copy-start.7
  0.6 0.0 copy-start.4
  0.7 0.0 copy-start.5
  0.7 2.6 %pack.1 = (f32[16,8,1664]{2,1,0:T(8,128)}, f32[128,128]{1,0:T(8,128)}, f32[128,128]{1,0:T(8,128)}) custom-call(f32[4,8,6144]{2,1,0:T(8,128)} %ocean.1, f32[128,384]{1,0:T(8,128)} %mass.3, f32[2,128,384]{2,1,0:T(8,128)} %momentum.3), custom_call_target="tpu_custom_call" | custom-call | tf_op jit(solution)/shard_map/pack/pallas_call | solution.py:336
  3.3 5.8 %all-to-all-start = ((f32[16,8,1664]{2,1,0:T(8,128)}), f32[16,8,1664]{2,1,0:T(8,128)}, u32[]{:S(2)}, u32[]{:S(2)}) async-start(f32[16,8,1664]{2,1,0:T(8,128)} %get-tuple-element.23), calls=%async_computation | async-start | bytes 1703936 | tf_op jit(solution)/shard_map/all_to_all | solution.py:634
  9.1 0.4 collective-permute-start
  9.4 3.6 %collective-permute-start.1 = (f32[128,128]{1,0:T(8,128)}, f32[128,128]{1,0:T(8,128)}, u32[]{:S(2)}, u32[]{:S(2)}) collective-permute-start(f32[128,128]{1,0:T(8,128)} %get-tuple-element.27), channel_id=1, source_target_pairs={{0,15},{1,0},{2,1},{3,2},{4,3},{5,4},{6,5},{7,6},{8,7},{9,8},{10,9... | collective-permute-start | bytes 196616 | tf_op jit(solution)/shard_map/ppermute | solution.py:629
  13.0 0.0 copy-done.7
  13.0 0.0 copy-done.4
  13.0 0.0 copy-done.5
  13.0 0.0 copy-start.6
  13.0 0.9 copy-done.6
  13.9 21.3 %plan.1 = (s32[32,8,128]{2,1,0:T(8,128)S(1)}, s32[4,128]{1,0:T(4,128)S(1)}, f32[2,32,8,128]{3,2,1,0:T(8,128)S(1)}, s32[4]{0:T(128)S(1)}, s32[2,9,32,8,128]{4,3,2...) custom-call(s32[256,128]{1,0:T(8,128)S(1)} %bitcast.16, f32[2,256,128]{2,1,0:T(8,128)S(1)} %bitcast.13, ...), custom_call_target="tpu_custom_call" | custom-call | flops 20000000 | bytes 8000000 | tf_op jit(solution)/shard_map/plan/pallas_call | solution.py:282
  35.2 0.0 all-to-all-done.forcing
  35.2 0.0 collective-permute-done.west
  35.2 0.0 collective-permute-done.1.east
  35.3 2.9 %table.1 = (f32[8,384,128]{2,1,0:T(8,128)}, f32[24,128]{1,0:T(8,128)}, f32[24,128]{1,0:T(8,128)}) custom-call(f32[16,8,1664]{2,1,0:T(8,128)} %all-to-all-done.forcing, f32[128,384]{1,0:T(8,128)} %mass.3, f32[2,128,384]{2,1,0:T(8,128)} %momentum.3, f32[128,128]{1,0:T(8,128)} %collective-permute-done.west, f32[128,128]{1,0:T(8,128)} %collective-permute-done.1.east), custom_call_target="tpu_custom_call" | custom-call | tf_op jit(solution)/shard_map/table/pallas_call | solution.py:397
  38.2 5.5 %collective-permute-start.2 = (f32[24,128]{1,0:T(8,128)}, f32[24,128]{1,0:T(8,128)S(1)}, u32[]{:S(2)}, u32[]{:S(2)}) collective-permute-start(f32[24,128]{1,0:T(8,128)} %get-tuple-element.29), channel_id=1, source_target_pairs={{0,16},{16,32},{32,48},{48,64},{64,80},{80,96},{96,112},{1,17},{17... | collective-permute-start | bytes 36872 | tf_op jit(solution)/shard_map/ppermute | solution.py:624
  43.7 2.9 %collective-permute-start.3 = (f32[24,128]{1,0:T(8,128)}, f32[24,128]{1,0:T(8,128)S(1)}, u32[]{:S(2)}, u32[]{:S(2)}) collective-permute-start(f32[24,128]{1,0:T(8,128)} %get-tuple-element.30), channel_id=1, source_target_pairs={{16,0},{32,16},{48,32},{64,48},{80,64},{96,80},{112,96},{17,1},{33... | collective-permute-start | bytes 36872 | tf_op jit(solution)/shard_map/ppermute | solution.py:624
  46.6 0.0 copy-start
  46.6 1.4 %copy-done = f32[8,384,128]{2,1,0:T(8,128)S(1)} copy-done((f32[8,384,128]{2,1,0:T(8,128)S(1)}, f32[8,384,128]{2,1,0:T(8,128)}, u32[]{:S(2)}) %copy-start) | copy-done | bytes 1572888
  48.0 0.0 copy-start.1
  48.0 16.0 %inner.1.early = f32[8,256,128]{2,1,0:T(8,128)S(1)} custom-call(s32[4,128]{1,0:T(4,128)S(1)} %get-tuple-element.21.ends, f32[3072,128]{1,0:T(8,128)S(1)} %bitcast.10, s32[256,128]{1,0:T(8,128)S(1)} %bitcast.14, f32[2,256,128]{2,1,0:T(8,128)S(1)} %bitcast.11), custom_call_target="tpu_custom_call" | custom-call | flops 20000000 | bytes 8000000 | tf_op jit(solution)/shard_map/inner/pallas_call | solution.py:497
  64.1 0.0 collective-permute-done.2.above
  64.1 0.0 collective-permute-done.3.below
  64.1 0.0 copy-done.1
  64.1 7.5 %transfer.1 = (f32[8,256,128]{2,1,0:T(8,128)S(1)}, f32[8,8192]{1,0:T(8,128)}, f32[8,8192]{1,0:T(8,128)}, f32[8,8192]{1,0:T(8,128)}, f32[8,8192]{1,0:T(8,128)S(1)}) custom-call(s32[4,128]{1,0:T(4,128)S(1)} %get-tuple-element.21.ends, s32[4]{0:T(128)S(1)} %get-tuple-element.22.counts, f32[8,384,128]{2,1,0:T(8,128)S(1)} %copy-done.1, ...), custom_call_target="tpu_custom_call" | custom-call | flops 10000000 | bytes 8000000 | tf_op jit(solution)/shard_map/transfer/pallas_call | solution.py:569
  71.6 0.0 copy-start.2
  71.6 1.0 %copy-done.2 = f32[8,256,128]{2,1,0:T(8,128)} copy-done((f32[8,256,128]{2,1,0:T(8,128)}, f32[8,256,128]{2,1,0:T(8,128)S(1)}, u32[]{:S(2)}) %copy-start.2) | copy-done | bytes 1048600
  72.6 4.8 %collective-permute-start.4 = (f32[8,8192]{1,0:T(8,128)}, f32[8,8192]{1,0:T(8,128)}, u32[]{:S(2)}, u32[]{:S(2)}) collective-permute-start(f32[8,8192]{1,0:T(8,128)} %get-tuple-element.36), channel_id=1, source_target_pairs={{0,16},{16,32},{32,48},{48,64},{64,80},{80,96},{96,112},{1,17},{17... | collective-permute-start | bytes 786440 | tf_op jit(solution)/shard_map/ppermute | solution.py:624
  77.4 3.5 %collective-permute-start.5 = (f32[8,8192]{1,0:T(8,128)}, f32[8,8192]{1,0:T(8,128)}, u32[]{:S(2)}, u32[]{:S(2)}) collective-permute-start(f32[8,8192]{1,0:T(8,128)} %get-tuple-element.37), channel_id=1, source_target_pairs={{16,0},{32,16},{48,32},{64,48},{80,64},{96,80},{112,96},{17,1},{33... | collective-permute-start | bytes 786440 | tf_op jit(solution)/shard_map/ppermute | solution.py:624
  80.9 0.1 collective-permute-start.6
  81.0 3.8 %collective-permute-start.7 = (f32[8,8192]{1,0:T(8,128)S(1)}, f32[8,8192]{1,0:T(8,128)}, u32[]{:S(2)}, u32[]{:S(2)}) collective-permute-start(f32[8,8192]{1,0:T(8,128)S(1)} %get-tuple-element.39), channel_id=1, source_target_pairs={{0,15},{1,0},{2,1},{3,2},{4,3},{5,4},{6,5},{7,6},{8,7},{9,8},{10,9... | collective-permute-start | bytes 786440 | tf_op jit(solution)/shard_map/ppermute | solution.py:629
  84.8 1.2 %reshape.37.offsets = f32[512,128]{1,0:T(8,128)S(1)} reshape(f32[2,32768]{1,0:T(2,128)} %param.11) | data formatting | bytes 524288 | tf_op jit(solution)/shard_map/reshape | solution.py:618
  86.0 0.0 copy-start.3
  86.0 1.2 %copy-done.3 = f32[8,256,128]{2,1,0:T(8,128)S(1)} copy-done((f32[8,256,128]{2,1,0:T(8,128)S(1)}, f32[8,256,128]{2,1,0:T(8,128)}, u32[]{:S(2)}) %copy-start.3) | copy-done | bytes 1048600
  87.2 4.9 %restore.1 = f32[8,32768]{1,0:T(8,128)} custom-call(f32[8,256,128]{2,1,0:T(8,128)S(1)} %copy-done.3, f32[512,128]{1,0:T(8,128)S(1)} %reshape.37.offsets, s32[2,9,32,8,128]{4,3,2,1,0:T(8,128)S(1)} %get-tuple-element.33.index, s32[2,2,32,8,128]{4,3,2,1,0:T(8,128)S(1)} %get-tuple-element.34.words), custom_call_target="tpu_custom_call" | custom-call | flops 10000000 | bytes 4000000 | tf_op jit(solution)/shard_map/restore/pallas_call | solution.py:609
  92.1 0.0 collective-permute-done.4
  92.1 0.0 collective-permute-done.5
  92.1 0.0 collective-permute-done.6
  92.1 0.0 collective-permute-done.7
  92.2 2.2 %pad_maximum_fusion = f32[8,32768]{1,0:T(8,128)} fusion(f32[8,8192]{1,0:T(8,128)} %collective-permute-done.7, f32[8,8192]{1,0:T(8,128)} %collective-permute-done.6, f32[8,8192]{1,0:T(8,128)} %collective-permute-done.5, f32[8,8192]{1,0:T(8,128)} %collective-permute-done.4), kind=kLoop, calls=%fused_computation | loop fusion | flops 786432 | bytes 2097152 | tf_op jit(solution)/shard_map/concatenate | solution.py:651
  (1 shorter events, 0.0 us)
Async XLA Ops:
  0.6 12.4 %copy-start.7 = (f32[2,32768]{1,0:T(2,128)S(1)}, f32[2,32768]{1,0:T(2,128)}, u32[]{:S(2)}) copy-start(f32[2,32768]{1,0:T(2,128)} %param.11) | copy-start | bytes 786436
  0.6 12.4 %copy-start.4 = (s32[32768]{0:T(1024)S(1)}, s32[32768]{0:T(1024)}, u32[]{:S(2)}) copy-start(s32[32768]{0:T(1024)} %param.10) | copy-start | bytes 393220
  0.7 12.4 %copy-start.5 = (s32[32768]{0:T(1024)S(1)}, s32[32768]{0:T(1024)}, u32[]{:S(2)}) copy-start(s32[32768]{0:T(1024)} %param.12) | copy-start | bytes 393220
  3.3 32.0 %all-to-all-start = ((f32[16,8,1664]{2,1,0:T(8,128)}), f32[16,8,1664]{2,1,0:T(8,128)}, u32[]{:S(2)}, u32[]{:S(2)}) async-start(f32[16,8,1664]{2,1,0:T(8,128)} %get-tuple-element.23), calls=%async_computation | async-start | bytes 1703936 | tf_op jit(solution)/shard_map/all_to_all | solution.py:634
  9.1 26.2 %collective-permute-start = (f32[128,128]{1,0:T(8,128)}, f32[128,128]{1,0:T(8,128)}, u32[]{:S(2)}, u32[]{:S(2)}) collective-permute-start(f32[128,128]{1,0:T(8,128)} %get-tuple-element.26), channel_id=1, source_target_pairs={{0,1},{1,2},{2,3},{3,4},{4,5},{5,6},{6,7},{7,8},{8,9},{9,10},{10,1... | collective-permute-start | bytes 196616 | tf_op jit(solution)/shard_map/ppermute | solution.py:629
  9.4 25.8 %collective-permute-start.1 = (f32[128,128]{1,0:T(8,128)}, f32[128,128]{1,0:T(8,128)}, u32[]{:S(2)}, u32[]{:S(2)}) collective-permute-start(f32[128,128]{1,0:T(8,128)} %get-tuple-element.27), channel_id=1, source_target_pairs={{0,15},{1,0},{2,1},{3,2},{4,3},{5,4},{6,5},{7,6},{8,7},{9,8},{10,9... | collective-permute-start | bytes 196616 | tf_op jit(solution)/shard_map/ppermute | solution.py:629
  13.0 0.9 copy-start.6
  38.2 25.9 %collective-permute-start.2 = (f32[24,128]{1,0:T(8,128)}, f32[24,128]{1,0:T(8,128)S(1)}, u32[]{:S(2)}, u32[]{:S(2)}) collective-permute-start(f32[24,128]{1,0:T(8,128)} %get-tuple-element.29), channel_id=1, source_target_pairs={{0,16},{16,32},{32,48},{48,64},{64,80},{80,96},{96,112},{1,17},{17... | collective-permute-start | bytes 36872 | tf_op jit(solution)/shard_map/ppermute | solution.py:624
  43.7 20.4 %collective-permute-start.3 = (f32[24,128]{1,0:T(8,128)}, f32[24,128]{1,0:T(8,128)S(1)}, u32[]{:S(2)}, u32[]{:S(2)}) collective-permute-start(f32[24,128]{1,0:T(8,128)} %get-tuple-element.30), channel_id=1, source_target_pairs={{16,0},{32,16},{48,32},{64,48},{80,64},{96,80},{112,96},{17,1},{33... | collective-permute-start | bytes 36872 | tf_op jit(solution)/shard_map/ppermute | solution.py:624
  46.6 1.4 %copy-start = (f32[8,384,128]{2,1,0:T(8,128)S(1)}, f32[8,384,128]{2,1,0:T(8,128)}, u32[]{:S(2)}) copy-start(f32[8,384,128]{2,1,0:T(8,128)} %get-tuple-element.28.table) | copy-start | bytes 4718596
  48.0 16.1 %copy-start.1 = (f32[8,384,128]{2,1,0:T(8,128)S(1)}, f32[8,384,128]{2,1,0:T(8,128)}, u32[]{:S(2)}) copy-start(f32[8,384,128]{2,1,0:T(8,128)} %get-tuple-element.28.table) | copy-start | bytes 4718596
  71.6 1.0 %copy-start.2 = (f32[8,256,128]{2,1,0:T(8,128)}, f32[8,256,128]{2,1,0:T(8,128)S(1)}, u32[]{:S(2)}) copy-start(f32[8,256,128]{2,1,0:T(8,128)S(1)} %get-tuple-element.35.state) | copy-start | bytes 3145732
  72.6 19.5 %collective-permute-start.4 = (f32[8,8192]{1,0:T(8,128)}, f32[8,8192]{1,0:T(8,128)}, u32[]{:S(2)}, u32[]{:S(2)}) collective-permute-start(f32[8,8192]{1,0:T(8,128)} %get-tuple-element.36), channel_id=1, source_target_pairs={{0,16},{16,32},{32,48},{48,64},{64,80},{80,96},{96,112},{1,17},{17... | collective-permute-start | bytes 786440 | tf_op jit(solution)/shard_map/ppermute | solution.py:624
  77.4 14.8 %collective-permute-start.5 = (f32[8,8192]{1,0:T(8,128)}, f32[8,8192]{1,0:T(8,128)}, u32[]{:S(2)}, u32[]{:S(2)}) collective-permute-start(f32[8,8192]{1,0:T(8,128)} %get-tuple-element.37), channel_id=1, source_target_pairs={{16,0},{32,16},{48,32},{64,48},{80,64},{96,80},{112,96},{17,1},{33... | collective-permute-start | bytes 786440 | tf_op jit(solution)/shard_map/ppermute | solution.py:624
  80.9 11.3 %collective-permute-start.6 = (f32[8,8192]{1,0:T(8,128)}, f32[8,8192]{1,0:T(8,128)}, u32[]{:S(2)}, u32[]{:S(2)}) collective-permute-start(f32[8,8192]{1,0:T(8,128)} %get-tuple-element.38), channel_id=1, source_target_pairs={{0,1},{1,2},{2,3},{3,4},{4,5},{5,6},{6,7},{7,8},{8,9},{9,10},{10,1... | collective-permute-start | bytes 786440 | tf_op jit(solution)/shard_map/ppermute | solution.py:629
  81.0 11.2 %collective-permute-start.7 = (f32[8,8192]{1,0:T(8,128)S(1)}, f32[8,8192]{1,0:T(8,128)}, u32[]{:S(2)}, u32[]{:S(2)}) collective-permute-start(f32[8,8192]{1,0:T(8,128)S(1)} %get-tuple-element.39), channel_id=1, source_target_pairs={{0,15},{1,0},{2,1},{3,2},{4,3},{5,4},{6,5},{7,6},{8,7},{9,8},{10,9... | collective-permute-start | bytes 786440 | tf_op jit(solution)/shard_map/ppermute | solution.py:629
  86.0 1.2 %copy-start.3 = (f32[8,256,128]{2,1,0:T(8,128)S(1)}, f32[8,256,128]{2,1,0:T(8,128)}, u32[]{:S(2)}) copy-start(f32[8,256,128]{2,1,0:T(8,128)} %copy-done.2) | copy-start | bytes 3145732

commit v4 on v3

--- a/solution.py
+++ b/solution.py
@@ -123,6 +123,8 @@
                         x, y = payload[a], payload[b]
                         payload[a] = jnp.where(swap, y, x)
                         payload[b] = jnp.where(swap, x, y)
+        if t == 8 and not record:
+            break
         if t <= 4:
             runs = [xs[v] for v in range(VREGS)]
             lane_done = []
@@ -252,11 +254,11 @@
     for v in range(VREGS):
         spots = lax.shift_right_logical(keys[v].astype(i32), 7)
         near_out[v] = spots
-        chunks[v * 8 : v * 8 + 8, :] = lax.shift_right_logical(spots, 7).astype(f32)
+        chunks[pl.ds(v, 8, stride=32), :] = lax.shift_right_logical(spots, 7).astype(f32)
     for half in range(2):
-        turned = jnp.transpose(chunks[half * 128 : half * 128 + 128, :]).astype(i32)
-        ends_out[half : half + 1, :] = turned[0:1]
-        ends_out[half + 2 : half + 3, :] = turned[127:128]
+        turned = jnp.transpose(chunks[half * 128 : half * 128 + 128, :])
+        ends_out[half : half + 1, :] = jnp.min(turned, axis=0, keepdims=True).astype(i32)
+        ends_out[half + 2 : half + 3, :] = jnp.max(turned, axis=0, keepdims=True).astype(i32)
 
     def one(which, carry):
         keys = [
@@ -298,7 +300,7 @@
     )(cells.reshape(256, 128), offsets.reshape(2, 256, 128), moves.reshape(256, 128), slots.reshape(256, 128))
 
 
-def pack_kernel(ocean, mass, momentum, out, last, first):
+def pack_kernel(ocean, mass, momentum, out):
     lane = lax.broadcasted_iota(i32, (8, 128), 1)
     tiles = LON * BLOCKS
 
@@ -318,30 +320,28 @@
             rim = jnp.where(lane == spot + 2, pltpu.roll(tile(part, BLOCKS * b + BLOCKS), spot + 2, 1), rim)
         out[b, :, 4 * COLS : 4 * COLS + 128] = rim
     lanes = lax.broadcasted_iota(i32, (ROWS, 128), 1)
-    for side, out_side in ((0, last), (1, first)):
+    beside = jnp.ones((ROWS, 128), f32)
+    for side in range(2):
         column = 0 if side else COLS - 128
         sources = [mass[:, column : column + 128]] * 2 + [
             momentum[part, :, column : column + 128] for part in range(2)
         ]
-        rim = jnp.ones((ROWS, 128), f32)
         for source, spot in zip(sources, spots):
             spot = spot + 2 * side
             shift = spot if side else spot + 1
-            rim = jnp.where(lanes == spot, pltpu.roll(source, shift, 1), rim)
-        out_side[...] = rim
+            beside = jnp.where(lanes == spot, pltpu.roll(source, shift, 1), beside)
+    turned = jnp.transpose(beside)[0:8]
+    for b in range(LON):
+        out[b, :, 4 * COLS + 128 : 4 * COLS + 256] = turned
 
 
 def pack(ocean, mass, momentum):
     vmem = pl.BlockSpec(memory_space=pltpu.VMEM)
     return pl.pallas_call(
         pack_kernel,
-        out_shape=[
-            jax.ShapeDtypeStruct((LON, 8, 4 * COLS + 128), f32),
-            jax.ShapeDtypeStruct((ROWS, 128), f32),
-            jax.ShapeDtypeStruct((ROWS, 128), f32),
-        ],
+        out_shape=jax.ShapeDtypeStruct((LON, 8, 4 * COLS + 256), f32),
         in_specs=[vmem] * 3,
-        out_specs=[vmem] * 3,
+        out_specs=vmem,
         name="pack",
     )(ocean, mass, momentum)
 
@@ -352,10 +352,14 @@
     )
 
 
-def table_kernel(forcing, mass, momentum, west, east, table, first_edge, last_edge):
+def table_kernel(beside_spots, forcing, mass, momentum, table, first_edge, last_edge):
     lane = lax.broadcasted_iota(i32, (ROWS, 128), 1)
     rim = forcing[:, :, 4 * COLS : 4 * COLS + 128].reshape(ROWS, 128)
-    beside = jnp.where((lane & 2) == 0, west[...], east[...])
+    west = forcing[beside_spots[0], :, 4 * COLS + 128 : 4 * COLS + 256]
+    east = forcing[beside_spots[1], :, 4 * COLS + 128 : 4 * COLS + 256]
+    beside = jnp.where((sublane_ids() & 2) == 0, west, east)
+    beside = jnp.concatenate([beside] + [jnp.ones((120, 128), f32)], axis=0)
+    beside = jnp.transpose(beside)
     rim = drive(pltpu.roll(beside, 124, 1), pltpu.roll(rim, 124, 1), beside, rim)
     for part in range(2):
         blocks, after, before = [], [], []
@@ -382,29 +386,30 @@
             )
             for q in range(3):
                 plane = part * 3 + q
-                spot = plane * BLOCKS + k
-                table[plane, ROWS * k : ROWS * k + ROWS, :] = shifted[q]
-                first_edge[spot : spot + 1, :] = shifted[q][0:1]
-                last_edge[spot : spot + 1, :] = shifted[q][ROWS - 1 : ROWS]
+                for r in range(0, ROWS, 8):
+                    table[pl.ds((ROWS * k + r) * 8 + plane, 8, stride=8), :] = shifted[q][r : r + 8]
     for plane in (6, 7):
-        table[plane] = jnp.zeros((PLANE, 128), f32)
-    first_edge[18:24, :] = jnp.zeros((6, 128), f32)
-    last_edge[18:24, :] = jnp.zeros((6, 128), f32)
-
-
-def node_table(forcing, mass, momentum, west, east):
+        for r in range(0, PLANE, 8):
+            table[pl.ds(r * 8 + plane, 8, stride=8), :] = jnp.zeros((8, 128), f32)
+    for k in range(BLOCKS):
+        top, end = ROWS * k * 8, (ROWS * k + ROWS - 1) * 8
+        first_edge[8 * k : 8 * k + 8, :] = table[top : top + 8, :]
+        last_edge[8 * k : 8 * k + 8, :] = table[end : end + 8, :]
+
+
+def node_table(beside_spots, forcing, mass, momentum):
     vmem = pl.BlockSpec(memory_space=pltpu.VMEM)
     return pl.pallas_call(
         table_kernel,
         out_shape=[
-            jax.ShapeDtypeStruct((8, PLANE, 128), f32),
+            jax.ShapeDtypeStruct((8 * PLANE, 128), f32),
             jax.ShapeDtypeStruct((24, 128), f32),
             jax.ShapeDtypeStruct((24, 128), f32),
         ],
-        in_specs=[vmem] * 5,
+        in_specs=[pl.BlockSpec(memory_space=pltpu.SMEM)] + [vmem] * 3,
         out_specs=[vmem] * 3,
         name="table",
-    )(forcing, mass, momentum, west, east)
+    )(beside_spots, forcing, mass, momentum)
 
 
 def spline(frac):
@@ -414,12 +419,12 @@
     return (lower, middle, upper)
 
 
-def interpolate_group(g, ends, near, frac, nodes, stride, address, samples, state):
-    high = lax.shift_right_logical(g & 3, 1)
-    low = (g & 1) * 64 + lax.shift_right_logical(g, 2)
+def interpolate_group(g, ends, near, frac, nodes, address, samples, state):
+    half = lax.shift_right_logical(g, 4)
+    low = (g & 15) * 8
     start = (g & 3) * 64 + lax.shift_right_logical(g, 2)
-    first = [ends[high, low + 8 * j] for j in range(8)]
-    last = [ends[high + 2, low + 8 * j] for j in range(8)]
+    first = [ends[half, low + j] for j in range(8)]
+    last = [ends[half + 2, low + j] for j in range(8)]
     span = last[0] - first[0]
     for j in range(1, 8):
         span = jnp.maximum(span, last[j] - first[j])
@@ -435,8 +440,8 @@
                 base = address(here)
                 inside = chunk == here
                 for r in range(3):
-                    got = from_lanes(nodes[pl.ds(base + r - 1, 8, stride=stride), :], lanes)
-                    sums[3 * j + r] = jnp.where(inside, got, sums[3 * j + r])
+                    tile = nodes[pl.ds(pl.multiple_of((base + r - 1) * 8, 8), 8), :]
+                    sums[3 * j + r] = jnp.where(inside, from_lanes(tile, lanes), sums[3 * j + r])
         return tuple(sums)
 
     trips = lax.shift_right_logical(span, 1) + 1
@@ -475,7 +480,7 @@
 
 
 def group_first(g, ends):
-    return ends[lax.shift_right_logical(g & 3, 1), (g & 1) * 64 + lax.shift_right_logical(g, 2)]
+    return ends[lax.shift_right_logical(g, 4), (g & 15) * 8]
 
 
 def inner_kernel(ends, table, near, frac, state, samples):
@@ -483,7 +488,7 @@
         @pl.when(group_first(g, ends) >= 8)
         def _():
             interpolate_group(
-                g, ends, near, frac, table, PLANE, lambda chunk: chunk - 8, samples, state
+                g, ends, near, frac, table, lambda chunk: chunk - 8, samples, state
             )
 
         return carry
@@ -503,7 +508,7 @@
         compiler_params=pltpu.CompilerParams(vmem_limit_bytes=24 << 20),
         cost_estimate=pl.CostEstimate(flops=20_000_000, bytes_accessed=8_000_000, transcendentals=0),
         name="inner",
-    )(ends, table.reshape(8 * PLANE, 128), near.reshape(256, 128), frac.reshape(2, 256, 128))
+    )(ends, table, near.reshape(256, 128), frac.reshape(2, 256, 128))
 
 
 def transfer_kernel(
@@ -514,18 +519,19 @@
 ):
     for c in range(8):
         state[c] = early[c]
-    for plane in range(6):
-        base = plane * EDGE_PLANE
-        nodes[base : base + PLANE, :] = table[plane]
-        for k in range(BLOCKS):
-            spot = plane * BLOCKS + k
-            edge = base + PLANE + 8 * k
-            top = k * ROWS
-            nodes[edge : edge + 1, :] = above[spot : spot + 1, :]
-            nodes[edge + 1 : edge + 3, :] = table[plane, top : top + 2, :]
-            nodes[edge + 4 : edge + 6, :] = table[plane, top + ROWS - 2 : top + ROWS, :]
-            nodes[edge + 6 : edge + 7, :] = below[spot : spot + 1, :]
-    nodes[6 * EDGE_PLANE : 8 * EDGE_PLANE, :] = jnp.zeros((2 * EDGE_PLANE, 128), f32)
+    nodes[0 : 8 * PLANE, :] = table[...]
+
+    def fill(spot, tile):
+        nodes[(PLANE + spot) * 8 : (PLANE + spot) * 8 + 8, :] = tile
+
+    for k in range(BLOCKS):
+        top, end = ROWS * k * 8, (ROWS * k + ROWS - 1) * 8
+        fill(8 * k, above[8 * k : 8 * k + 8, :])
+        fill(8 * k + 1, table[top : top + 8, :])
+        fill(8 * k + 2, table[top + 8 : top + 16, :])
+        fill(8 * k + 4, table[end - 8 : end, :])
+        fill(8 * k + 5, table[end : end + 8, :])
+        fill(8 * k + 6, below[8 * k : 8 * k + 8, :])
 
     def address(chunk):
         return jnp.where(chunk < 8, PLANE + 1 + 4 * chunk, jnp.maximum(chunk - 8, 1))
@@ -533,7 +539,7 @@
     def group(g, carry):
         @pl.when(group_first(g, ends) < 8)
         def _():
-            interpolate_group(g, ends, near, frac, nodes, EDGE_PLANE, address, samples, state)
+            interpolate_group(g, ends, near, frac, nodes, address, samples, state)
 
         return carry
 
@@ -590,7 +596,7 @@
 def restore_kernel(state, offsets, index, words, out, columns, buffer):
     def finish(v, moved):
         for c in range(2):
-            frac = offsets[pl.ds(c * 256 + v, 8, stride=32), :]
+            frac = offsets[c, pl.ds(v, 8, stride=32), :]
             columns[pl.ds(v * 8 + c, 8, stride=256), :] = frac + step_dt * moved[c]
         for c in range(6):
             columns[pl.ds(v * 8 + c + 2, 8, stride=256), :] = moved[c]
@@ -615,7 +621,7 @@
         compiler_params=pltpu.CompilerParams(vmem_limit_bytes=32 << 20),
         cost_estimate=pl.CostEstimate(flops=10_000_000, bytes_accessed=4_000_000, transcendentals=0),
         name="restore",
-    )(state, offsets.reshape(512, 128), index, words)
+    )(state, offsets.reshape(2, 256, 128), index, words)
 
 
 def from_behind(block, axis, distance):
@@ -630,13 +636,13 @@
 
 
 def shards(ocean, grid_mass, grid_momentum, cells, offsets, moves, slots):
-    outgoing, last, first = pack(ocean, grid_mass, grid_momentum)
+    outgoing = pack(ocean, grid_mass, grid_momentum)
     forcing = lax.all_to_all(outgoing, "lon", 0, 0)
-    west = passed_along(last, "lon", 1)
-    east = passed_along(first, "lon", -1)
     near, ends, frac, counts, index, words = plan(cells, offsets, moves, slots)
     forcing, near = lax.optimization_barrier((forcing, near))
-    table, first_edge, last_edge = node_table(forcing, grid_mass, grid_momentum, west, east)
+    here = lax.axis_index("lon")
+    beside_spots = jnp.stack([(here + LON - 1) % LON, (here + 1) % LON])
+    table, first_edge, last_edge = node_table(beside_spots, forcing, grid_mass, grid_momentum)
     above = from_behind(last_edge, "lat", 1)
     below = from_behind(first_edge, "lat", -1)
     early = inner(ends, table, near, frac)

time: 95 us -> 88.6 us (0.933)
  Pallas kernels: 55.3 us -> 51.2 us
  starting transfers between devices: 30.3 us -> 26.4 us
  waiting for transfers between devices: 0.02 us -> 3.45 us
  local copies, waits for them, and re-layouts: 5.7 us -> 4.13 us
    ppermute x4 -> x2, starting transfers between devices: 7.84 us -> 3.92 us  [passed_along(): lax.ppermute(value, axis, [(i, (i + by) % count) for i in range(count)])]
    ppermute x4, waiting for transfers between devices: 0.01 us -> 3.44 us  [from_behind(): return lax.ppermute(block, axis, route)]
    pallas_call x1, Pallas kernels: 16 us -> 13.4 us  [inner(): pl.pallas_call(inner_kernel, out_shape=jax.ShapeDtypeStruct((8, 256, 128)...]
    concatenate x1, other arithmetic: 2.23 us -> 1.04 us  [shards(): return (parcels, jnp.concatenate([north, south, east, west], axis=1))]
    reshape x1 -> x0, local copies, waits for them, and re-layouts: 1.18 us -> none  [restore(): offsets.reshape(512, 128)]
    pallas_call x1, Pallas kernels: 7.55 us -> 6.48 us  [transfer(): pl.pallas_call(transfer_kernel, out_shape=[jax.ShapeDtypeStruct((8, 256,...]
    unnamed x17 -> x13, local copies, waits for them, and re-layouts: 4.53 us -> 4.13 us
  transfers between devices with their start and end apart: 9 -> 7, of which waited for: 0 -> 2; matrix products, arithmetic and copies ran while one was open for 1% -> 1% of each run, Pallas kernels for 45% -> 45%
where the time goes in v4:
time: 88.6 us; the launch traced here: 87.6 us
  Pallas kernels  51.2 us (58%)
  starting transfers between devices  26.4 us (30%)
  local copies, waits for them, and re-layouts  4.13 us (5%)
  waiting for transfers between devices  3.45 us (4%)
  other arithmetic  1.63 us (2%)
    pallas_call x1, Pallas kernels, plan(): pl.pallas_call(plan_kernel, out_shape=[jax.ShapeDtypeStruct((VREGS, 8, 12...  20.6 us
    ppermute x4, starting transfers between devices, from_behind(): return lax.ppermute(block, axis, route)  16.7 us
    pallas_call x1, Pallas kernels, inner(): pl.pallas_call(inner_kernel, out_shape=jax.ShapeDtypeStruct((8, 256, 128)...  13.4 us
    pallas_call x1, Pallas kernels, transfer(): pl.pallas_call(transfer_kernel, out_shape=[jax.ShapeDtypeStruct((8, 256,...  6.48 us
    all_to_all x1, starting transfers between devices, shards(): forcing = lax.all_to_all(outgoing, 'lon', 0, 0)  5.8 us
    pallas_call x1, Pallas kernels, restore(): pl.pallas_call(restore_kernel, out_shape=jax.ShapeDtypeStruct((8, 4 * CAP...  4.94 us
    unnamed x13, local copies, waits for them, and re-layouts  4.13 us
    ppermute x2, starting transfers between devices, passed_along(): lax.ppermute(value, axis, [(i, (i + by) % count) for i in range(count)])  3.92 us
  transfers between devices with their start and end apart: 7, of which 2 were waited for; matrix products, arithmetic and copies ran while one was open for 1% of the time, Pallas kernels for 45%

profile of v4, /device:TPU:8, one launch (start us, length us, event | category | flops | bytes accessed | tf_op | source)
XLA Modules:
  0.0 87.6 jit_solution(1114143089963743306)
XLA Ops:
  0.6 0.0 copy-start.5
  0.6 2.7 %pack.1 = f32[16,8,1792]{2,1,0:T(8,128)} custom-call(f32[4,8,6144]{2,1,0:T(8,128)} %ocean.1, f32[128,384]{1,0:T(8,128)} %mass.3, f32[2,128,384]{2,1,0:T(8,128)} %momentum.3), custom_call_target="tpu_custom_call" | custom-call | tf_op jit(solution)/shard_map/pack/pallas_call | solution.py:340
  3.3 5.8 %all-to-all-start = ((f32[16,8,1792]{2,1,0:T(8,128)}), f32[16,8,1792]{2,1,0:T(8,128)}, u32[]{:S(2)}, u32[]{:S(2)}) async-start(f32[16,8,1792]{2,1,0:T(8,128)} %pack.1), calls=%async_computation | async-start | bytes 1835008 | tf_op jit(solution)/shard_map/all_to_all | solution.py:640
  9.1 0.0 copy-done.5
  9.2 0.0 copy-start.2
  9.2 0.9 %copy-done.2 = s32[32768]{0:T(1024)S(1)} copy-done((s32[32768]{0:T(1024)S(1)}, s32[32768]{0:T(1024)}, u32[]{:S(2)}) %copy-start.2) | copy-done | bytes 131096
  10.1 0.0 copy-start.3
  10.1 0.9 %copy-done.3 = s32[32768]{0:T(1024)S(1)} copy-done((s32[32768]{0:T(1024)S(1)}, s32[32768]{0:T(1024)}, u32[]{:S(2)}) %copy-start.3) | copy-done | bytes 131096
  11.0 0.0 copy-start.4
  11.0 0.9 %copy-done.4 = s32[32768]{0:T(1024)S(1)} copy-done((s32[32768]{0:T(1024)S(1)}, s32[32768]{0:T(1024)}, u32[]{:S(2)}) %copy-start.4) | copy-done | bytes 131096
  11.9 20.6 %plan.1 = (s32[32,8,128]{2,1,0:T(8,128)S(1)}, s32[4,128]{1,0:T(4,128)S(1)}, f32[2,32,8,128]{3,2,1,0:T(8,128)S(1)}, s32[4]{0:T(128)S(1)}, s32[2,9,32,8,128]{4,3,2...) custom-call(s32[256,128]{1,0:T(8,128)S(1)} %bitcast.17, f32[2,256,128]{2,1,0:T(8,128)S(1)} %bitcast.11, ...), custom_call_target="tpu_custom_call" | custom-call | flops 20000000 | bytes 8000000 | tf_op jit(solution)/shard_map/plan/pallas_call | solution.py:284
  32.6 0.6 pad_add_fusion.beside_spots
  33.2 0.0 all-to-all-done.forcing
  33.2 3.1 %table.1 = (f32[3072,128]{1,0:T(8,128)}, f32[24,128]{1,0:T(8,128)}, f32[24,128]{1,0:T(8,128)}) custom-call(s32[2]{0:T(128)} %pad_add_fusion.beside_spots, f32[16,8,1792]{2,1,0:T(8,128)} %all-to-all-done.forcing, f32[128,384]{1,0:T(8,128)} %mass.3, f32[2,128,384]{2,1,0:T(8,128)} %momentum.3), custom_call_target="tpu_custom_call" | custom-call | tf_op jit(solution)/shard_map/table/pallas_call | solution.py:402
  36.2 5.5 %collective-permute-start = (f32[24,128]{1,0:T(8,128)}, f32[24,128]{1,0:T(8,128)S(1)}, u32[]{:S(2)}, u32[]{:S(2)}) collective-permute-start(f32[24,128]{1,0:T(8,128)} %get-tuple-element.23), channel_id=1, source_target_pairs={{0,16},{16,32},{32,48},{48,64},{64,80},{80,96},{96,112},{1,17},{17... | collective-permute-start | bytes 36872 | tf_op jit(solution)/shard_map/ppermute | solution.py:630
  41.7 2.9 %collective-permute-start.1 = (f32[24,128]{1,0:T(8,128)}, f32[24,128]{1,0:T(8,128)S(1)}, u32[]{:S(2)}, u32[]{:S(2)}) collective-permute-start(f32[24,128]{1,0:T(8,128)} %get-tuple-element.24), channel_id=1, source_target_pairs={{16,0},{32,16},{48,32},{64,48},{80,64},{96,80},{112,96},{17,1},{33... | collective-permute-start | bytes 36872 | tf_op jit(solution)/shard_map/ppermute | solution.py:630
  44.7 0.0 copy-start
  44.7 1.4 %copy-done = f32[3072,128]{1,0:T(8,128)S(1)} copy-done((f32[3072,128]{1,0:T(8,128)S(1)}, f32[3072,128]{1,0:T(8,128)}, u32[]{:S(2)}) %copy-start) | copy-done | bytes 1572888
  46.1 0.0 copy-start.1
  46.1 13.4 %inner.1.early = f32[8,256,128]{2,1,0:T(8,128)S(1)} custom-call(s32[4,128]{1,0:T(4,128)S(1)} %get-tuple-element.18.ends, f32[3072,128]{1,0:T(8,128)S(1)} %copy-done, s32[256,128]{1,0:T(8,128)S(1)} %bitcast.15, f32[2,256,128]{2,1,0:T(8,128)S(1)} %bitcast.13), custom_call_target="tpu_custom_call" | custom-call | flops 20000000 | bytes 8000000 | tf_op jit(solution)/shard_map/inner/pallas_call | solution.py:502
  59.5 0.0 collective-permute-done.above
  59.5 0.0 collective-permute-done.1.below
  59.5 0.0 copy-done.1
  59.5 6.5 %transfer.1 = (f32[8,256,128]{2,1,0:T(8,128)S(1)}, f32[8,8192]{1,0:T(8,128)S(1)}, f32[8,8192]{1,0:T(8,128)S(1)}, f32[8,8192]{1,0:T(8,128)S(1)}, f32[8,8192]{1,0:T(8,128)S(1)}) custom-call(s32[4,128]{1,0:T(4,128)S(1)} %get-tuple-element.18.ends, s32[4]{0:T(128)S(1)} %get-tuple-element.19.counts, f32[3072,128]{1,0:T(8,128)S(1)} %copy-done.1, ...), custom_call_target="tpu_custom_call" | custom-call | flops 10000000 | bytes 8000000 | tf_op jit(solution)/shard_map/transfer/pallas_call | solution.py:575
  66.0 4.7 %collective-permute-start.2 = (f32[8,8192]{1,0:T(8,128)S(1)}, f32[8,8192]{1,0:T(8,128)S(1)}, u32[]{:S(2)}, u32[]{:S(2)}) collective-permute-start(f32[8,8192]{1,0:T(8,128)S(1)} %get-tuple-element.30), channel_id=1, source_target_pairs={{0,16},{16,32},{32,48},{48,64},{64,80},{80,96},{96,112},{1,17},{17... | collective-permute-start | bytes 786440 | tf_op jit(solution)/shard_map/ppermute | solution.py:630
  70.8 3.5 %collective-permute-start.3 = (f32[8,8192]{1,0:T(8,128)S(1)}, f32[8,8192]{1,0:T(8,128)S(1)}, u32[]{:S(2)}, u32[]{:S(2)}) collective-permute-start(f32[8,8192]{1,0:T(8,128)S(1)} %get-tuple-element.31), channel_id=1, source_target_pairs={{16,0},{32,16},{48,32},{64,48},{80,64},{96,80},{112,96},{17,1},{33... | collective-permute-start | bytes 786440 | tf_op jit(solution)/shard_map/ppermute | solution.py:630
  74.3 0.1 collective-permute-start.4
  74.4 3.8 %collective-permute-start.5 = (f32[8,8192]{1,0:T(8,128)S(1)}, f32[8,8192]{1,0:T(8,128)S(1)}, u32[]{:S(2)}, u32[]{:S(2)}) collective-permute-start(f32[8,8192]{1,0:T(8,128)S(1)} %get-tuple-element.33), channel_id=1, source_target_pairs={{0,15},{1,0},{2,1},{3,2},{4,3},{5,4},{6,5},{7,6},{8,7},{9,8},{10,9... | collective-permute-start | bytes 786440 | tf_op jit(solution)/shard_map/ppermute | solution.py:635
  78.2 4.9 %restore.1 = f32[8,32768]{1,0:T(8,128)} custom-call(f32[8,256,128]{2,1,0:T(8,128)S(1)} %get-tuple-element.29.state, f32[2,256,128]{2,1,0:T(8,128)S(1)} %bitcast.12, s32[2,9,32,8,128]{4,3,2,1,0:T(8,128)S(1)} %get-tuple-element.27.index, s32[2,2,32,8,128]{4,3,2,1,0:T(8,128)S(1)} %get-tuple-element.28.words), custom_call_target="tpu_custom_call" | custom-call | flops 10000000 | bytes 4000000 | tf_op jit(solution)/shard_map/restore/pallas_call | solution.py:615
  83.1 1.4 %collective-permute-done.2 = f32[8,8192]{1,0:T(8,128)S(1)} collective-permute-done((f32[8,8192]{1,0:T(8,128)S(1)}, f32[8,8192]{1,0:T(8,128)S(1)}, u32[]{:S(2)}, u32[]{:S(2)}) %collective-permute-start.2) | collective-permute-done | bytes 262176 | tf_op jit(solution)/shard_map/ppermute | solution.py:630
  84.5 2.1 %collective-permute-done.3 = f32[8,8192]{1,0:T(8,128)S(1)} collective-permute-done((f32[8,8192]{1,0:T(8,128)S(1)}, f32[8,8192]{1,0:T(8,128)S(1)}, u32[]{:S(2)}, u32[]{:S(2)}) %collective-permute-start.3) | collective-permute-done | bytes 262176 | tf_op jit(solution)/shard_map/ppermute | solution.py:630
  86.6 0.0 collective-permute-done.4
  86.6 0.0 collective-permute-done.5
  86.6 1.0 %pad_maximum_fusion = f32[8,32768]{1,0:T(8,128)} fusion(f32[8,8192]{1,0:T(8,128)S(1)} %collective-permute-done.5, f32[8,8192]{1,0:T(8,128)S(1)} %collective-permute-done.4, f32[8,8192]{1,0:T(8,128)S(1)} %collective-permute-done.3, f32[8,8192]{1,0:T(8,128)S(1)} %collective-permute-done.2), kind=kLoop, calls=%fused_computation | loop fusion | flops 786432 | bytes 2097152 | tf_op jit(solution)/shard_map/concatenate | solution.py:657
  (1 shorter events, 0.0 us)
Async XLA Ops:
  0.6 8.5 %copy-start.5 = (f32[2,32768]{1,0:T(2,128)S(1)}, f32[2,32768]{1,0:T(2,128)}, u32[]{:S(2)}) copy-start(f32[2,32768]{1,0:T(2,128)} %param.11) | copy-start | bytes 786436
  3.3 29.8 %all-to-all-start = ((f32[16,8,1792]{2,1,0:T(8,128)}), f32[16,8,1792]{2,1,0:T(8,128)}, u32[]{:S(2)}, u32[]{:S(2)}) async-start(f32[16,8,1792]{2,1,0:T(8,128)} %pack.1), calls=%async_computation | async-start | bytes 1835008 | tf_op jit(solution)/shard_map/all_to_all | solution.py:640
  9.2 0.9 %copy-start.2 = (s32[32768]{0:T(1024)S(1)}, s32[32768]{0:T(1024)}, u32[]{:S(2)}) copy-start(s32[32768]{0:T(1024)} %param.10) | copy-start | bytes 393220
  10.1 0.9 %copy-start.3 = (s32[32768]{0:T(1024)S(1)}, s32[32768]{0:T(1024)}, u32[]{:S(2)}) copy-start(s32[32768]{0:T(1024)} %param.12) | copy-start | bytes 393220
  11.0 0.9 %copy-start.4 = (s32[32768]{0:T(1024)S(1)}, s32[32768]{0:T(1024)}, u32[]{:S(2)}) copy-start(s32[32768]{0:T(1024)} %param.13) | copy-start | bytes 393220
  36.2 23.3 %collective-permute-start = (f32[24,128]{1,0:T(8,128)}, f32[24,128]{1,0:T(8,128)S(1)}, u32[]{:S(2)}, u32[]{:S(2)}) collective-permute-start(f32[24,128]{1,0:T(8,128)} %get-tuple-element.23), channel_id=1, source_target_pairs={{0,16},{16,32},{32,48},{48,64},{64,80},{80,96},{96,112},{1,17},{17... | collective-permute-start | bytes 36872 | tf_op jit(solution)/shard_map/ppermute | solution.py:630
  41.7 17.8 %collective-permute-start.1 = (f32[24,128]{1,0:T(8,128)}, f32[24,128]{1,0:T(8,128)S(1)}, u32[]{:S(2)}, u32[]{:S(2)}) collective-permute-start(f32[24,128]{1,0:T(8,128)} %get-tuple-element.24), channel_id=1, source_target_pairs={{16,0},{32,16},{48,32},{64,48},{80,64},{96,80},{112,96},{17,1},{33... | collective-permute-start | bytes 36872 | tf_op jit(solution)/shard_map/ppermute | solution.py:630
  44.7 1.4 %copy-start = (f32[3072,128]{1,0:T(8,128)S(1)}, f32[3072,128]{1,0:T(8,128)}, u32[]{:S(2)}) copy-start(f32[3072,128]{1,0:T(8,128)} %get-tuple-element.22.table) | copy-start | bytes 4718596
  46.1 13.5 %copy-start.1 = (f32[3072,128]{1,0:T(8,128)S(1)}, f32[3072,128]{1,0:T(8,128)}, u32[]{:S(2)}) copy-start(f32[3072,128]{1,0:T(8,128)} %get-tuple-element.22.table) | copy-start | bytes 4718596
  66.0 18.5 %collective-permute-start.2 = (f32[8,8192]{1,0:T(8,128)S(1)}, f32[8,8192]{1,0:T(8,128)S(1)}, u32[]{:S(2)}, u32[]{:S(2)}) collective-permute-start(f32[8,8192]{1,0:T(8,128)S(1)} %get-tuple-element.30), channel_id=1, source_target_pairs={{0,16},{16,32},{32,48},{48,64},{64,80},{80,96},{96,112},{1,17},{17... | collective-permute-start | bytes 786440 | tf_op jit(solution)/shard_map/ppermute | solution.py:630
  70.8 15.8 %collective-permute-start.3 = (f32[8,8192]{1,0:T(8,128)S(1)}, f32[8,8192]{1,0:T(8,128)S(1)}, u32[]{:S(2)}, u32[]{:S(2)}) collective-permute-start(f32[8,8192]{1,0:T(8,128)S(1)} %get-tuple-element.31), channel_id=1, source_target_pairs={{16,0},{32,16},{48,32},{64,48},{80,64},{96,80},{112,96},{17,1},{33... | collective-permute-start | bytes 786440 | tf_op jit(solution)/shard_map/ppermute | solution.py:630
  74.3 12.3 %collective-permute-start.4 = (f32[8,8192]{1,0:T(8,128)S(1)}, f32[8,8192]{1,0:T(8,128)S(1)}, u32[]{:S(2)}, u32[]{:S(2)}) collective-permute-start(f32[8,8192]{1,0:T(8,128)S(1)} %get-tuple-element.32), channel_id=1, source_target_pairs={{0,1},{1,2},{2,3},{3,4},{4,5},{5,6},{6,7},{7,8},{8,9},{9,10},{10,1... | collective-permute-start | bytes 786440 | tf_op jit(solution)/shard_map/ppermute | solution.py:635
  74.4 12.2 %collective-permute-start.5 = (f32[8,8192]{1,0:T(8,128)S(1)}, f32[8,8192]{1,0:T(8,128)S(1)}, u32[]{:S(2)}, u32[]{:S(2)}) collective-permute-start(f32[8,8192]{1,0:T(8,128)S(1)} %get-tuple-element.33), channel_id=1, source_target_pairs={{0,15},{1,0},{2,1},{3,2},{4,3},{5,4},{6,5},{7,6},{8,7},{9,8},{10,9... | collective-permute-start | bytes 786440 | tf_op jit(solution)/shard_map/ppermute | solution.py:635

commit v5 on v4

--- a/solution.py
+++ b/solution.py
@@ -154,20 +154,20 @@
 
 def apply_network(count, source, buffer, index, words, sub_words, finish):
     sub = sublane_ids()
+    def lane_phase(t, v, get):
+        lanes = index[t, v]
+        moved = [from_lanes(get(c), lanes) for c in range(count)]
+        for i in range(t, 4, -1):
+            if t < 8:
+                take = bit_set(sub_words[v], sub_place(t + 1, i))
+                perm = sub ^ (1 << (i - 5))
+                moved = [jnp.where(take, from_sublanes(x, perm), x) for x in moved]
+        return moved
+
     for v in range(VREGS):
-        lanes = index[0, v]
-        for c in range(count):
-            buffer[c, v] = from_lanes(source(c, v), lanes)
+        for c, x in enumerate(lane_phase(0, v, lambda c: source(c, v))):
+            buffer[c, v] = x
     for t in range(1, 9):
-        steps = [i for i in range(t - 1, -1, -1) if i >= 5]
-        if steps:
-            for v in range(VREGS):
-                takes = [bit_set(sub_words[v], sub_place(t, i)) for i in steps]
-                for c in range(count):
-                    x = buffer[c, v]
-                    for i, take in zip(steps, takes):
-                        x = jnp.where(take, from_sublanes(x, sub ^ (1 << (i - 5))), x)
-                    buffer[c, v] = x
         top = min(t, 5)
         rounds = {1: ((0,),), 2: ((1, 0),), 3: ((2, 1, 0),), 4: ((3, 2), (1, 0)), 5: ((4, 3), (2, 1, 0))}[top]
         for bits in rounds:
@@ -194,8 +194,7 @@
                     for v in members:
                         buffer[c, v] = xs[v]
         for v in range(VREGS):
-            lanes = index[t, v]
-            moved = [from_lanes(buffer[c, v], lanes) for c in range(count)]
+            moved = lane_phase(t, v, lambda c: buffer[c, v])
             if t < 8:
                 for c in range(count):
                     buffer[c, v] = moved[c]
@@ -352,11 +351,12 @@
     )
 
 
-def table_kernel(beside_spots, forcing, mass, momentum, table, first_edge, last_edge):
+def table_kernel(forcing, mass, momentum, table, first_edge, last_edge):
     lane = lax.broadcasted_iota(i32, (ROWS, 128), 1)
     rim = forcing[:, :, 4 * COLS : 4 * COLS + 128].reshape(ROWS, 128)
-    west = forcing[beside_spots[0], :, 4 * COLS + 128 : 4 * COLS + 256]
-    east = forcing[beside_spots[1], :, 4 * COLS + 128 : 4 * COLS + 256]
+    here = lax.axis_index("lon")
+    west = forcing[lax.rem(here + LON - 1, LON), :, 4 * COLS + 128 : 4 * COLS + 256]
+    east = forcing[lax.rem(here + 1, LON), :, 4 * COLS + 128 : 4 * COLS + 256]
     beside = jnp.where((sublane_ids() & 2) == 0, west, east)
     beside = jnp.concatenate([beside] + [jnp.ones((120, 128), f32)], axis=0)
     beside = jnp.transpose(beside)
@@ -397,7 +397,7 @@
         last_edge[8 * k : 8 * k + 8, :] = table[end : end + 8, :]
 
 
-def node_table(beside_spots, forcing, mass, momentum):
+def node_table(forcing, mass, momentum):
     vmem = pl.BlockSpec(memory_space=pltpu.VMEM)
     return pl.pallas_call(
         table_kernel,
@@ -406,10 +406,10 @@
             jax.ShapeDtypeStruct((24, 128), f32),
             jax.ShapeDtypeStruct((24, 128), f32),
         ],
-        in_specs=[pl.BlockSpec(memory_space=pltpu.SMEM)] + [vmem] * 3,
+        in_specs=[vmem] * 3,
         out_specs=[vmem] * 3,
         name="table",
-    )(beside_spots, forcing, mass, momentum)
+    )(forcing, mass, momentum)
 
 
 def spline(frac):
@@ -435,8 +435,8 @@
             spot = near[pl.ds(start + 8 * j, 8, stride=0), :]
             lanes = spot & 127
             chunk = lax.shift_right_logical(spot, 7)
-            for more in range(2):
-                here = jnp.minimum(first[j] + 2 * step + more, last[j])
+            for more in range(3):
+                here = jnp.minimum(first[j] + 3 * step + more, last[j])
                 base = address(here)
                 inside = chunk == here
                 for r in range(3):
@@ -444,8 +444,9 @@
                     sums[3 * j + r] = jnp.where(inside, from_lanes(tile, lanes), sums[3 * j + r])
         return tuple(sums)
 
-    trips = lax.shift_right_logical(span, 1) + 1
-    sums = lax.fori_loop(0, trips, trip, tuple(jnp.zeros((8, 128), f32) for _ in range(24)))
+    trips = lax.shift_right_logical(span * 171, 9) + 1
+    sums = trip(0, tuple(jnp.zeros((8, 128), f32) for _ in range(24)))
+    sums = lax.fori_loop(1, trips, trip, sums)
     for j in range(8):
         for r in range(3):
             samples[pl.ds(r * 64 + j, 8, stride=8), :] = sums[3 * j + r]
@@ -640,9 +641,7 @@
     forcing = lax.all_to_all(outgoing, "lon", 0, 0)
     near, ends, frac, counts, index, words = plan(cells, offsets, moves, slots)
     forcing, near = lax.optimization_barrier((forcing, near))
-    here = lax.axis_index("lon")
-    beside_spots = jnp.stack([(here + LON - 1) % LON, (here + 1) % LON])
-    table, first_edge, last_edge = node_table(beside_spots, forcing, grid_mass, grid_momentum)
+    table, first_edge, last_edge = node_table(forcing, grid_mass, grid_momentum)
     above = from_behind(last_edge, "lat", 1)
     below = from_behind(first_edge, "lat", -1)
     early = inner(ends, table, near, frac)

time: 88.6 us -> 82.7 us (0.933)
  Pallas kernels: 51.2 us -> 46 us
    pallas_call x1, Pallas kernels: 13.4 us -> 8.37 us  [inner(): pl.pallas_call(inner_kernel, out_shape=jax.ShapeDtypeStruct((8, 256, 128)...]
  transfers between devices with their start and end apart: 7 -> 7, of which waited for: 2 -> 2; matrix products, arithmetic and copies ran while one was open for 1% -> 0% of each run, Pallas kernels for 45% -> 41%
where the time goes in v5:
time: 82.7 us; the launch traced here: 82 us
  Pallas kernels  46 us (56%)
  starting transfers between devices  26.4 us (32%)
  local copies, waits for them, and re-layouts  4.13 us (5%)
  waiting for transfers between devices  3.61 us (4%)
  other arithmetic  1.04 us (1%)
    pallas_call x1, Pallas kernels, plan(): pl.pallas_call(plan_kernel, out_shape=[jax.ShapeDtypeStruct((VREGS, 8, 12...  20.6 us
    ppermute x4, starting transfers between devices, from_behind(): return lax.ppermute(block, axis, route)  16.7 us
    pallas_call x1, Pallas kernels, inner(): pl.pallas_call(inner_kernel, out_shape=jax.ShapeDtypeStruct((8, 256, 128)...  8.37 us
    pallas_call x1, Pallas kernels, transfer(): pl.pallas_call(transfer_kernel, out_shape=[jax.ShapeDtypeStruct((8, 256,...  6.35 us
    all_to_all x1, starting transfers between devices, shards(): forcing = lax.all_to_all(outgoing, 'lon', 0, 0)  5.8 us
    pallas_call x1, Pallas kernels, restore(): pl.pallas_call(restore_kernel, out_shape=jax.ShapeDtypeStruct((8, 4 * CAP...  4.93 us
    unnamed x13, local copies, waits for them, and re-layouts  4.13 us
    ppermute x2, starting transfers between devices, passed_along(): lax.ppermute(value, axis, [(i, (i + by) % count) for i in range(count)])  3.92 us
  transfers between devices with their start and end apart: 7, of which 2 were waited for; matrix products, arithmetic and copies ran while one was open for 0% of the time, Pallas kernels for 41%

profile of v5, /device:TPU:8, one launch (start us, length us, event | category | flops | bytes accessed | tf_op | source)
XLA Modules:
  0.0 82.0 jit_solution(2727104745291578323)
XLA Ops:
  0.6 0.0 copy-start.5
  0.6 2.7 %pack.1 = f32[16,8,1792]{2,1,0:T(8,128)} custom-call(f32[4,8,6144]{2,1,0:T(8,128)} %ocean.1, f32[128,384]{1,0:T(8,128)} %mass.3, f32[2,128,384]{2,1,0:T(8,128)} %momentum.3), custom_call_target="tpu_custom_call" | custom-call | tf_op jit(solution)/shard_map/pack/pallas_call | solution.py:339
  3.3 5.8 %all-to-all-start = ((f32[16,8,1792]{2,1,0:T(8,128)}), f32[16,8,1792]{2,1,0:T(8,128)}, u32[]{:S(2)}, u32[]{:S(2)}) async-start(f32[16,8,1792]{2,1,0:T(8,128)} %pack.1), calls=%async_computation | async-start | bytes 1835008 | tf_op jit(solution)/shard_map/all_to_all | solution.py:641
  9.1 0.0 copy-done.5
  9.2 0.0 copy-start.2
  9.2 0.9 %copy-done.2 = s32[32768]{0:T(1024)S(1)} copy-done((s32[32768]{0:T(1024)S(1)}, s32[32768]{0:T(1024)}, u32[]{:S(2)}) %copy-start.2) | copy-done | bytes 131096
  10.1 0.0 copy-start.3
  10.1 0.9 %copy-done.3 = s32[32768]{0:T(1024)S(1)} copy-done((s32[32768]{0:T(1024)S(1)}, s32[32768]{0:T(1024)}, u32[]{:S(2)}) %copy-start.3) | copy-done | bytes 131096
  11.0 0.0 copy-start.4
  11.0 0.9 %copy-done.4 = s32[32768]{0:T(1024)S(1)} copy-done((s32[32768]{0:T(1024)S(1)}, s32[32768]{0:T(1024)}, u32[]{:S(2)}) %copy-start.4) | copy-done | bytes 131096
  11.9 20.6 %plan.1 = (s32[32,8,128]{2,1,0:T(8,128)S(1)}, s32[4,128]{1,0:T(4,128)S(1)}, f32[2,32,8,128]{3,2,1,0:T(8,128)S(1)}, s32[4]{0:T(128)S(1)}, s32[2,9,32,8,128]{4,3,2...) custom-call(s32[256,128]{1,0:T(8,128)S(1)} %bitcast.15, f32[2,256,128]{2,1,0:T(8,128)S(1)} %bitcast.9, ...), custom_call_target="tpu_custom_call" | custom-call | flops 20000000 | bytes 8000000 | tf_op jit(solution)/shard_map/plan/pallas_call | solution.py:283
  32.5 0.0 all-to-all-done.forcing
  32.5 3.1 %table.1 = (f32[3072,128]{1,0:T(8,128)}, f32[24,128]{1,0:T(8,128)}, f32[24,128]{1,0:T(8,128)}) custom-call(f32[16,8,1792]{2,1,0:T(8,128)} %all-to-all-done.forcing, f32[128,384]{1,0:T(8,128)} %mass.3, f32[2,128,384]{2,1,0:T(8,128)} %momentum.3), custom_call_target="tpu_custom_call" | custom-call | tf_op jit(solution)/shard_map/table/pallas_call | solution.py:402
  35.6 5.5 %collective-permute-start = (f32[24,128]{1,0:T(8,128)}, f32[24,128]{1,0:T(8,128)S(1)}, u32[]{:S(2)}, u32[]{:S(2)}) collective-permute-start(f32[24,128]{1,0:T(8,128)} %get-tuple-element.23), channel_id=1, source_target_pairs={{0,16},{16,32},{32,48},{48,64},{64,80},{80,96},{96,112},{1,17},{17... | collective-permute-start | bytes 36872 | tf_op jit(solution)/shard_map/ppermute | solution.py:631
  41.1 2.9 %collective-permute-start.1 = (f32[24,128]{1,0:T(8,128)}, f32[24,128]{1,0:T(8,128)S(1)}, u32[]{:S(2)}, u32[]{:S(2)}) collective-permute-start(f32[24,128]{1,0:T(8,128)} %get-tuple-element.24), channel_id=1, source_target_pairs={{16,0},{32,16},{48,32},{64,48},{80,64},{96,80},{112,96},{17,1},{33... | collective-permute-start | bytes 36872 | tf_op jit(solution)/shard_map/ppermute | solution.py:631
  44.0 0.0 copy-start
  44.0 1.4 %copy-done = f32[3072,128]{1,0:T(8,128)S(1)} copy-done((f32[3072,128]{1,0:T(8,128)S(1)}, f32[3072,128]{1,0:T(8,128)}, u32[]{:S(2)}) %copy-start) | copy-done | bytes 1572888
  45.4 0.0 copy-start.1
  45.4 8.4 %inner.1.early = f32[8,256,128]{2,1,0:T(8,128)S(1)} custom-call(s32[4,128]{1,0:T(4,128)S(1)} %get-tuple-element.18.ends, f32[3072,128]{1,0:T(8,128)S(1)} %copy-done, s32[256,128]{1,0:T(8,128)S(1)} %bitcast.13, f32[2,256,128]{2,1,0:T(8,128)S(1)} %bitcast.11), custom_call_target="tpu_custom_call" | custom-call | flops 20000000 | bytes 8000000 | tf_op jit(solution)/shard_map/inner/pallas_call | solution.py:503
  53.8 0.0 collective-permute-done.above
  53.8 0.0 collective-permute-done.1.below
  53.9 0.0 copy-done.1
  53.9 6.3 %transfer.1 = (f32[8,256,128]{2,1,0:T(8,128)S(1)}, f32[8,8192]{1,0:T(8,128)S(1)}, f32[8,8192]{1,0:T(8,128)S(1)}, f32[8,8192]{1,0:T(8,128)S(1)}, f32[8,8192]{1,0:T(8,128)S(1)}) custom-call(s32[4,128]{1,0:T(4,128)S(1)} %get-tuple-element.18.ends, s32[4]{0:T(128)S(1)} %get-tuple-element.19.counts, f32[3072,128]{1,0:T(8,128)S(1)} %copy-done.1, ...), custom_call_target="tpu_custom_call" | custom-call | flops 10000000 | bytes 8000000 | tf_op jit(solution)/shard_map/transfer/pallas_call | solution.py:576
  60.2 4.6 %collective-permute-start.2 = (f32[8,8192]{1,0:T(8,128)S(1)}, f32[8,8192]{1,0:T(8,128)S(1)}, u32[]{:S(2)}, u32[]{:S(2)}) collective-permute-start(f32[8,8192]{1,0:T(8,128)S(1)} %get-tuple-element.30), channel_id=1, source_target_pairs={{0,16},{16,32},{32,48},{48,64},{64,80},{80,96},{96,112},{1,17},{17... | collective-permute-start | bytes 786440 | tf_op jit(solution)/shard_map/ppermute | solution.py:631
  64.8 3.7 %collective-permute-start.3 = (f32[8,8192]{1,0:T(8,128)S(1)}, f32[8,8192]{1,0:T(8,128)S(1)}, u32[]{:S(2)}, u32[]{:S(2)}) collective-permute-start(f32[8,8192]{1,0:T(8,128)S(1)} %get-tuple-element.31), channel_id=1, source_target_pairs={{16,0},{32,16},{48,32},{64,48},{80,64},{96,80},{112,96},{17,1},{33... | collective-permute-start | bytes 786440 | tf_op jit(solution)/shard_map/ppermute | solution.py:631
  68.5 0.1 collective-permute-start.4
  68.6 3.8 %collective-permute-start.5 = (f32[8,8192]{1,0:T(8,128)S(1)}, f32[8,8192]{1,0:T(8,128)S(1)}, u32[]{:S(2)}, u32[]{:S(2)}) collective-permute-start(f32[8,8192]{1,0:T(8,128)S(1)} %get-tuple-element.33), channel_id=1, source_target_pairs={{0,15},{1,0},{2,1},{3,2},{4,3},{5,4},{6,5},{7,6},{8,7},{9,8},{10,9... | collective-permute-start | bytes 786440 | tf_op jit(solution)/shard_map/ppermute | solution.py:636
  72.4 4.9 %restore.1 = f32[8,32768]{1,0:T(8,128)} custom-call(f32[8,256,128]{2,1,0:T(8,128)S(1)} %get-tuple-element.29.state, f32[2,256,128]{2,1,0:T(8,128)S(1)} %bitcast.10, s32[2,9,32,8,128]{4,3,2,1,0:T(8,128)S(1)} %get-tuple-element.27.index, s32[2,2,32,8,128]{4,3,2,1,0:T(8,128)S(1)} %get-tuple-element.28.words), custom_call_target="tpu_custom_call" | custom-call | flops 10000000 | bytes 4000000 | tf_op jit(solution)/shard_map/restore/pallas_call | solution.py:616
  77.3 1.6 %collective-permute-done.2 = f32[8,8192]{1,0:T(8,128)S(1)} collective-permute-done((f32[8,8192]{1,0:T(8,128)S(1)}, f32[8,8192]{1,0:T(8,128)S(1)}, u32[]{:S(2)}, u32[]{:S(2)}) %collective-permute-start.2) | collective-permute-done | bytes 262176 | tf_op jit(solution)/shard_map/ppermute | solution.py:631
  78.9 2.0 %collective-permute-done.3 = f32[8,8192]{1,0:T(8,128)S(1)} collective-permute-done((f32[8,8192]{1,0:T(8,128)S(1)}, f32[8,8192]{1,0:T(8,128)S(1)}, u32[]{:S(2)}, u32[]{:S(2)}) %collective-permute-start.3) | collective-permute-done | bytes 262176 | tf_op jit(solution)/shard_map/ppermute | solution.py:631
  80.9 0.0 collective-permute-done.4
  80.9 0.0 collective-permute-done.5
  80.9 1.0 %pad_maximum_fusion = f32[8,32768]{1,0:T(8,128)} fusion(f32[8,8192]{1,0:T(8,128)S(1)} %collective-permute-done.5, f32[8,8192]{1,0:T(8,128)S(1)} %collective-permute-done.4, f32[8,8192]{1,0:T(8,128)S(1)} %collective-permute-done.3, f32[8,8192]{1,0:T(8,128)S(1)} %collective-permute-done.2), kind=kLoop, calls=%fused_computation | loop fusion | flops 786432 | bytes 2097152 | tf_op jit(solution)/shard_map/concatenate | solution.py:656
  (1 shorter events, 0.0 us)
Async XLA Ops:
  0.6 8.5 %copy-start.5 = (f32[2,32768]{1,0:T(2,128)S(1)}, f32[2,32768]{1,0:T(2,128)}, u32[]{:S(2)}) copy-start(f32[2,32768]{1,0:T(2,128)} %param.11) | copy-start | bytes 786436
  3.3 29.2 %all-to-all-start = ((f32[16,8,1792]{2,1,0:T(8,128)}), f32[16,8,1792]{2,1,0:T(8,128)}, u32[]{:S(2)}, u32[]{:S(2)}) async-start(f32[16,8,1792]{2,1,0:T(8,128)} %pack.1), calls=%async_computation | async-start | bytes 1835008 | tf_op jit(solution)/shard_map/all_to_all | solution.py:641
  9.2 0.9 %copy-start.2 = (s32[32768]{0:T(1024)S(1)}, s32[32768]{0:T(1024)}, u32[]{:S(2)}) copy-start(s32[32768]{0:T(1024)} %param.10) | copy-start | bytes 393220
  10.1 0.9 %copy-start.3 = (s32[32768]{0:T(1024)S(1)}, s32[32768]{0:T(1024)}, u32[]{:S(2)}) copy-start(s32[32768]{0:T(1024)} %param.12) | copy-start | bytes 393220
  11.0 0.9 %copy-start.4 = (s32[32768]{0:T(1024)S(1)}, s32[32768]{0:T(1024)}, u32[]{:S(2)}) copy-start(s32[32768]{0:T(1024)} %param.13) | copy-start | bytes 393220
  35.6 18.2 %collective-permute-start = (f32[24,128]{1,0:T(8,128)}, f32[24,128]{1,0:T(8,128)S(1)}, u32[]{:S(2)}, u32[]{:S(2)}) collective-permute-start(f32[24,128]{1,0:T(8,128)} %get-tuple-element.23), channel_id=1, source_target_pairs={{0,16},{16,32},{32,48},{48,64},{64,80},{80,96},{96,112},{1,17},{17... | collective-permute-start | bytes 36872 | tf_op jit(solution)/shard_map/ppermute | solution.py:631
  41.1 12.7 %collective-permute-start.1 = (f32[24,128]{1,0:T(8,128)}, f32[24,128]{1,0:T(8,128)S(1)}, u32[]{:S(2)}, u32[]{:S(2)}) collective-permute-start(f32[24,128]{1,0:T(8,128)} %get-tuple-element.24), channel_id=1, source_target_pairs={{16,0},{32,16},{48,32},{64,48},{80,64},{96,80},{112,96},{17,1},{33... | collective-permute-start | bytes 36872 | tf_op jit(solution)/shard_map/ppermute | solution.py:631
  44.0 1.4 %copy-start = (f32[3072,128]{1,0:T(8,128)S(1)}, f32[3072,128]{1,0:T(8,128)}, u32[]{:S(2)}) copy-start(f32[3072,128]{1,0:T(8,128)} %get-tuple-element.22.table) | copy-start | bytes 4718596
  45.4 8.4 %copy-start.1 = (f32[3072,128]{1,0:T(8,128)S(1)}, f32[3072,128]{1,0:T(8,128)}, u32[]{:S(2)}) copy-start(f32[3072,128]{1,0:T(8,128)} %get-tuple-element.22.table) | copy-start | bytes 4718596
  60.2 18.7 %collective-permute-start.2 = (f32[8,8192]{1,0:T(8,128)S(1)}, f32[8,8192]{1,0:T(8,128)S(1)}, u32[]{:S(2)}, u32[]{:S(2)}) collective-permute-start(f32[8,8192]{1,0:T(8,128)S(1)} %get-tuple-element.30), channel_id=1, source_target_pairs={{0,16},{16,32},{32,48},{48,64},{64,80},{80,96},{96,112},{1,17},{17... | collective-permute-start | bytes 786440 | tf_op jit(solution)/shard_map/ppermute | solution.py:631
  64.8 16.1 %collective-permute-start.3 = (f32[8,8192]{1,0:T(8,128)S(1)}, f32[8,8192]{1,0:T(8,128)S(1)}, u32[]{:S(2)}, u32[]{:S(2)}) collective-permute-start(f32[8,8192]{1,0:T(8,128)S(1)} %get-tuple-element.31), channel_id=1, source_target_pairs={{16,0},{32,16},{48,32},{64,48},{80,64},{96,80},{112,96},{17,1},{33... | collective-permute-start | bytes 786440 | tf_op jit(solution)/shard_map/ppermute | solution.py:631
  68.5 12.5 %collective-permute-start.4 = (f32[8,8192]{1,0:T(8,128)S(1)}, f32[8,8192]{1,0:T(8,128)S(1)}, u32[]{:S(2)}, u32[]{:S(2)}) collective-permute-start(f32[8,8192]{1,0:T(8,128)S(1)} %get-tuple-element.32), channel_id=1, source_target_pairs={{0,1},{1,2},{2,3},{3,4},{4,5},{5,6},{6,7},{7,8},{8,9},{9,10},{10,1... | collective-permute-start | bytes 786440 | tf_op jit(solution)/shard_map/ppermute | solution.py:636
  68.6 12.4 %collective-permute-start.5 = (f32[8,8192]{1,0:T(8,128)S(1)}, f32[8,8192]{1,0:T(8,128)S(1)}, u32[]{:S(2)}, u32[]{:S(2)}) collective-permute-start(f32[8,8192]{1,0:T(8,128)S(1)} %get-tuple-element.33), channel_id=1, source_target_pairs={{0,15},{1,0},{2,1},{3,2},{4,3},{5,4},{6,5},{7,6},{8,7},{9,8},{10,9... | collective-permute-start | bytes 786440 | tf_op jit(solution)/shard_map/ppermute | solution.py:636

commit v6 on v5

--- a/solution.py
+++ b/solution.py
@@ -203,13 +203,15 @@
 
 
 def plan_kernel(
-    cells, offsets, moves, slots,
+    packed, offsets,
     near_out, ends_out, frac_out, counts_out,
-    index_out, words_out,
-    tags, chunks,
+    index_out, words_out, tags,
+    moves, chunks,
 ):
     lane = lane_ids()
     sub = sublane_ids()
+    moves[...] = lax.shift_right_logical(packed[...], 29)
+    slots = lax.shift_right_logical(packed[...], 16) & (CAP - 1)
     stay = jnp.where(moves[...] == 0, 1.0, 0.0)
     before = jnp.where(
         lax.broadcasted_iota(i32, (128, 128), 0) < lax.broadcasted_iota(i32, (128, 128), 1), 1.0, 0.0
@@ -231,9 +233,9 @@
     for k in range(1, 4):
         hole = hole + jnp.where(rank >= k * CAP - filled, counts[k], 0)
         filled = filled + counts[k]
-    target = jnp.where(moves[...] > 0, (moves[...] - 1) * CAP + slots[...], hole)
+    target = jnp.where(moves[...] > 0, (moves[...] - 1) * CAP + slots, hole)
     number = lax.broadcasted_iota(i32, (256, 128), 0) * 128 + lax.broadcasted_iota(i32, (256, 128), 1)
-    cell = cells[...]
+    cell = packed[...] & 65535
     row = (cell.astype(f32) * (1.0 / COLS)).astype(i32)
     row = row - jnp.where(row * COLS > cell, 1, 0)
     row = row + jnp.where((row + 1) * COLS <= cell, 1, 0)
@@ -259,25 +261,23 @@
         ends_out[half : half + 1, :] = jnp.min(turned, axis=0, keepdims=True).astype(i32)
         ends_out[half + 2 : half + 3, :] = jnp.max(turned, axis=0, keepdims=True).astype(i32)
 
-    def one(which, carry):
-        keys = [
-            (lax.shift_right_logical(tags[v], jnp.where(which == 0, 15, 0)) & 32767).astype(f32)
-            for v in range(VREGS)
-        ]
-
-        def record(t, v, index):
-            index_out[which, t, v] = index
-
-        _, words, sub_words = sort_network(keys, (), record)
-        for v in range(VREGS):
-            words_out[which, 0, v] = words[v]
-            words_out[which, 1, v] = sub_words[v]
-        return carry
-
-    lax.fori_loop(0, 2, one, 0)
+    plan_moves(lambda v: lax.shift_right_logical(tags[v], 15), index_out, words_out)
+
+
+def plan_moves(rank, index_out, words_out):
+    keys = [rank(v).astype(f32) for v in range(VREGS)]
+
+    def record(t, v, index):
+        index_out[t, v] = index
+
+    _, words, sub_words = sort_network(keys, (), record)
+    for v in range(VREGS):
+        words_out[0, v] = words[v]
+        words_out[1, v] = sub_words[v]
 
 
 def plan(cells, offsets, moves, slots):
+    packed = cells | lax.shift_left(slots, 16) | lax.shift_left(moves, 29)
     vmem = pl.BlockSpec(memory_space=pltpu.VMEM)
     smem = pl.BlockSpec(memory_space=pltpu.SMEM)
     return pl.pallas_call(
@@ -287,16 +287,17 @@
             jax.ShapeDtypeStruct((4, 128), i32),
             jax.ShapeDtypeStruct((2, VREGS, 8, 128), f32),
             jax.ShapeDtypeStruct((4,), i32),
-            jax.ShapeDtypeStruct((2, 9, VREGS, 8, 128), i32),
-            jax.ShapeDtypeStruct((2, 2, VREGS, 8, 128), i32),
+            jax.ShapeDtypeStruct((9, VREGS, 8, 128), i32),
+            jax.ShapeDtypeStruct((2, VREGS, 8, 128), i32),
+            jax.ShapeDtypeStruct((VREGS, 8, 128), i32),
         ],
-        in_specs=[vmem] * 4,
-        out_specs=[vmem, vmem, vmem, smem, vmem, vmem],
-        scratch_shapes=[pltpu.VMEM((VREGS, 8, 128), i32), pltpu.VMEM((256, 128), f32)],
+        in_specs=[vmem] * 2,
+        out_specs=[vmem, vmem, vmem, smem, vmem, vmem, vmem],
+        scratch_shapes=[pltpu.VMEM((256, 128), i32), pltpu.VMEM((256, 128), f32)],
         compiler_params=pltpu.CompilerParams(vmem_limit_bytes=32 << 20),
         cost_estimate=pl.CostEstimate(flops=20_000_000, bytes_accessed=8_000_000, transcendentals=0),
         name="plan",
-    )(cells.reshape(256, 128), offsets.reshape(2, 256, 128), moves.reshape(256, 128), slots.reshape(256, 128))
+    )(packed.reshape(256, 128), offsets.reshape(2, 256, 128))
 
 
 def pack_kernel(ocean, mass, momentum, out):
@@ -408,6 +409,7 @@
         ],
         in_specs=[vmem] * 3,
         out_specs=[vmem] * 3,
+        compiler_params=pltpu.CompilerParams(vmem_limit_bytes=40 << 20),
         name="table",
     )(forcing, mass, momentum)
 
@@ -562,7 +564,7 @@
     apply_network(
         8,
         lambda c, v: state[c, 8 * v : 8 * v + 8, :],
-        buffer, index.at[0], words.at[0, 0], words.at[0, 1], finish,
+        buffer, index, words.at[0], words.at[1], finish,
     )
     for k, out in enumerate((north, south, east, west)):
         for j in range(64):
@@ -594,7 +596,9 @@
     )
 
 
-def restore_kernel(state, offsets, index, words, out, columns, buffer):
+def restore_kernel(state, offsets, tags, out, columns, buffer, index, words):
+    plan_moves(lambda v: tags[v] & 32767, index, words)
+
     def finish(v, moved):
         for c in range(2):
             frac = offsets[c, pl.ds(v, 8, stride=32), :]
@@ -605,24 +609,29 @@
     apply_network(
         6,
         lambda c, v: state[c + 2, 8 * v : 8 * v + 8, :],
-        buffer, index.at[1], words.at[1, 0], words.at[1, 1], finish,
+        buffer, index, words.at[0], words.at[1], finish,
     )
     for j in range(256):
         out[:, 128 * j : 128 * j + 128] = columns[8 * j : 8 * j + 8, :]
 
 
-def restore(state, offsets, index, words):
+def restore(state, offsets, tags):
     vmem = pl.BlockSpec(memory_space=pltpu.VMEM)
     return pl.pallas_call(
         restore_kernel,
         out_shape=jax.ShapeDtypeStruct((8, 4 * CAP), f32),
-        in_specs=[vmem] * 4,
+        in_specs=[vmem] * 3,
         out_specs=vmem,
-        scratch_shapes=[pltpu.VMEM((2048, 128), f32), pltpu.VMEM((6, VREGS, 8, 128), f32)],
+        scratch_shapes=[
+            pltpu.VMEM((2048, 128), f32),
+            pltpu.VMEM((6, VREGS, 8, 128), f32),
+            pltpu.VMEM((9, VREGS, 8, 128), i32),
+            pltpu.VMEM((2, VREGS, 8, 128), i32),
+        ],
         compiler_params=pltpu.CompilerParams(vmem_limit_bytes=32 << 20),
         cost_estimate=pl.CostEstimate(flops=10_000_000, bytes_accessed=4_000_000, transcendentals=0),
         name="restore",
-    )(state, offsets.reshape(2, 256, 128), index, words)
+    )(state, offsets.reshape(2, 256, 128), tags)
 
 
 def from_behind(block, axis, distance):
@@ -639,7 +648,7 @@
 def shards(ocean, grid_mass, grid_momentum, cells, offsets, moves, slots):
     outgoing = pack(ocean, grid_mass, grid_momentum)
     forcing = lax.all_to_all(outgoing, "lon", 0, 0)
-    near, ends, frac, counts, index, words = plan(cells, offsets, moves, slots)
+    near, ends, frac, counts, index, words, tags = plan(cells, offsets, moves, slots)
     forcing, near = lax.optimization_barrier((forcing, near))
     table, first_edge, last_edge = node_table(forcing, grid_mass, grid_momentum)
     above = from_behind(last_edge, "lat", 1)
@@ -652,7 +661,7 @@
     south = from_behind(south, "lat", -1)
     east = passed_along(east, "lon", 1)
     west = passed_along(west, "lon", -1)
-    parcels = restore(state, offsets, index, words)
+    parcels = restore(state, offsets, tags)
     return (parcels, jnp.concatenate([north, south, east, west], axis=1))
 
 

time: 82.7 us -> 72.8 us (0.88)
  waiting for transfers between devices: 3.61 us -> 0.13 us
  local copies, waits for them, and re-layouts: 4.13 us -> 0.75 us
  Pallas kernels: 46 us -> 43.1 us
    pallas_call x1, Pallas kernels: 20.6 us -> 14.1 us  [plan(): pl.pallas_call(plan_kernel, out_shape=[jax.ShapeDtypeStruct((VREGS, 8, 12...]
    pallas_call x1, Pallas kernels: 4.93 us -> 11 us  [restore(): pl.pallas_call(restore_kernel, out_shape=jax.ShapeDtypeStruct((8, 4 * CAP...]
    ppermute x4, waiting for transfers between devices: 3.6 us -> 0.01 us  [from_behind(): return lax.ppermute(block, axis, route)]
    unnamed x13 -> x17, local copies, waits for them, and re-layouts: 4.13 us -> 0.75 us
    pallas_call x1, Pallas kernels: 3.05 us -> 0.52 us  [node_table(): pl.pallas_call(table_kernel, out_shape=[jax.ShapeDtypeStruct((8 * PLANE,...]
  transfers between devices with their start and end apart: 7 -> 7, of which waited for: 2 -> 1; matrix products, arithmetic and copies ran while one was open for 0% -> 0% of each run, Pallas kernels for 41% -> 46%
where the time goes in v6:
time: 72.8 us; the launch traced here: 72.5 us
  Pallas kernels  43.1 us (59%)
  starting transfers between devices  26.6 us (37%)
  other arithmetic  1.06 us (1%)
  between operations  0.83 us (1%)
  local copies, waits for them, and re-layouts  0.75 us (1%)
    ppermute x4, starting transfers between devices, from_behind(): return lax.ppermute(block, axis, route)  16.8 us
    pallas_call x1, Pallas kernels, plan(): pl.pallas_call(plan_kernel, out_shape=[jax.ShapeDtypeStruct((VREGS, 8, 12...  14.1 us
    pallas_call x1, Pallas kernels, restore(): pl.pallas_call(restore_kernel, out_shape=jax.ShapeDtypeStruct((8, 4 * CAP...  11 us
    pallas_call x1, Pallas kernels, inner(): pl.pallas_call(inner_kernel, out_shape=jax.ShapeDtypeStruct((8, 256, 128)...  8.38 us
    pallas_call x1, Pallas kernels, transfer(): pl.pallas_call(transfer_kernel, out_shape=[jax.ShapeDtypeStruct((8, 256,...  6.35 us
    all_to_all x1, starting transfers between devices, shards(): forcing = lax.all_to_all(outgoing, 'lon', 0, 0)  5.9 us
    ppermute x2, starting transfers between devices, passed_along(): lax.ppermute(value, axis, [(i, (i + by) % count) for i in range(count)])  3.92 us
    pallas_call x1, Pallas kernels, pack(): pl.pallas_call(pack_kernel, out_shape=jax.ShapeDtypeStruct((LON, 8, 4 * C...  2.67 us
  transfers between devices with their start and end apart: 7, of which 1 were waited for; matrix products, arithmetic and copies ran while one was open for 0% of the time, Pallas kernels for 46%

profile of v6, /device:TPU:8, one launch (start us, length us, event | category | flops | bytes accessed | tf_op | source)
XLA Modules:
  0.0 72.5 jit_solution(10588189450609436997)
XLA Ops:
  0.6 0.0 copy-start.4
  0.6 2.7 %pack.1 = f32[16,8,1792]{2,1,0:T(8,128)} custom-call(f32[4,8,6144]{2,1,0:T(8,128)} %ocean.1, f32[128,384]{1,0:T(8,128)} %mass.3, f32[2,128,384]{2,1,0:T(8,128)} %momentum.3), custom_call_target="tpu_custom_call" | custom-call | tf_op jit(solution)/shard_map/pack/pallas_call | solution.py:340
  3.3 0.0 copy-start.5
  3.3 0.0 copy-start.6
  3.3 0.0 copy-start.7
  3.3 0.0 copy-start
  3.3 0.0 copy-start.1
  3.3 5.9 %all-to-all-start = ((f32[16,8,1792]{2,1,0:T(8,128)}), f32[16,8,1792]{2,1,0:T(8,128)S(1)}, u32[]{:S(2)}, u32[]{:S(2)}) async-start(f32[16,8,1792]{2,1,0:T(8,128)} %pack.1), calls=%async_computation | async-start | bytes 1835008 | tf_op jit(solution)/shard_map/all_to_all | solution.py:650
  9.2 0.0 copy-done.4
  9.3 0.0 copy-done.5
  9.3 0.0 copy-done.6
  9.3 0.0 copy-done.7
  9.3 14.1 %plan.1 = (s32[32,8,128]{2,1,0:T(8,128)S(1)}, s32[4,128]{1,0:T(4,128)S(1)}, f32[2,32,8,128]{3,2,1,0:T(8,128)S(1)}, s32[4]{0:T(128)S(1)}, s32[9,32,8,128]{3,2,1,0...) custom-call(s32[256,128]{1,0:T(8,128)S(1)} %or_bitcast_fusion.packed, f32[2,256,128]{2,1,0:T(8,128)S(1)} %bitcast.8), custom_call_target="tpu_custom_call" | custom-call | flops 20000000 | bytes 8000000 | tf_op jit(solution)/shard_map/plan/pallas_call | solution.py:283
  23.5 0.0 copy-start.2
  23.5 0.7 copy-done.2
  24.2 0.1 all-to-all-done.forcing
  24.3 0.0 copy-done
  24.3 0.0 copy-done.1
  24.3 0.5 table.1
  24.8 0.0 copy-start.3
  24.9 5.6 %collective-permute-start = (f32[24,128]{1,0:T(8,128)S(1)}, f32[24,128]{1,0:T(8,128)S(1)}, u32[]{:S(2)}, u32[]{:S(2)}) collective-permute-start(f32[24,128]{1,0:T(8,128)S(1)} %get-tuple-element.24), channel_id=1, source_target_pairs={{0,16},{16,32},{32,48},{48,64},{64,80},{80,96},{96,112},{1,17},{17... | collective-permute-start | bytes 36872 | tf_op jit(solution)/shard_map/ppermute | solution.py:640
  30.5 2.9 %collective-permute-start.1 = (f32[24,128]{1,0:T(8,128)S(1)}, f32[24,128]{1,0:T(8,128)S(1)}, u32[]{:S(2)}, u32[]{:S(2)}) collective-permute-start(f32[24,128]{1,0:T(8,128)S(1)} %get-tuple-element.25), channel_id=1, source_target_pairs={{16,0},{32,16},{48,32},{64,48},{80,64},{96,80},{112,96},{17,1},{33... | collective-permute-start | bytes 36872 | tf_op jit(solution)/shard_map/ppermute | solution.py:640
  33.4 8.4 %inner.1.early = f32[8,256,128]{2,1,0:T(8,128)S(1)} custom-call(s32[4,128]{1,0:T(4,128)S(1)} %get-tuple-element.19.ends, f32[3072,128]{1,0:T(8,128)S(1)} %get-tuple-element.23.table, s32[256,128]{1,0:T(8,128)S(1)} %bitcast.12, f32[2,256,128]{2,1,0:T(8,128)S(1)} %bitcast.10), custom_call_target="tpu_custom_call" | custom-call | flops 20000000 | bytes 8000000 | tf_op jit(solution)/shard_map/inner/pallas_call | solution.py:505
  41.8 0.0 collective-permute-done.above
  41.8 0.0 collective-permute-done.1.below
  41.8 0.0 copy-done.3
  41.8 6.4 %transfer.1 = (f32[8,256,128]{2,1,0:T(8,128)S(1)}, f32[8,8192]{1,0:T(8,128)S(1)}, f32[8,8192]{1,0:T(8,128)S(1)}, f32[8,8192]{1,0:T(8,128)S(1)}, f32[8,8192]{1,0:T(8,128)S(1)}) custom-call(s32[4,128]{1,0:T(4,128)S(1)} %get-tuple-element.19.ends, s32[4]{0:T(128)S(1)} %get-tuple-element.20.counts, f32[3072,128]{1,0:T(8,128)S(1)} %get-tuple-element.23.table, ...), custom_call_target="tpu_custom_call" | custom-call | flops 10000000 | bytes 8000000 | tf_op jit(solution)/shard_map/transfer/pallas_call | solution.py:578
  48.2 4.6 %collective-permute-start.2 = (f32[8,8192]{1,0:T(8,128)S(1)}, f32[8,8192]{1,0:T(8,128)S(1)}, u32[]{:S(2)}, u32[]{:S(2)}) collective-permute-start(f32[8,8192]{1,0:T(8,128)S(1)} %get-tuple-element.32), channel_id=1, source_target_pairs={{0,16},{16,32},{32,48},{48,64},{64,80},{80,96},{96,112},{1,17},{17... | collective-permute-start | bytes 786440 | tf_op jit(solution)/shard_map/ppermute | solution.py:640
  52.8 3.7 %collective-permute-start.3 = (f32[8,8192]{1,0:T(8,128)S(1)}, f32[8,8192]{1,0:T(8,128)S(1)}, u32[]{:S(2)}, u32[]{:S(2)}) collective-permute-start(f32[8,8192]{1,0:T(8,128)S(1)} %get-tuple-element.33), channel_id=1, source_target_pairs={{16,0},{32,16},{48,32},{64,48},{80,64},{96,80},{112,96},{17,1},{33... | collective-permute-start | bytes 786440 | tf_op jit(solution)/shard_map/ppermute | solution.py:640
  56.5 0.1 collective-permute-start.4
  56.6 3.8 %collective-permute-start.5 = (f32[8,8192]{1,0:T(8,128)S(1)}, f32[8,8192]{1,0:T(8,128)S(1)}, u32[]{:S(2)}, u32[]{:S(2)}) collective-permute-start(f32[8,8192]{1,0:T(8,128)S(1)} %get-tuple-element.35), channel_id=1, source_target_pairs={{0,15},{1,0},{2,1},{3,2},{4,3},{5,4},{6,5},{7,6},{8,7},{9,8},{10,9... | collective-permute-start | bytes 786440 | tf_op jit(solution)/shard_map/ppermute | solution.py:645
  60.4 11.0 %restore.1 = f32[8,32768]{1,0:T(8,128)} custom-call(f32[8,256,128]{2,1,0:T(8,128)S(1)} %get-tuple-element.30.state, f32[2,256,128]{2,1,0:T(8,128)S(1)} %bitcast.9, s32[32,8,128]{2,1,0:T(8,128)S(1)} %get-tuple-element.31.tags), custom_call_target="tpu_custom_call" | custom-call | flops 10000000 | bytes 4000000 | tf_op jit(solution)/shard_map/restore/pallas_call | solution.py:620
  71.4 0.0 collective-permute-done.2
  71.4 0.0 collective-permute-done.3
  71.4 0.0 collective-permute-done.4
  71.4 0.0 collective-permute-done.5
  71.4 1.0 %pad_maximum_fusion = f32[8,32768]{1,0:T(8,128)} fusion(f32[8,8192]{1,0:T(8,128)S(1)} %collective-permute-done.5, f32[8,8192]{1,0:T(8,128)S(1)} %collective-permute-done.4, f32[8,8192]{1,0:T(8,128)S(1)} %collective-permute-done.3, f32[8,8192]{1,0:T(8,128)S(1)} %collective-permute-done.2), kind=kLoop, calls=%fused_computation | loop fusion | flops 786432 | bytes 2097152 | tf_op jit(solution)/shard_map/concatenate | solution.py:665
  (2 shorter events, 0.0 us)
Async XLA Ops:
  0.6 8.6 %copy-start.4 = (f32[2,32768]{1,0:T(2,128)S(1)}, f32[2,32768]{1,0:T(2,128)}, u32[]{:S(2)}) copy-start(f32[2,32768]{1,0:T(2,128)} %param.11) | copy-start | bytes 786436
  3.3 6.0 %copy-start.5 = (s32[32768]{0:T(1024)S(1)}, s32[32768]{0:T(1024)}, u32[]{:S(2)}) copy-start(s32[32768]{0:T(1024)} %param.12) | copy-start | bytes 393220
  3.3 6.0 %copy-start.6 = (s32[32768]{0:T(1024)S(1)}, s32[32768]{0:T(1024)}, u32[]{:S(2)}) copy-start(s32[32768]{0:T(1024)} %param.10) | copy-start | bytes 393220
  3.3 6.0 %copy-start.7 = (s32[32768]{0:T(1024)S(1)}, s32[32768]{0:T(1024)}, u32[]{:S(2)}) copy-start(s32[32768]{0:T(1024)} %param.13) | copy-start | bytes 393220
  3.3 21.0 %copy-start = (f32[2,128,384]{2,1,0:T(8,128)S(1)}, f32[2,128,384]{2,1,0:T(8,128)}, u32[]{:S(2)}) copy-start(f32[2,128,384]{2,1,0:T(8,128)} %momentum.3) | copy-start | bytes 1179652
  3.3 21.0 %copy-start.1 = (f32[128,384]{1,0:T(8,128)S(1)}, f32[128,384]{1,0:T(8,128)}, u32[]{:S(2)}) copy-start(f32[128,384]{1,0:T(8,128)} %mass.3) | copy-start | bytes 589828
  3.3 21.0 %all-to-all-start = ((f32[16,8,1792]{2,1,0:T(8,128)}), f32[16,8,1792]{2,1,0:T(8,128)S(1)}, u32[]{:S(2)}, u32[]{:S(2)}) async-start(f32[16,8,1792]{2,1,0:T(8,128)} %pack.1), calls=%async_computation | async-start | bytes 1835008 | tf_op jit(solution)/shard_map/all_to_all | solution.py:650
  23.5 0.7 copy-start.2
  24.8 17.0 %copy-start.3 = (s32[2,32,8,128]{3,2,1,0:T(8,128)S(1)}, s32[2,32,8,128]{3,2,1,0:T(8,128)}, u32[]{:S(2)}) copy-start(s32[2,32,8,128]{3,2,1,0:T(8,128)} %copy-done.2) | copy-start | bytes 786436
  24.9 17.0 %collective-permute-start = (f32[24,128]{1,0:T(8,128)S(1)}, f32[24,128]{1,0:T(8,128)S(1)}, u32[]{:S(2)}, u32[]{:S(2)}) collective-permute-start(f32[24,128]{1,0:T(8,128)S(1)} %get-tuple-element.24), channel_id=1, source_target_pairs={{0,16},{16,32},{32,48},{48,64},{64,80},{80,96},{96,112},{1,17},{17... | collective-permute-start | bytes 36872 | tf_op jit(solution)/shard_map/ppermute | solution.py:640
  30.5 11.3 %collective-permute-start.1 = (f32[24,128]{1,0:T(8,128)S(1)}, f32[24,128]{1,0:T(8,128)S(1)}, u32[]{:S(2)}, u32[]{:S(2)}) collective-permute-start(f32[24,128]{1,0:T(8,128)S(1)} %get-tuple-element.25), channel_id=1, source_target_pairs={{16,0},{32,16},{48,32},{64,48},{80,64},{96,80},{112,96},{17,1},{33... | collective-permute-start | bytes 36872 | tf_op jit(solution)/shard_map/ppermute | solution.py:640
  48.2 23.2 %collective-permute-start.2 = (f32[8,8192]{1,0:T(8,128)S(1)}, f32[8,8192]{1,0:T(8,128)S(1)}, u32[]{:S(2)}, u32[]{:S(2)}) collective-permute-start(f32[8,8192]{1,0:T(8,128)S(1)} %get-tuple-element.32), channel_id=1, source_target_pairs={{0,16},{16,32},{32,48},{48,64},{64,80},{80,96},{96,112},{1,17},{17... | collective-permute-start | bytes 786440 | tf_op jit(solution)/shard_map/ppermute | solution.py:640
  52.8 18.6 %collective-permute-start.3 = (f32[8,8192]{1,0:T(8,128)S(1)}, f32[8,8192]{1,0:T(8,128)S(1)}, u32[]{:S(2)}, u32[]{:S(2)}) collective-permute-start(f32[8,8192]{1,0:T(8,128)S(1)} %get-tuple-element.33), channel_id=1, source_target_pairs={{16,0},{32,16},{48,32},{64,48},{80,64},{96,80},{112,96},{17,1},{33... | collective-permute-start | bytes 786440 | tf_op jit(solution)/shard_map/ppermute | solution.py:640
  56.5 14.9 %collective-permute-start.4 = (f32[8,8192]{1,0:T(8,128)S(1)}, f32[8,8192]{1,0:T(8,128)S(1)}, u32[]{:S(2)}, u32[]{:S(2)}) collective-permute-start(f32[8,8192]{1,0:T(8,128)S(1)} %get-tuple-element.34), channel_id=1, source_target_pairs={{0,1},{1,2},{2,3},{3,4},{4,5},{5,6},{6,7},{7,8},{8,9},{9,10},{10,1... | collective-permute-start | bytes 786440 | tf_op jit(solution)/shard_map/ppermute | solution.py:645
  56.6 14.9 %collective-permute-start.5 = (f32[8,8192]{1,0:T(8,128)S(1)}, f32[8,8192]{1,0:T(8,128)S(1)}, u32[]{:S(2)}, u32[]{:S(2)}) collective-permute-start(f32[8,8192]{1,0:T(8,128)S(1)} %get-tuple-element.35), channel_id=1, source_target_pairs={{0,15},{1,0},{2,1},{3,2},{4,3},{5,4},{6,5},{7,6},{8,7},{9,8},{10,9... | collective-permute-start | bytes 786440 | tf_op jit(solution)/shard_map/ppermute | solution.py:645

commit v7 on v6

--- a/solution.py
+++ b/solution.py
@@ -205,7 +205,7 @@
 def plan_kernel(
     packed, offsets,
     near_out, ends_out, frac_out, counts_out,
-    index_out, words_out, tags,
+    index_out, tags,
     moves, chunks,
 ):
     lane = lane_ids()
@@ -261,10 +261,10 @@
         ends_out[half : half + 1, :] = jnp.min(turned, axis=0, keepdims=True).astype(i32)
         ends_out[half + 2 : half + 3, :] = jnp.max(turned, axis=0, keepdims=True).astype(i32)
 
-    plan_moves(lambda v: lax.shift_right_logical(tags[v], 15), index_out, words_out)
-
-
-def plan_moves(rank, index_out, words_out):
+    plan_moves(lambda v: lax.shift_right_logical(tags[v], 15), index_out)
+
+
+def plan_moves(rank, index_out):
     keys = [rank(v).astype(f32) for v in range(VREGS)]
 
     def record(t, v, index):
@@ -272,8 +272,8 @@
 
     _, words, sub_words = sort_network(keys, (), record)
     for v in range(VREGS):
-        words_out[0, v] = words[v]
-        words_out[1, v] = sub_words[v]
+        index_out[9, v] = words[v]
+        index_out[10, v] = sub_words[v]
 
 
 def plan(cells, offsets, moves, slots):
@@ -287,12 +287,11 @@
             jax.ShapeDtypeStruct((4, 128), i32),
             jax.ShapeDtypeStruct((2, VREGS, 8, 128), f32),
             jax.ShapeDtypeStruct((4,), i32),
-            jax.ShapeDtypeStruct((9, VREGS, 8, 128), i32),
-            jax.ShapeDtypeStruct((2, VREGS, 8, 128), i32),
+            jax.ShapeDtypeStruct((11, VREGS, 8, 128), i32),
             jax.ShapeDtypeStruct((VREGS, 8, 128), i32),
         ],
         in_specs=[vmem] * 2,
-        out_specs=[vmem, vmem, vmem, smem, vmem, vmem, vmem],
+        out_specs=[vmem, vmem, vmem, smem, vmem, vmem],
         scratch_shapes=[pltpu.VMEM((256, 128), i32), pltpu.VMEM((256, 128), f32)],
         compiler_params=pltpu.CompilerParams(vmem_limit_bytes=32 << 20),
         cost_estimate=pl.CostEstimate(flops=20_000_000, bytes_accessed=8_000_000, transcendentals=0),
@@ -516,7 +515,7 @@
 
 def transfer_kernel(
     ends, counts,
-    table, above, below, near, frac, early, index, words,
+    table, above, below, near, frac, early, index,
     state, north, south, east, west,
     nodes, samples, columns, buffer,
 ):
@@ -564,7 +563,7 @@
     apply_network(
         8,
         lambda c, v: state[c, 8 * v : 8 * v + 8, :],
-        buffer, index, words.at[0], words.at[1], finish,
+        buffer, index, index.at[9], index.at[10], finish,
     )
     for k, out in enumerate((north, south, east, west)):
         for j in range(64):
@@ -572,14 +571,14 @@
             out[:, 128 * j : 128 * j + 128] = columns[base : base + 8, :]
 
 
-def transfer(ends, counts, table, above, below, near, frac, early, index, words):
+def transfer(ends, counts, table, above, below, near, frac, early, index):
     vmem = pl.BlockSpec(memory_space=pltpu.VMEM)
     smem = pl.BlockSpec(memory_space=pltpu.SMEM)
     return pl.pallas_call(
         transfer_kernel,
         out_shape=[jax.ShapeDtypeStruct((8, 256, 128), f32)]
         + [jax.ShapeDtypeStruct((8, CAP), f32)] * 4,
-        in_specs=[smem] * 2 + [vmem] * 8,
+        in_specs=[smem] * 2 + [vmem] * 7,
         out_specs=[vmem] * 5,
         scratch_shapes=[
             pltpu.VMEM((8 * EDGE_PLANE, 128), f32),
@@ -592,12 +591,12 @@
         name="transfer",
     )(
         ends, counts, table, above, below,
-        near.reshape(256, 128), frac.reshape(2, 256, 128), early, index, words,
-    )
-
-
-def restore_kernel(state, offsets, tags, out, columns, buffer, index, words):
-    plan_moves(lambda v: tags[v] & 32767, index, words)
+        near.reshape(256, 128), frac.reshape(2, 256, 128), early, index,
+    )
+
+
+def restore_kernel(state, offsets, tags, out, columns, buffer, index):
+    plan_moves(lambda v: tags[v] & 32767, index)
 
     def finish(v, moved):
         for c in range(2):
@@ -609,7 +608,7 @@
     apply_network(
         6,
         lambda c, v: state[c + 2, 8 * v : 8 * v + 8, :],
-        buffer, index, words.at[0], words.at[1], finish,
+        buffer, index, index.at[9], index.at[10], finish,
     )
     for j in range(256):
         out[:, 128 * j : 128 * j + 128] = columns[8 * j : 8 * j + 8, :]
@@ -625,8 +624,7 @@
         scratch_shapes=[
             pltpu.VMEM((2048, 128), f32),
             pltpu.VMEM((6, VREGS, 8, 128), f32),
-            pltpu.VMEM((9, VREGS, 8, 128), i32),
-            pltpu.VMEM((2, VREGS, 8, 128), i32),
+            pltpu.VMEM((11, VREGS, 8, 128), i32),
         ],
         compiler_params=pltpu.CompilerParams(vmem_limit_bytes=32 << 20),
         cost_estimate=pl.CostEstimate(flops=10_000_000, bytes_accessed=4_000_000, transcendentals=0),
@@ -648,14 +646,14 @@
 def shards(ocean, grid_mass, grid_momentum, cells, offsets, moves, slots):
     outgoing = pack(ocean, grid_mass, grid_momentum)
     forcing = lax.all_to_all(outgoing, "lon", 0, 0)
-    near, ends, frac, counts, index, words, tags = plan(cells, offsets, moves, slots)
+    near, ends, frac, counts, index, tags = plan(cells, offsets, moves, slots)
     forcing, near = lax.optimization_barrier((forcing, near))
     table, first_edge, last_edge = node_table(forcing, grid_mass, grid_momentum)
     above = from_behind(last_edge, "lat", 1)
     below = from_behind(first_edge, "lat", -1)
     early = inner(ends, table, near, frac)
     state, north, south, east, west = transfer(
-        ends, counts, table, above, below, near, frac, early, index, words
+        ends, counts, table, above, below, near, frac, early, index
     )
     north = from_behind(north, "lat", 1)
     south = from_behind(south, "lat", -1)

time: 72.8 us -> 73.1 us (level)
  transfers between devices with their start and end apart: 7 -> 7, of which waited for: 1 -> 0; matrix products, arithmetic and copies ran while one was open for 0% -> 0% of each run, Pallas kernels for 46% -> 46%
where the time goes in v7:
time: 73.1 us; the launch traced here: 72.8 us
  Pallas kernels  43.1 us (59%)
  starting transfers between devices  26.5 us (36%)
  local copies, waits for them, and re-layouts  1.35 us (2%)
  other arithmetic  1.06 us (1%)
  between operations  0.84 us (1%)
    ppermute x4, starting transfers between devices, from_behind(): return lax.ppermute(block, axis, route)  16.7 us
    pallas_call x1, Pallas kernels, plan(): pl.pallas_call(plan_kernel, out_shape=[jax.ShapeDtypeStruct((VREGS, 8, 12...  14.1 us
    pallas_call x1, Pallas kernels, restore(): pl.pallas_call(restore_kernel, out_shape=jax.ShapeDtypeStruct((8, 4 * CAP...  11 us
    pallas_call x1, Pallas kernels, inner(): pl.pallas_call(inner_kernel, out_shape=jax.ShapeDtypeStruct((8, 256, 128)...  8.38 us
    pallas_call x1, Pallas kernels, transfer(): pl.pallas_call(transfer_kernel, out_shape=[jax.ShapeDtypeStruct((8, 256,...  6.35 us
    all_to_all x1, starting transfers between devices, shards(): forcing = lax.all_to_all(outgoing, 'lon', 0, 0)  5.9 us
    ppermute x2, starting transfers between devices, passed_along(): lax.ppermute(value, axis, [(i, (i + by) % count) for i in range(count)])  3.92 us
    pallas_call x1, Pallas kernels, pack(): pl.pallas_call(pack_kernel, out_shape=jax.ShapeDtypeStruct((LON, 8, 4 * C...  2.67 us
  transfers between devices with their start and end apart: 7, of which 0 were waited for; matrix products, arithmetic and copies ran while one was open for 0% of the time, Pallas kernels for 46%

profile of v7, /device:TPU:8, one launch (start us, length us, event | category | flops | bytes accessed | tf_op | source)
XLA Modules:
  0.0 72.8 jit_solution(17231570830989492520)
XLA Ops:
  0.6 0.0 copy-start.6
  0.6 2.7 %pack.1 = f32[16,8,1792]{2,1,0:T(8,128)} custom-call(f32[4,8,6144]{2,1,0:T(8,128)} %ocean.1, f32[128,384]{1,0:T(8,128)} %mass.3, f32[2,128,384]{2,1,0:T(8,128)} %momentum.3), custom_call_target="tpu_custom_call" | custom-call | tf_op jit(solution)/shard_map/pack/pallas_call | solution.py:339
  3.3 0.0 copy-start.7
  3.3 0.0 copy-start.8
  3.3 0.0 copy-start.9
  3.3 0.0 copy-start
  3.3 0.0 copy-start.1
  3.3 5.9 %all-to-all-start = ((f32[16,8,1792]{2,1,0:T(8,128)}), f32[16,8,1792]{2,1,0:T(8,128)S(1)}, u32[]{:S(2)}, u32[]{:S(2)}) async-start(f32[16,8,1792]{2,1,0:T(8,128)} %pack.1), calls=%async_computation | async-start | bytes 1835008 | tf_op jit(solution)/shard_map/all_to_all | solution.py:648
  9.2 0.0 copy-done.6
  9.3 0.0 copy-done.7
  9.3 0.0 copy-done.8
  9.3 0.0 copy-done.9
  9.3 14.1 %plan.1 = (s32[32,8,128]{2,1,0:T(8,128)S(1)}, s32[4,128]{1,0:T(4,128)S(1)}, f32[2,32,8,128]{3,2,1,0:T(8,128)S(1)}, s32[4]{0:T(128)S(1)}, s32[11,32,8,128]{3,2,1,0:T(8,128)S(1)}, /*index=5*/s32[32,8,128]{2,1,0:T(8,128)S(1)}) custom-call(s32[256,128]{1,0:T(8,128)S(1)} %or_bitcast_fusion.packed, f32[2,256,128]{2,1,0:T(8,128)S(1)} %bitcast.8), custom_call_target="tpu_custom_call" | custom-call | flops 20000000 | bytes 8000000 | tf_op jit(solution)/shard_map/plan/pallas_call | solution.py:283
  23.5 0.0 copy-start.2
  23.5 0.6 copy-done.2
  24.2 0.0 copy-start.4
  24.2 0.6 copy-done.4
  24.8 0.0 all-to-all-done.forcing
  24.8 0.0 copy-start.3
  24.8 0.0 copy-done
  24.8 0.0 copy-done.1
  24.8 0.5 table.1
  25.3 5.5 %collective-permute-start = (f32[24,128]{1,0:T(8,128)S(1)}, f32[24,128]{1,0:T(8,128)S(1)}, u32[]{:S(2)}, u32[]{:S(2)}) collective-permute-start(f32[24,128]{1,0:T(8,128)S(1)} %get-tuple-element.23), channel_id=1, source_target_pairs={{0,16},{16,32},{32,48},{48,64},{64,80},{80,96},{96,112},{1,17},{17... | collective-permute-start | bytes 36872 | tf_op jit(solution)/shard_map/ppermute | solution.py:638
  30.8 2.9 %collective-permute-start.1 = (f32[24,128]{1,0:T(8,128)S(1)}, f32[24,128]{1,0:T(8,128)S(1)}, u32[]{:S(2)}, u32[]{:S(2)}) collective-permute-start(f32[24,128]{1,0:T(8,128)S(1)} %get-tuple-element.24), channel_id=1, source_target_pairs={{16,0},{32,16},{48,32},{64,48},{80,64},{96,80},{112,96},{17,1},{33... | collective-permute-start | bytes 36872 | tf_op jit(solution)/shard_map/ppermute | solution.py:638
  33.8 0.0 copy-done.3
  33.8 8.4 %inner.1.early = f32[8,256,128]{2,1,0:T(8,128)S(1)} custom-call(s32[4,128]{1,0:T(4,128)S(1)} %get-tuple-element.18.ends, f32[3072,128]{1,0:T(8,128)S(1)} %get-tuple-element.22.table, s32[256,128]{1,0:T(8,128)S(1)} %bitcast.12, f32[2,256,128]{2,1,0:T(8,128)S(1)} %bitcast.10), custom_call_target="tpu_custom_call" | custom-call | flops 20000000 | bytes 8000000 | tf_op jit(solution)/shard_map/inner/pallas_call | solution.py:504
  42.2 0.0 collective-permute-done.above
  42.2 0.0 collective-permute-done.1.below
  42.2 0.0 copy-start.5
  42.2 6.3 %transfer.1 = (f32[8,256,128]{2,1,0:T(8,128)S(1)}, f32[8,8192]{1,0:T(8,128)S(1)}, f32[8,8192]{1,0:T(8,128)S(1)}, f32[8,8192]{1,0:T(8,128)S(1)}, f32[8,8192]{1,0:T(8,128)S(1)}) custom-call(s32[4,128]{1,0:T(4,128)S(1)} %get-tuple-element.18.ends, s32[4]{0:T(128)S(1)} %get-tuple-element.19.counts, f32[3072,128]{1,0:T(8,128)S(1)} %get-tuple-element.22.table, ...), custom_call_target="tpu_custom_call" | custom-call | flops 10000000 | bytes 8000000 | tf_op jit(solution)/shard_map/transfer/pallas_call | solution.py:577
  48.6 4.6 %collective-permute-start.2 = (f32[8,8192]{1,0:T(8,128)S(1)}, f32[8,8192]{1,0:T(8,128)S(1)}, u32[]{:S(2)}, u32[]{:S(2)}) collective-permute-start(f32[8,8192]{1,0:T(8,128)S(1)} %get-tuple-element.30), channel_id=1, source_target_pairs={{0,16},{16,32},{32,48},{48,64},{64,80},{80,96},{96,112},{1,17},{17... | collective-permute-start | bytes 786440 | tf_op jit(solution)/shard_map/ppermute | solution.py:638
  53.2 3.7 %collective-permute-start.3 = (f32[8,8192]{1,0:T(8,128)S(1)}, f32[8,8192]{1,0:T(8,128)S(1)}, u32[]{:S(2)}, u32[]{:S(2)}) collective-permute-start(f32[8,8192]{1,0:T(8,128)S(1)} %get-tuple-element.31), channel_id=1, source_target_pairs={{16,0},{32,16},{48,32},{64,48},{80,64},{96,80},{112,96},{17,1},{33... | collective-permute-start | bytes 786440 | tf_op jit(solution)/shard_map/ppermute | solution.py:638
  56.8 0.1 collective-permute-start.4
  56.9 3.8 %collective-permute-start.5 = (f32[8,8192]{1,0:T(8,128)S(1)}, f32[8,8192]{1,0:T(8,128)S(1)}, u32[]{:S(2)}, u32[]{:S(2)}) collective-permute-start(f32[8,8192]{1,0:T(8,128)S(1)} %get-tuple-element.33), channel_id=1, source_target_pairs={{0,15},{1,0},{2,1},{3,2},{4,3},{5,4},{6,5},{7,6},{8,7},{9,8},{10,9... | collective-permute-start | bytes 786440 | tf_op jit(solution)/shard_map/ppermute | solution.py:643
  60.7 0.0 copy-done.5
  60.7 11.0 %restore.1 = f32[8,32768]{1,0:T(8,128)} custom-call(f32[8,256,128]{2,1,0:T(8,128)S(1)} %get-tuple-element.28.state, f32[2,256,128]{2,1,0:T(8,128)S(1)} %bitcast.9, s32[32,8,128]{2,1,0:T(8,128)S(1)} %copy-done.5), custom_call_target="tpu_custom_call" | custom-call | flops 10000000 | bytes 4000000 | tf_op jit(solution)/shard_map/restore/pallas_call | solution.py:619
  71.8 0.0 collective-permute-done.2
  71.8 0.0 collective-permute-done.3
  71.8 0.0 collective-permute-done.4
  71.8 0.0 collective-permute-done.5
  71.8 1.0 %pad_maximum_fusion = f32[8,32768]{1,0:T(8,128)} fusion(f32[8,8192]{1,0:T(8,128)S(1)} %collective-permute-done.5, f32[8,8192]{1,0:T(8,128)S(1)} %collective-permute-done.4, f32[8,8192]{1,0:T(8,128)S(1)} %collective-permute-done.3, f32[8,8192]{1,0:T(8,128)S(1)} %collective-permute-done.2), kind=kLoop, calls=%fused_computation | loop fusion | flops 786432 | bytes 2097152 | tf_op jit(solution)/shard_map/concatenate | solution.py:663
  (2 shorter events, 0.0 us)
Async XLA Ops:
  0.6 8.6 %copy-start.6 = (f32[2,32768]{1,0:T(2,128)S(1)}, f32[2,32768]{1,0:T(2,128)}, u32[]{:S(2)}) copy-start(f32[2,32768]{1,0:T(2,128)} %param.11) | copy-start | bytes 786436
  3.3 6.0 %copy-start.7 = (s32[32768]{0:T(1024)S(1)}, s32[32768]{0:T(1024)}, u32[]{:S(2)}) copy-start(s32[32768]{0:T(1024)} %param.12) | copy-start | bytes 393220
  3.3 6.0 %copy-start.8 = (s32[32768]{0:T(1024)S(1)}, s32[32768]{0:T(1024)}, u32[]{:S(2)}) copy-start(s32[32768]{0:T(1024)} %param.10) | copy-start | bytes 393220
  3.3 6.0 %copy-start.9 = (s32[32768]{0:T(1024)S(1)}, s32[32768]{0:T(1024)}, u32[]{:S(2)}) copy-start(s32[32768]{0:T(1024)} %param.13) | copy-start | bytes 393220
  3.3 21.5 %copy-start = (f32[2,128,384]{2,1,0:T(8,128)S(1)}, f32[2,128,384]{2,1,0:T(8,128)}, u32[]{:S(2)}) copy-start(f32[2,128,384]{2,1,0:T(8,128)} %momentum.3) | copy-start | bytes 1179652
  3.3 21.5 %copy-start.1 = (f32[128,384]{1,0:T(8,128)S(1)}, f32[128,384]{1,0:T(8,128)}, u32[]{:S(2)}) copy-start(f32[128,384]{1,0:T(8,128)} %mass.3) | copy-start | bytes 589828
  3.3 21.5 %all-to-all-start = ((f32[16,8,1792]{2,1,0:T(8,128)}), f32[16,8,1792]{2,1,0:T(8,128)S(1)}, u32[]{:S(2)}, u32[]{:S(2)}) async-start(f32[16,8,1792]{2,1,0:T(8,128)} %pack.1), calls=%async_computation | async-start | bytes 1835008 | tf_op jit(solution)/shard_map/all_to_all | solution.py:648
  23.5 0.7 copy-start.2
  24.2 0.6 copy-start.4
  24.8 9.0 %copy-start.3 = (s32[32,8,128]{2,1,0:T(8,128)S(1)}, s32[32,8,128]{2,1,0:T(8,128)}, u32[]{:S(2)}) copy-start(s32[32,8,128]{2,1,0:T(8,128)} %copy-done.2) | copy-start | bytes 393220
  25.3 16.8 %collective-permute-start = (f32[24,128]{1,0:T(8,128)S(1)}, f32[24,128]{1,0:T(8,128)S(1)}, u32[]{:S(2)}, u32[]{:S(2)}) collective-permute-start(f32[24,128]{1,0:T(8,128)S(1)} %get-tuple-element.23), channel_id=1, source_target_pairs={{0,16},{16,32},{32,48},{48,64},{64,80},{80,96},{96,112},{1,17},{17... | collective-permute-start | bytes 36872 | tf_op jit(solution)/shard_map/ppermute | solution.py:638
  30.8 11.4 %collective-permute-start.1 = (f32[24,128]{1,0:T(8,128)S(1)}, f32[24,128]{1,0:T(8,128)S(1)}, u32[]{:S(2)}, u32[]{:S(2)}) collective-permute-start(f32[24,128]{1,0:T(8,128)S(1)} %get-tuple-element.24), channel_id=1, source_target_pairs={{16,0},{32,16},{48,32},{64,48},{80,64},{96,80},{112,96},{17,1},{33... | collective-permute-start | bytes 36872 | tf_op jit(solution)/shard_map/ppermute | solution.py:638
  42.2 18.6 %copy-start.5 = (s32[32,8,128]{2,1,0:T(8,128)S(1)}, s32[32,8,128]{2,1,0:T(8,128)}, u32[]{:S(2)}) copy-start(s32[32,8,128]{2,1,0:T(8,128)} %copy-done.4) | copy-start | bytes 393220
  48.6 23.2 %collective-permute-start.2 = (f32[8,8192]{1,0:T(8,128)S(1)}, f32[8,8192]{1,0:T(8,128)S(1)}, u32[]{:S(2)}, u32[]{:S(2)}) collective-permute-start(f32[8,8192]{1,0:T(8,128)S(1)} %get-tuple-element.30), channel_id=1, source_target_pairs={{0,16},{16,32},{32,48},{48,64},{64,80},{80,96},{96,112},{1,17},{17... | collective-permute-start | bytes 786440 | tf_op jit(solution)/shard_map/ppermute | solution.py:638
  53.2 18.6 %collective-permute-start.3 = (f32[8,8192]{1,0:T(8,128)S(1)}, f32[8,8192]{1,0:T(8,128)S(1)}, u32[]{:S(2)}, u32[]{:S(2)}) collective-permute-start(f32[8,8192]{1,0:T(8,128)S(1)} %get-tuple-element.31), channel_id=1, source_target_pairs={{16,0},{32,16},{48,32},{64,48},{80,64},{96,80},{112,96},{17,1},{33... | collective-permute-start | bytes 786440 | tf_op jit(solution)/shard_map/ppermute | solution.py:638
  56.8 14.9 %collective-permute-start.4 = (f32[8,8192]{1,0:T(8,128)S(1)}, f32[8,8192]{1,0:T(8,128)S(1)}, u32[]{:S(2)}, u32[]{:S(2)}) collective-permute-start(f32[8,8192]{1,0:T(8,128)S(1)} %get-tuple-element.32), channel_id=1, source_target_pairs={{0,1},{1,2},{2,3},{3,4},{4,5},{5,6},{6,7},{7,8},{8,9},{9,10},{10,1... | collective-permute-start | bytes 786440 | tf_op jit(solution)/shard_map/ppermute | solution.py:643
  56.9 14.9 %collective-permute-start.5 = (f32[8,8192]{1,0:T(8,128)S(1)}, f32[8,8192]{1,0:T(8,128)S(1)}, u32[]{:S(2)}, u32[]{:S(2)}) collective-permute-start(f32[8,8192]{1,0:T(8,128)S(1)} %get-tuple-element.33), channel_id=1, source_target_pairs={{0,15},{1,0},{2,1},{3,2},{4,3},{5,4},{6,5},{7,6},{8,7},{9,8},{10,9... | collective-permute-start | bytes 786440 | tf_op jit(solution)/shard_map/ppermute | solution.py:643
